TPU v7x, 512 devices: a whole 4x8x8 slice. The times are simulated.
512 devices in a mesh: guide: 2 (over core), blk: 64 (over y, z), batch: 4 (over x).
Axes of the slice: x: 4, y: 8, z: 8, core: 2. Of those that a mesh axis runs over, the one named last changes fastest.
Arguments:
- hidden: bfloat16 [2, 64, 1536], P('guide', 'batch'), may hold values from -6 to 6
- w_qkv: bfloat16 [1536, 2560], P('blk'), may hold values from -0.15625 to 0.15625
- key_cache: bfloat16 [2, 64, 1024, 512], P('guide', 'batch', 'blk'), may hold values from -700 to 700
- value_cache: bfloat16 [2, 64, 1024, 512], P('guide', 'batch', 'blk'), may hold values from -6 to 6
- lengths: int32 [2, 64], P('guide', 'batch'), may hold values from 128 to 1024, as said below
- w_out: bfloat16 [1536, 1536], P('blk'), may hold values from -0.15625 to 0.15625
- router: bfloat16 [1536, 16], replicated, may hold values from -0.15625 to 0.15625
- routes: int32 [2, 64, 2], P('guide', 'batch'), may hold values from 0 to 15, all different within a row
- w_gate: bfloat16 [1536, 16384], P(None, 'blk'), may hold values from -0.15625 to 0.15625
- w_up: bfloat16 [1536, 16384], P(None, 'blk'), may hold values from -0.15625 to 0.15625
- w_down: bfloat16 [16384, 1536], P('blk'), may hold values from -0.125 to 0.125
- w_vocab: bfloat16 [1536, 65536], P(None, ('blk', 'batch')), may hold values from -0.15625 to 0.15625
- group_ids: int32 [64], replicated, may hold values from 0 to 7, never falling along the last dimension, each value on 1 to 16 neighbouring positions
- weight_index: int32 [8], replicated, may hold values from 0 to 7
- guidance_levels: float32 [8], replicated, may hold values from 1 to 5
Outputs:
- logits: float32 [64, 65536], P('guide', ('blk', 'batch'))
- new_keys: bfloat16 [2, 64, 512], P('guide', 'batch')
- new_values: bfloat16 [2, 64, 512], P('guide', 'batch')
Inputs may be any that keep to these rules, and one draw needn't show every extreme that they name: `lengths`: every stream and index of batch has a request whose cache is full.
All inputs are finite; a program needn't handle non-finite values.
Results may differ from a plain program's by a relative error of at most 0.008.
Values may be sent and summed in bfloat16 or wider, within the bound.
No kernel may reach another device: no remote copies, remote signals or barrier semaphores. Data moves between devices by JAX's collectives and lax.ppermute only.
A program may use at most 64 MiB of HBM per device.

v0:
```python
import jax
import jax.numpy as jnp
from jax import lax
from jax.sharding import PartitionSpec as P

HEADS = 24
KV_HEADS = 8
HEAD_DIM = 64
EXPERTS = 16
EXPERT_UNITS = 1024


EPS = 1e-05


def from_partner(value, axis, bit):
    mask = 2**bit
    pairs = [(source, source ^ mask) for source in range(lax.axis_size(axis))]
    return lax.ppermute(value, axis, pairs)


def rms(values):
    return values * lax.rsqrt(jnp.mean(values * values, axis=-1, keepdims=True) + EPS)


def local(
    hidden,
    w_qkv,
    key_cache,
    value_cache,
    lengths,
    w_out,
    router,
    routes,
    w_gate,
    w_up,
    w_down,
    w_vocab,
    group_ids,
    weight_index,
    guidance_levels,
):
    width_q = HEADS * HEAD_DIM
    width_k = KV_HEADS * HEAD_DIM
    group = HEADS // KV_HEADS
    position_block = lax.axis_index("blk")
    count = hidden.shape[1]
    x = hidden[0].astype(jnp.float32)
    normed = rms(x).astype(jnp.bfloat16)
    feat_rows = w_qkv.shape[0]
    normed_part = lax.dynamic_slice_in_dim(normed, position_block * feat_rows, feat_rows, 1)
    partial_qkv = jnp.dot(normed_part, w_qkv, preferred_element_type=jnp.float32)
    qkv = lax.psum(partial_qkv, "blk").astype(jnp.bfloat16)
    query = qkv[:, :width_q]
    new_key = qkv[:, width_q : width_q + width_k]
    new_value = qkv[:, width_q + width_k :]
    span = key_cache.shape[2]
    query_heads = query.reshape(count, KV_HEADS, group, HEAD_DIM)
    keys_here = key_cache[0].reshape(count, span, KV_HEADS, HEAD_DIM)
    values_here = value_cache[0].reshape(count, span, KV_HEADS, HEAD_DIM)
    scale = HEAD_DIM ** (-0.5)
    scores = (
        jnp.einsum("rkgd,rckd->rkgc", query_heads, keys_here, preferred_element_type=jnp.float32)
        * scale
    )
    own = (
        jnp.einsum(
            "rkgd,rkd->rkg",
            query_heads,
            new_key.reshape(count, KV_HEADS, HEAD_DIM),
            preferred_element_type=jnp.float32,
        )
        * scale
    )
    positions = position_block * span + jnp.arange(span)
    valid = (positions[None, :] < lengths[0][:, None])[:, None, None, :]
    local_top = jnp.max(jnp.where(valid, scores, -1e30), axis=-1)
    top = lax.pmax(jnp.maximum(local_top, own), "blk")
    probs = jnp.exp(jnp.where(valid, scores - top[..., None], -1e30))
    partial_total = jnp.sum(probs, axis=-1)
    acc = jnp.einsum(
        "rkgc,rckd->rkgd",
        probs.astype(jnp.bfloat16),
        values_here,
        preferred_element_type=jnp.float32,
    ).reshape(count, width_q)
    own_prob = jnp.exp(own - top)
    own_rounded = lax.optimization_barrier(own_prob.astype(jnp.bfloat16)).astype(jnp.float32)
    own_term = (
        own_rounded[..., None] * new_value.astype(jnp.float32).reshape(count, KV_HEADS, 1, HEAD_DIM)
    ).reshape(count, width_q)
    out_rows = w_out.shape[0]
    acc_sum, total_sum = lax.psum((acc, partial_total), "blk")
    totals = jnp.repeat((total_sum + own_prob).reshape(count, HEADS), HEAD_DIM, axis=1)
    attn = ((acc_sum + own_term) / totals).astype(jnp.bfloat16)
    attn_cols = lax.dynamic_slice_in_dim(attn, position_block * out_rows, out_rows, 1)
    mixed = x + lax.psum(jnp.dot(attn_cols, w_out, preferred_element_type=jnp.float32), "blk")
    expert_in = rms(mixed).astype(jnp.bfloat16)
    choice_logits = jnp.dot(expert_in, router, preferred_element_type=jnp.float32)
    picks = (routes[0][:, :, None] == jnp.arange(EXPERTS)[None, None, :]).astype(jnp.float32)
    chosen = jnp.sum(picks * choice_logits[:, None, :], axis=-1)
    first = jax.nn.sigmoid(chosen[:, 0] - chosen[:, 1])
    shares = jnp.stack([first, 1.0 - first], axis=1)
    per_expert = jnp.sum(picks * shares[:, :, None], axis=1)
    local_units = w_gate.shape[1]
    owner = (position_block * local_units + jnp.arange(local_units)) // EXPERT_UNITS
    member = (owner[None, :] == jnp.arange(EXPERTS)[:, None]).astype(jnp.float32)
    unit_weight = jnp.sum(per_expert[:, :, None] * member[None, :, :], axis=1)
    gate = jnp.dot(expert_in, w_gate, preferred_element_type=jnp.float32)
    upper = jnp.dot(expert_in, w_up, preferred_element_type=jnp.float32)
    act = (jax.nn.silu(gate) * upper * unit_weight).astype(jnp.bfloat16)
    expert_out = lax.psum(jnp.dot(act, w_down, preferred_element_type=jnp.float32), "blk")
    final_in = rms(mixed + expert_out).astype(jnp.bfloat16)
    stream_logits = jnp.dot(
        lax.all_gather(final_in, "batch", axis=0, tiled=True),
        w_vocab,
        preferred_element_type=jnp.float32,
    ).astype(jnp.bfloat16)
    stream_index = lax.axis_index("guide")
    half_rows = stream_logits.shape[0] // 2
    kept_rows = lax.dynamic_slice_in_dim(stream_logits, stream_index * half_rows, half_rows, 0)
    sent_rows = lax.dynamic_slice_in_dim(
        stream_logits, (1 - stream_index) * half_rows, half_rows, 0
    )
    partner = from_partner(sent_rows, "guide", 0)
    is_first = stream_index == 0
    cond = jnp.where(is_first, kept_rows, partner).astype(jnp.float32)
    uncond = jnp.where(is_first, partner, kept_rows).astype(jnp.float32)
    group_count = weight_index.shape[0]
    level_count = guidance_levels.shape[0]
    in_group = (group_ids[:, None] == jnp.arange(group_count)[None, :]).astype(jnp.float32)
    level_pick = (weight_index[:, None] == jnp.arange(level_count)[None, :]).astype(jnp.float32)
    group_weight = jnp.sum(level_pick * guidance_levels[None, :], axis=1)
    request_weight = jnp.sum(in_group * group_weight[None, :], axis=1)
    weight_rows = lax.dynamic_slice_in_dim(request_weight, stream_index * half_rows, half_rows, 0)
    logits = uncond + weight_rows[:, None] * (cond - uncond)
    return (logits, new_key[None], new_value[None])


def solution(mesh):
    placed = (
        P("guide", "batch", None),
        P("blk", None),
        P("guide", "batch", "blk", None),
        P("guide", "batch", "blk", None),
        P("guide", "batch"),
        P("blk", None),
        P(),
        P("guide", "batch", None),
        P(None, "blk"),
        P(None, "blk"),
        P("blk", None),
        P(None, ("blk", "batch")),
        P(),
        P(),
        P(),
    )
    return jax.shard_map(
        local,
        mesh=mesh,
        in_specs=placed,
        out_specs=(
            P("guide", ("blk", "batch")),
            P("guide", "batch", None),
            P("guide", "batch", None),
        ),
        check_vma=False,
    )
```

profile of v0, /device:TPU:1, one launch (start us, length us, event | category | flops | bytes accessed | tf_op | source)
XLA Modules:
  0.0 1172.0 jit_solution(4721336274266858184)
XLA Ops:
  7.2 0.9 bitcast_convert_fusion
  8.5 232.3 %all-reduce.10 = bf16[16,2560]{1,0:T(8,128)(2,1)S(1)} all-reduce(f32[16,2560]{1,0:T(8,128)S(1)} %fusion.25), channel_id=1, replica_groups=mesh['guide'=2,'blk'=64,'batch'=4] {'blk'}, use_global_device_ids=true, to_apply=%region_1.0 | all-reduce | flops 40960 | bytes 245760 | tf_op jit(solution)/shard_map/psum | solution.py:53
  240.8 0.6 slice_bitcast_fusion
  241.5 0.7 slice-done
  243.0 0.7 copy-done.13
  243.7 0.5 select_reduce_fusion
  244.2 219.4 %pmax.7 = f32[16,8,3]{2,1,0:T(8,128)S(1)} all-reduce(f32[16,8,3]{2,1,0:T(8,128)S(1)} %multiply_maximum_fusion), channel_id=1, replica_groups=mesh['guide'=2,'blk'=64,'batch'=4] {'blk'}, use_global_device_ids=true, to_apply=%region_3.4 | all-reduce | flops 384 | bytes 3072 | tf_op jit(solution)/shard_map/pmax | solution.py:78
  464.2 0.8 reshape.136
  465.1 0.4 fusion.6
  465.5 219.4 %psum.37 = f32[16,8,3]{2,1,0:T(8,128)S(1)} all-reduce(f32[16,8,3]{2,1,0:T(8,128)S(1)} %fusion.6), channel_id=1, replica_groups=mesh['guide'=2,'blk'=64,'batch'=4] {'blk'}, use_global_device_ids=true, to_apply=%region_6.7 | all-reduce | flops 384 | bytes 3072 | tf_op jit(solution)/shard_map/psum | solution.py:93
  685.8 28.6 %all-reduce.5.cloned.1.call-done = f32[16,1536]{1,0:T(8,128)} async-done(((f32[16,1536]{1,0:T(8,128)}), f32[16,1536]{1,0:T(8,128)}) %all-reduce.5.cloned.1.call-update) | async-done | bytes 98320 | tf_op jit(solution)/shard_map/psum | solution.py:93
  714.3 1.6 fusion.27
  716.0 275.4 %all-reduce.7.cloned.1.call-done = f32[16,1536]{1,0:T(8,128)} async-done(((f32[16,1536]{1,0:T(8,128)}), f32[16,1536]{1,0:T(8,128)}) %all-reduce.7.cloned.1.call-update) | async-done | bytes 98320 | tf_op jit(solution)/shard_map/psum | solution.py:97
  991.4 1.1 multiply_reduce_fusion.2
  992.6 0.7 copy-done.11
  993.4 0.7 copy-done.12
  994.8 1.2 fusion.2
  996.2 146.6 %all-reduce.9.cloned.1.call-done = f32[16,1536]{1,0:T(8,128)} async-done(((f32[16,1536]{1,0:T(8,128)}), f32[16,1536]{1,0:T(8,128)}) %all-reduce.9.cloned.1.call-update) | async-done | bytes 98320 | tf_op jit(solution)/shard_map/psum | solution.py:112
  1142.8 1.0 multiply_reduce_fusion.1
  1143.8 1.0 multiply_convert_fusion
  1144.8 10.0 all_gather.3
  1155.1 8.9 collective-permute-start
  1164.1 0.6 collective-permute-done
  1164.8 0.7 convert_add_fusion.1
  (75 shorter events, 4.4 us)
Async XLA Ops:
  7.2 987.6 %copy-start = (bf16[256,1536]{1,0:T(8,128)(2,1)S(1)}, bf16[256,1536]{1,0:T(8,128)(2,1)}, u32[]{:S(2)}) copy-start(bf16[256,1536]{1,0:T(8,128)(2,1)} %param.25) | copy-start | bytes 2359300
  7.2 707.1 %all-reduce.5.cloned.1.call-start = ((), (), s32[]{:S(2)}) async-start(), calls=%async_computation | async-start | bytes 196608 | tf_op jit(solution)/shard_map/psum | solution.py:93
  7.2 0.9 copy-start.1
  7.2 1.0 copy-start.9
  8.5 233.9 %copy-start.7 = (bf16[1,16,16,512]{3,2,1,0:T(8,128)(2,1)S(1)}, bf16[1,16,16,512]{3,2,1,0:T(8,128)(2,1)}, u32[]{:S(2)}) copy-start(bf16[1,16,16,512]{3,2,1,0:T(8,128)(2,1)} %param.17) | copy-start | bytes 786436
  240.8 0.6 copy-start.6
  241.4 0.8 slice-start
  243.0 0.7 copy-start.13
  244.2 219.4 %copy-start.8 = (bf16[1,16,16,512]{3,2,1,0:T(8,128)(2,1)S(1)}, bf16[1,16,16,512]{3,2,1,0:T(8,128)(2,1)}, u32[]{:S(2)}) copy-start(bf16[1,16,16,512]{3,2,1,0:T(8,128)(2,1)} %param.18) | copy-start | bytes 786436
  465.1 526.3 %all-reduce.7.cloned.1.call-start = ((), (), s32[]{:S(2)}) async-start(), calls=%async_computation.1 | async-start | bytes 196608 | tf_op jit(solution)/shard_map/psum | solution.py:97
  685.0 309.4 %copy-start.4 = (bf16[1536,256]{1,0:T(8,128)(2,1)S(1)}, bf16[1536,256]{1,0:T(8,128)(2,1)}, u32[]{:S(2)}) copy-start(bf16[1536,256]{1,0:T(8,128)(2,1)} %param.23) | copy-start | bytes 2359300
  685.2 29.1 %copy-start.10 = (bf16[24,1536]{1,0:T(8,128)(2,1)S(1)}, bf16[24,1536]{1,0:T(8,128)(2,1)}, u32[]{:S(2)}) copy-start(bf16[24,1536]{1,0:T(8,128)(2,1)} %param.20) | copy-start | bytes 221188
  685.5 309.2 %copy-start.3 = (bf16[1536,256]{1,0:T(8,128)(2,1)S(1)}, bf16[1536,256]{1,0:T(8,128)(2,1)}, u32[]{:S(2)}) copy-start(bf16[1536,256]{1,0:T(8,128)(2,1)} %param.24) | copy-start | bytes 2359300
  715.9 426.9 %all-reduce.9.cloned.1.call-start = ((), (), s32[]{:S(2)}) async-start(), calls=%async_computation.2 | async-start | bytes 196608 | tf_op jit(solution)/shard_map/psum | solution.py:112
  991.4 1.1 copy-start.2
  992.5 0.8 copy-start.11
  993.4 0.7 copy-start.12
  994.8 1.3 copy-start.14
  994.8 1.3 copy-start.15
  996.0 158.8 %copy-start.5 = (bf16[1536,256]{1,0:T(8,128)(2,1)S(1)}, bf16[1536,256]{1,0:T(8,128)(2,1)}, u32[]{:S(2)}) copy-start(bf16[1536,256]{1,0:T(8,128)(2,1)} %param.26) | copy-start | bytes 2359300
  1155.0 8.9 copy-start.16
  1155.1 9.7 collective-permute-start
Sparse Core Ops, SparseCore 0:
  465.2 249.0 all-reduce.4
  717.9 273.4 all-reduce.6
  996.2 146.5 all-reduce.8
where the time goes:
time: 1170 us
  blocking collectives  681 us (58%)
  waiting for transfers between devices  451 us (39%)
  between operations  14.1 us (1%)
    psum x1, waiting for transfers between devices, local(): lax.psum(jnp.dot(attn_cols, w_out, preferred_element_type=jnp.float32), '...  275 us
    psum x1, blocking collectives, local(): qkv = lax.psum(partial_qkv, 'blk').astype(jnp.bfloat16)  232 us
    pmax x1, blocking collectives, local(): top = lax.pmax(jnp.maximum(local_top, own), 'blk')  219 us
    psum x1, blocking collectives, local(): acc_sum, total_sum = lax.psum((acc, partial_total), 'blk')  219 us
    psum x1, waiting for transfers between devices, local(): lax.psum(jnp.dot(act, w_down, preferred_element_type=jnp.float32), 'blk')  147 us
    psum x1, waiting for transfers between devices, local(): acc_sum, total_sum = lax.psum((acc, partial_total), 'blk')  28.6 us
  transfers between devices with their start and end apart: 4, of which 4 were waited for; matrix products, arithmetic and copies ran while one was open for 0% of the time, Pallas kernels for 0%

commit v1 on v0

v1 whole, which is shorter than its diff:
```python
import jax
import jax.numpy as jnp
from jax import lax
from jax.sharding import Mesh, PartitionSpec as P

HEADS = 24
KV_HEADS = 8
HEAD_DIM = 64
EXPERTS = 16
EXPERT_UNITS = 1024
EPS = 1e-05
F32 = jnp.float32
BF16 = jnp.bfloat16
BLK = ("y", "z")


def rms(values):
    return values * lax.rsqrt(jnp.mean(values * values, axis=-1, keepdims=True) + EPS)


def exchange(value, axes):
    return lax.all_to_all(value, axes, 0, 0, tiled=True)


def halves(value):
    high = lax.reduce_precision(value, 8, 7)
    return high.astype(BF16), (value - high).astype(BF16)


def local(
    hidden,
    w_qkv,
    key_cache,
    value_cache,
    lengths,
    w_out,
    router,
    routes,
    w_gate,
    w_up,
    w_down,
    w_vocab,
    group_ids,
    weight_index,
    guidance_levels,
):
    group = HEADS // KV_HEADS
    y, z = lax.axis_index("y"), lax.axis_index("z")
    ny, nz = lax.axis_size("y"), lax.axis_size("z")
    blocks = ny * nz
    block = y * nz + z
    count = hidden.shape[1]
    pair = count // nz
    width = hidden.shape[2]
    width_q = HEADS * HEAD_DIM
    width_k = KV_HEADS * HEAD_DIM
    head_w = gathered_rows(w_out)

    x = hidden[0].astype(F32)
    normed = rms(x).astype(BF16)
    rows = w_qkv.shape[0]
    part = lax.dynamic_slice_in_dim(normed, block * rows, rows, 1)
    qkv = jnp.dot(part, w_qkv, preferred_element_type=F32)
    q = qkv[:, :width_q].reshape(pair, nz, KV_HEADS, group, HEAD_DIM)
    k = qkv[:, width_q : width_q + width_k].reshape(pair, nz, KV_HEADS, 1, HEAD_DIM)
    v = qkv[:, width_q + width_k :].reshape(pair, nz, KV_HEADS, 1, HEAD_DIM)
    upper = jnp.concatenate([k, v, jnp.zeros_like(k)], axis=3)
    lines = jnp.concatenate([q, upper], axis=4).transpose(2, 1, 0, 3, 4)
    lines = lines.reshape(blocks, pair * group, 2 * HEAD_DIM)
    high, low = halves(lines)
    span = key_cache.shape[2]
    kc = key_cache[0].reshape(pair, nz, span, KV_HEADS, HEAD_DIM)
    vc = value_cache[0].reshape(pair, nz, span, KV_HEADS, HEAD_DIM)
    kv = jnp.concatenate([kc, vc], axis=4).transpose(3, 1, 0, 2, 4)
    kv = kv.reshape(blocks, pair * span, 2 * HEAD_DIM)
    fill = jnp.zeros((blocks, 4, 2 * HEAD_DIM), BF16)
    got = exchange(jnp.concatenate([kv, high, low, fill], axis=1), BLK)

    n_kv, n_l = pair * span, pair * group
    kv = got[:, :n_kv].reshape(blocks, pair, span, 2 * HEAD_DIM).transpose(1, 0, 2, 3)
    kv = kv.reshape(pair, blocks * span, 2 * HEAD_DIM)
    sums = jnp.sum(
        got[:, n_kv : n_kv + n_l].astype(F32) + got[:, n_kv + n_l : n_kv + 2 * n_l].astype(F32), axis=0
    )
    sums = sums.reshape(pair, group, 2 * HEAD_DIM).astype(BF16)
    query, new_k, new_v = sums[:, :, :HEAD_DIM], sums[:, 0, HEAD_DIM:], sums[:, 1, HEAD_DIM:]
    scale = HEAD_DIM ** (-0.5)
    scores = jnp.einsum("ihd,ipd->ihp", query, kv[:, :, :HEAD_DIM], preferred_element_type=F32) * scale
    own = jnp.sum(query.astype(F32) * new_k.astype(F32)[:, None, :], axis=-1) * scale
    lens = lax.dynamic_index_in_dim(lengths[0].reshape(pair, nz), z, 1, False)
    valid = (jnp.arange(blocks * span)[None, :] < lens[:, None])[:, None, :]
    top = jnp.maximum(jnp.max(jnp.where(valid, scores, -1e30), axis=-1), own)
    probs = jnp.exp(jnp.where(valid, scores - top[..., None], -1e30))
    own_prob = jnp.exp(own - top)
    total = jnp.sum(probs, axis=-1) + own_prob
    acc = jnp.einsum("ihp,ipd->ihd", probs.astype(BF16), kv[:, :, HEAD_DIM:], preferred_element_type=F32)
    own_r = lax.reduce_precision(own_prob, 8, 7)
    acc = acc + own_r[..., None] * new_v.astype(F32)[:, None, :]
    attn = (acc / total[..., None]).astype(BF16).reshape(pair, group * HEAD_DIM)
    part = jnp.dot(attn, head_w, preferred_element_type=F32).astype(BF16)
    part = part.reshape(pair * width // 128, 128)
    got = exchange(jnp.broadcast_to(part[None], (blocks,) + part.shape), BLK)

    got = jnp.sum(got.reshape(ny, nz, pair, width).astype(F32), axis=0)
    mixed = x + got.transpose(1, 0, 2).reshape(count, width)
    expert_in = rms(mixed).astype(BF16)
    choice_logits = jnp.dot(expert_in, router, preferred_element_type=F32)
    picks = (routes[0][:, :, None] == jnp.arange(EXPERTS)[None, None, :]).astype(F32)
    chosen = jnp.sum(picks * choice_logits[:, None, :], axis=-1)
    first = jax.nn.sigmoid(chosen[:, 0] - chosen[:, 1])
    shares = jnp.stack([first, 1.0 - first], axis=1)
    per_expert = jnp.sum(picks * shares[:, :, None], axis=1)
    units = w_gate.shape[1]
    owner = (block * units + jnp.arange(units)) // EXPERT_UNITS
    member = (owner[None, :] == jnp.arange(EXPERTS)[:, None]).astype(F32)
    unit_weight = jnp.sum(per_expert[:, :, None] * member[None, :, :], axis=1)
    gate = jnp.dot(expert_in, w_gate, preferred_element_type=F32)
    upper = jnp.dot(expert_in, w_up, preferred_element_type=F32)
    act = (jax.nn.silu(gate) * upper * unit_weight).astype(BF16)
    expert_out = jnp.dot(act, w_down, preferred_element_type=F32)
    own_lines = count * width // blocks // 128
    high, low = halves(expert_out.reshape(blocks, own_lines, 128))
    fresh = jnp.concatenate([new_k, new_v], axis=1)
    fresh = jnp.broadcast_to(fresh[None], (blocks,) + fresh.shape)
    got = exchange(jnp.concatenate([high, low, fresh], axis=1), BLK)

    piece = jnp.sum(got[:, :own_lines].astype(F32) + got[:, own_lines : 2 * own_lines].astype(F32), axis=0)
    mixed_piece = lax.dynamic_index_in_dim(mixed.reshape(blocks, own_lines, 128), block, 0, False)
    piece = (mixed_piece + piece).astype(BF16)
    piece = jnp.concatenate([piece, jnp.zeros((1, 128), BF16)], axis=0)
    everyone = blocks * lax.axis_size("batch")
    fresh = got[:, 2 * own_lines :].reshape(ny, nz, pair, 2, HEAD_DIM).transpose(3, 2, 1, 0, 4)
    fresh = fresh.reshape(2, count, width_k)
    got = exchange(jnp.broadcast_to(piece[None], (everyone,) + piece.shape), ("batch",) + BLK)
    outgoing = got[:, :own_lines].reshape(-1, width).astype(F32)
    final_in = rms(outgoing).astype(BF16)
    stream_logits = jnp.dot(final_in, w_vocab, preferred_element_type=F32).astype(BF16)
    stream = lax.axis_index("guide")
    half_rows = stream_logits.shape[0] // 2
    kept = lax.dynamic_slice_in_dim(stream_logits, stream * half_rows, half_rows, 0)
    sent = lax.dynamic_slice_in_dim(stream_logits, (1 - stream) * half_rows, half_rows, 0)
    partner = lax.ppermute(sent, "guide", [(0, 1), (1, 0)])
    is_first = stream == 0
    cond = jnp.where(is_first, kept, partner).astype(F32)
    uncond = jnp.where(is_first, partner, kept).astype(F32)
    group_count = weight_index.shape[0]
    level_count = guidance_levels.shape[0]
    in_group = (group_ids[:, None] == jnp.arange(group_count)[None, :]).astype(F32)
    level_pick = (weight_index[:, None] == jnp.arange(level_count)[None, :]).astype(F32)
    group_weight = jnp.sum(level_pick * guidance_levels[None, :], axis=1)
    request_weight = jnp.sum(in_group * group_weight[None, :], axis=1)
    weight_rows = lax.dynamic_slice_in_dim(request_weight, stream * half_rows, half_rows, 0)
    logits = uncond + weight_rows[:, None] * (cond - uncond)
    return (logits, fresh[0][None], fresh[1][None])


def gathered_rows(w_out):
    return lax.all_gather(w_out, "z", axis=0, tiled=True)


def solution(mesh):
    guide, blk, batch = (mesh.shape[a] for a in ("guide", "blk", "batch"))
    ny = KV_HEADS
    mesh = Mesh(mesh.devices.reshape(guide, ny, blk // ny, batch), ("guide",) + BLK + ("batch",))
    placed = (
        P("guide", "batch", None),
        P(BLK, None),
        P("guide", "batch", BLK, None),
        P("guide", "batch", BLK, None),
        P("guide", "batch"),
        P(BLK, None),
        P(),
        P("guide", "batch", None),
        P(None, BLK),
        P(None, BLK),
        P(BLK, None),
        P(None, BLK + ("batch",)),
        P(),
        P(),
        P(),
    )
    return jax.shard_map(
        local,
        mesh=mesh,
        in_specs=placed,
        out_specs=(
            P("guide", BLK + ("batch",)),
            P("guide", "batch", None),
            P("guide", "batch", None),
        ),
        check_vma=False,
    )
```

time: 1170 us -> 145 us (0.12)
  blocking collectives: 681 us -> 32.8 us
  waiting for transfers between devices: 451 us -> 36.6 us
  starting transfers between devices: 9 us -> 53.8 us
  between operations: 14.1 us -> 1.17 us
    psum x2 -> x0, blocking collectives: 452 us -> none  [the longest x1 232 us: local(): qkv = lax.psum(partial_qkv, 'blk').astype(jnp.bfloat16)]
    psum x3 -> x0, waiting for transfers between devices: 451 us -> none  [the longest x1 275 us: local(): lax.psum(jnp.dot(attn_cols, w_out, preferred_element_type=jnp.float32), '...]
    pmax x1 -> x0, blocking collectives: 219 us -> none  [local(): top = lax.pmax(jnp.maximum(local_top, own), 'blk')]
    all_to_all x0 -> x4, starting transfers between devices: none -> 43.1 us  [exchange(): return lax.all_to_all(value, axes, 0, 0, tiled=True)]
    all_to_all x0 -> x4, waiting for transfers between devices: none -> 36.6 us  [exchange(): return lax.all_to_all(value, axes, 0, 0, tiled=True)]
    all_gather x1, blocking collectives: 9.96 us -> 32.8 us  [gathered_rows(): return lax.all_gather(w_out, 'z', axis=0, tiled=True)]
  transfers between devices with their start and end apart: 4 -> 5, of which waited for: 4 -> 3; matrix products, arithmetic and copies ran while one was open for 0% -> 3% of each run, Pallas kernels for 0% -> 0%
where the time goes in v1:
time: 145 us; the launch traced here: 144 us
  starting transfers between devices  53.8 us (37%)
  waiting for transfers between devices  36.6 us (25%)
  blocking collectives  32.8 us (23%)
  other arithmetic  8.8 us (6%)
  local copies, waits for them, and re-layouts  7.66 us (5%)
  matrix products  3.18 us (2%)
    all_to_all x4, starting transfers between devices, exchange(): return lax.all_to_all(value, axes, 0, 0, tiled=True)  43.1 us
    all_to_all x4, waiting for transfers between devices, exchange(): return lax.all_to_all(value, axes, 0, 0, tiled=True)  36.6 us
    all_gather x1, blocking collectives, gathered_rows(): return lax.all_gather(w_out, 'z', axis=0, tiled=True)  32.8 us
    ppermute x1, starting transfers between devices, local(): partner = lax.ppermute(sent, 'guide', [(0, 1), (1, 0)])  10.7 us
  transfers between devices with their start and end apart: 5, of which 3 were waited for; matrix products, arithmetic and copies ran while one was open for 3% of the time, Pallas kernels for 0%

profile of v1, /device:TPU:1, one launch (start us, length us, event | category | flops | bytes accessed | tf_op | source)
XLA Modules:
  0.0 144.0 jit_solution(8832884430931903974)
XLA Ops:
  0.6 0.9 convert_bitcast_fusion
  1.5 0.9 multiply_reduce_fusion.2
  2.5 1.1 fusion.29
  4.7 0.6 copy-done.5
  6.4 1.2 maximum_maximum_fusion
  7.5 17.3 %all-to-all-start = ((bf16[64,48,128]{2,1,0:T(8,128)(2,1)}), bf16[64,48,128]{2,1,0:T(8,128)(2,1)S(1)}, u32[]{:S(2)}, u32[]{:S(2)}) async-start(bf16[64,48,128]{2,1,0:T(8,128)(2,1)} %maximum_maximum_fusion), calls=%async_computation | async-start | bytes 1572864 | tf_op jit(solution)/shard_map/all_to_all | solution.py:22
  24.8 0.5 broadcast.193
  25.3 0.7 reduce.8
  26.3 32.8 %all_gather.3 = bf16[192,1536]{1,0:T(8,128)(2,1)S(1)} all-gather(bf16[24,1536]{1,0:T(8,128)(2,1)S(1)} %copy-done.7), channel_id=1, replica_groups=mesh['guide'=2,'y'=8,'z'=8,'batch'=4] {'z'}, dimensions={0}, use_global_device_ids=true | all-gather | bytes 663552 | tf_op jit(solution)/shard_map/all_gather | solution.py:158
  60.7 0.8 broadcast_in_dim.33
  61.5 11.8 %all-to-all-start.1 = ((bf16[64,24,128]{2,1,0:T(8,128)(2,1)}), bf16[64,24,128]{2,1,0:T(8,128)(2,1)S(1)}, u32[]{:S(2)}, u32[]{:S(2)}) async-start(bf16[64,24,128]{2,1,0:T(8,128)(2,1)} %broadcast_in_dim.33), calls=%async_computation.1 | async-start | bytes 786432 | tf_op jit(solution)/shard_map/all_to_all | solution.py:22
  73.4 13.2 %all-to-all-done.1 = bf16[64,24,128]{2,1,0:T(8,128)(2,1)S(1)} async-done(((bf16[64,24,128]{2,1,0:T(8,128)(2,1)}), bf16[64,24,128]{2,1,0:T(8,128)(2,1)S(1)}, u32[]{:S(2)}, u32[]{:S(2)}) %all-to-all-start.1) | async-done | bytes 393248 | tf_op jit(solution)/shard_map/all_to_all | solution.py:22
  88.7 0.6 fusion.2
  89.5 0.8 pad_maximum_fusion
  90.2 4.6 %all-to-all-start.2 = ((bf16[64,8,128]{2,1,0:T(8,128)(2,1)}), bf16[64,8,128]{2,1,0:T(8,128)(2,1)S(1)}, u32[]{:S(2)}, u32[]{:S(2)}) async-start(bf16[64,8,128]{2,1,0:T(8,128)(2,1)} %pad_maximum_fusion), calls=%async_computation.2 | async-start | bytes 262144 | tf_op jit(solution)/shard_map/all_to_all | solution.py:22
  95.1 11.4 %all-to-all-done.2 = bf16[64,8,128]{2,1,0:T(8,128)(2,1)S(1)} async-done(((bf16[64,8,128]{2,1,0:T(8,128)(2,1)}), bf16[64,8,128]{2,1,0:T(8,128)(2,1)S(1)}, u32[]{:S(2)}, u32[]{:S(2)}) %all-to-all-start.2) | async-done | bytes 131104 | tf_op jit(solution)/shard_map/all_to_all | solution.py:22
  106.6 0.8 broadcast_in_dim.35
  107.3 9.3 %all-to-all-start.3 = ((bf16[256,4,128]{2,1,0:T(4,128)(2,1)}), bf16[256,4,128]{2,1,0:T(4,128)(2,1)S(1)}, u32[]{:S(2)}, u32[]{:S(2)}) async-start(bf16[256,4,128]{2,1,0:T(4,128)(2,1)} %broadcast_in_dim.35), calls=%async_computation.3 | async-start | bytes 524288 | tf_op jit(solution)/shard_map/all_to_all | solution.py:22
  117.2 12.0 %all-to-all-done.3 = bf16[256,4,128]{2,1,0:T(4,128)(2,1)S(1)} async-done(((bf16[256,4,128]{2,1,0:T(4,128)(2,1)}), bf16[256,4,128]{2,1,0:T(4,128)(2,1)S(1)}, u32[]{:S(2)}, u32[]{:S(2)}) %all-to-all-start.3) | async-done | bytes 262176 | tf_op jit(solution)/shard_map/all_to_all | solution.py:22
  129.5 1.0 multiply_reduce_fusion
  131.1 10.7 %collective-permute-start = (bf16[32,256]{1,0:T(8,128)(2,1)S(1)}, bf16[32,256]{1,0:T(8,128)(2,1)S(1)}, u32[]{:S(2)}, u32[]{:S(2)}) collective-permute-start(bf16[32,256]{1,0:T(8,128)(2,1)S(1)} %constant_dynamic-slice_fusion), channel_id=1, source_target_pairs={{0,256},{256,0},{1,257},{257,1},{2,258},{258,2},{3,259},{259,3},{4... | collective-permute-start | bytes 49160 | tf_op jit(solution)/shard_map/ppermute | solution.py:142
  141.9 0.7 slice.81
  142.6 0.7 slice.83
  143.3 0.7 convert_add_fusion
  (106 shorter events, 7.8 us)
Async XLA Ops:
  0.6 88.0 %copy-start = (bf16[256,1536]{1,0:T(8,128)(2,1)S(1)}, bf16[256,1536]{1,0:T(8,128)(2,1)}, u32[]{:S(2)}) copy-start(bf16[256,1536]{1,0:T(8,128)(2,1)} %param.25) | copy-start | bytes 2359300
  4.4 1.0 copy-start.5
  4.5 1.1 copy-start.6
  7.5 17.8 %copy-start.10 = (s32[1,16]{1,0:T(1,128)S(1)}, s32[1,16]{1,0:T(1,128)}, u32[]{:S(2)}) copy-start(s32[1,16]{1,0:T(1,128)} %param.19) | copy-start | bytes 196
  7.5 18.8 %copy-start.7 = (bf16[24,1536]{1,0:T(8,128)(2,1)S(1)}, bf16[24,1536]{1,0:T(8,128)(2,1)}, u32[]{:S(2)}) copy-start(bf16[24,1536]{1,0:T(8,128)(2,1)} %param.20) | copy-start | bytes 221188
  7.5 51.7 %all-to-all-start = ((bf16[64,48,128]{2,1,0:T(8,128)(2,1)}), bf16[64,48,128]{2,1,0:T(8,128)(2,1)S(1)}, u32[]{:S(2)}, u32[]{:S(2)}) async-start(bf16[64,48,128]{2,1,0:T(8,128)(2,1)} %maximum_maximum_fusion), calls=%async_computation | async-start | bytes 1572864 | tf_op jit(solution)/shard_map/all_to_all | solution.py:22
  61.5 25.2 %all-to-all-start.1 = ((bf16[64,24,128]{2,1,0:T(8,128)(2,1)}), bf16[64,24,128]{2,1,0:T(8,128)(2,1)S(1)}, u32[]{:S(2)}, u32[]{:S(2)}) async-start(bf16[64,24,128]{2,1,0:T(8,128)(2,1)} %broadcast_in_dim.33), calls=%async_computation.1 | async-start | bytes 786432 | tf_op jit(solution)/shard_map/all_to_all | solution.py:22
  73.4 14.0 %copy-start.1 = (bf16[1,16,1536]{2,1,0:T(8,128)(2,1)S(1)}, bf16[1,16,1536]{2,1,0:T(8,128)(2,1)}, u32[]{:S(2)}) copy-start(bf16[1,16,1536]{2,1,0:T(8,128)(2,1)} %param.15) | copy-start | bytes 147460
  87.1 0.8 copy-start.8
  87.1 0.9 copy-start.9
  87.1 1.2 copy-start.4
  87.5 1.2 copy-start.2
  90.2 16.2 %all-to-all-start.2 = ((bf16[64,8,128]{2,1,0:T(8,128)(2,1)}), bf16[64,8,128]{2,1,0:T(8,128)(2,1)S(1)}, u32[]{:S(2)}, u32[]{:S(2)}) async-start(bf16[64,8,128]{2,1,0:T(8,128)(2,1)} %pad_maximum_fusion), calls=%async_computation.2 | async-start | bytes 262144 | tf_op jit(solution)/shard_map/all_to_all | solution.py:22
  94.8 21.8 %copy-start.11 = (f32[8]{0:T(128)S(1)}, f32[8]{0:T(128)}, u32[]{:S(2)}) copy-start(f32[8]{0:T(128)} %param.29) | copy-start | bytes 100
  94.8 21.8 %copy-start.12 = (s32[8]{0:T(128)S(1)}, s32[8]{0:T(128)}, u32[]{:S(2)}) copy-start(s32[8]{0:T(128)} %param.28) | copy-start | bytes 100
  94.9 22.0 %copy-start.13 = (s32[64]{0:T(128)S(1)}, s32[64]{0:T(128)}, u32[]{:S(2)}) copy-start(s32[64]{0:T(128)} %param.27) | copy-start | bytes 772
  107.3 21.9 %all-to-all-start.3 = ((bf16[256,4,128]{2,1,0:T(4,128)(2,1)}), bf16[256,4,128]{2,1,0:T(4,128)(2,1)S(1)}, u32[]{:S(2)}, u32[]{:S(2)}) async-start(bf16[256,4,128]{2,1,0:T(4,128)(2,1)} %broadcast_in_dim.35), calls=%async_computation.3 | async-start | bytes 524288 | tf_op jit(solution)/shard_map/all_to_all | solution.py:22
  129.2 1.5 %copy-start.3 = (bf16[1536,256]{1,0:T(8,128)(2,1)S(1)}, bf16[1536,256]{1,0:T(8,128)(2,1)}, u32[]{:S(2)}) copy-start(bf16[1536,256]{1,0:T(8,128)(2,1)} %param.26) | copy-start | bytes 2359300
  131.1 12.3 %collective-permute-start = (bf16[32,256]{1,0:T(8,128)(2,1)S(1)}, bf16[32,256]{1,0:T(8,128)(2,1)S(1)}, u32[]{:S(2)}, u32[]{:S(2)}) collective-permute-start(bf16[32,256]{1,0:T(8,128)(2,1)S(1)} %constant_dynamic-slice_fusion), channel_id=1, source_target_pairs={{0,256},{256,0},{1,257},{257,1},{2,258},{258,2},{3,259},{259,3},{4... | collective-permute-start | bytes 49160 | tf_op jit(solution)/shard_map/ppermute | solution.py:142

commit v2 on v1

--- a/solution.py
+++ b/solution.py
@@ -155,7 +155,13 @@
 
 
 def gathered_rows(w_out):
-    return lax.all_gather(w_out, "z", axis=0, tiled=True)
+    rows, width = w_out.shape
+    size = lax.axis_size("z") * width * 2
+    want = -(-(2**20) // size)
+    want += -want % 4
+    padded = jnp.concatenate([w_out, w_out[: want - rows]], axis=0)
+    gathered = lax.all_gather(padded, "z", axis=0, tiled=False)
+    return gathered[:, :rows].reshape(-1, width)
 
 
 def solution(mesh):

time: 145 us -> 164 us (1.13)
  waiting for transfers between devices: 36.6 us -> 76.1 us
  blocking collectives: 32.8 us -> 0 us
  between operations: 1.17 us -> 14.5 us
  starting transfers between devices: 53.8 us -> 50.7 us
    all_gather x1 -> x0, blocking collectives: 32.8 us -> none  [gathered_rows(): return lax.all_gather(w_out, 'z', axis=0, tiled=True)]
    all_gather x0 -> x1, waiting for transfers between devices: none -> 20.5 us  [gathered_rows(): gathered = lax.all_gather(padded, 'z', axis=0, tiled=False)]
    all_to_all x4, waiting for transfers between devices: 36.6 us -> 55.6 us  [exchange(): return lax.all_to_all(value, axes, 0, 0, tiled=True)]
    all_to_all x4, starting transfers between devices: 43.1 us -> 40.7 us  [exchange(): return lax.all_to_all(value, axes, 0, 0, tiled=True)]
  transfers between devices with their start and end apart: 5 -> 6, of which waited for: 3 -> 5; matrix products, arithmetic and copies ran while one was open for 3% -> 4% of each run, Pallas kernels for 0% -> 0%
where the time goes in v2:
time: 164 us; the launch traced here: 163 us
  waiting for transfers between devices  76.1 us (46%)
  starting transfers between devices  50.7 us (31%)
  between operations  14.5 us (9%)
  other arithmetic  9.51 us (6%)
  local copies, waits for them, and re-layouts  8.32 us (5%)
  matrix products  4.31 us (3%)
    all_to_all x4, waiting for transfers between devices, exchange(): return lax.all_to_all(value, axes, 0, 0, tiled=True)  55.6 us
    all_to_all x4, starting transfers between devices, exchange(): return lax.all_to_all(value, axes, 0, 0, tiled=True)  40.7 us
    all_gather x1, waiting for transfers between devices, gathered_rows(): gathered = lax.all_gather(padded, 'z', axis=0, tiled=False)  20.5 us
    ppermute x1, starting transfers between devices, local(): partner = lax.ppermute(sent, 'guide', [(0, 1), (1, 0)])  9.94 us
  transfers between devices with their start and end apart: 6, of which 5 were waited for; matrix products, arithmetic and copies ran while one was open for 4% of the time, Pallas kernels for 0%

profile of v2, /device:TPU:1, one launch (start us, length us, event | category | flops | bytes accessed | tf_op | source)
XLA Modules:
  0.0 163.4 jit_solution(6202291418831958683)
XLA Ops:
  7.2 0.9 convert_bitcast_fusion
  8.1 0.9 multiply_reduce_fusion.2
  9.0 1.1 fusion.29
  12.6 1.2 maximum_maximum_fusion
  13.8 17.3 %all-to-all-start = ((bf16[64,48,128]{2,1,0:T(8,128)(2,1)}), bf16[64,48,128]{2,1,0:T(8,128)(2,1)S(1)}, u32[]{:S(2)}, u32[]{:S(2)}) async-start(bf16[64,48,128]{2,1,0:T(8,128)(2,1)} %maximum_maximum_fusion), calls=%async_computation | async-start | bytes 1572864 | tf_op jit(solution)/shard_map/all_to_all | solution.py:22
  31.2 0.7 maximum_bitcast_fusion.2
  33.4 18.9 %all-to-all-done = bf16[64,48,128]{2,1,0:T(8,128)(2,1)S(1)} async-done(((bf16[64,48,128]{2,1,0:T(8,128)(2,1)}), bf16[64,48,128]{2,1,0:T(8,128)(2,1)S(1)}, u32[]{:S(2)}, u32[]{:S(2)}) %all-to-all-start) | async-done | bytes 786464 | tf_op jit(solution)/shard_map/all_to_all | solution.py:22
  53.6 20.5 %all-gather.4.cloned.1.call-done = bf16[8,44,1536]{2,1,0:T(8,128)(2,1)} async-done(((bf16[1,44,1536]{2,1,0:T(8,128)(2,1)}), bf16[8,44,1536]{2,1,0:T(8,128)(2,1)}) %all-gather.4.cloned.1.call-update) | async-done | bytes 1081360 | tf_op jit(solution)/shard_map/all_gather | solution.py:163
  74.1 1.1 slice-done
  75.3 0.8 broadcast_in_dim.33
  76.1 9.5 %all-to-all-start.1 = ((bf16[64,24,128]{2,1,0:T(8,128)(2,1)}), bf16[64,24,128]{2,1,0:T(8,128)(2,1)S(1)}, u32[]{:S(2)}, u32[]{:S(2)}) async-start(bf16[64,24,128]{2,1,0:T(8,128)(2,1)} %broadcast_in_dim.33), calls=%async_computation.1 | async-start | bytes 786432 | tf_op jit(solution)/shard_map/all_to_all | solution.py:22
  85.7 13.3 %all-to-all-done.1 = bf16[64,24,128]{2,1,0:T(8,128)(2,1)S(1)} async-done(((bf16[64,24,128]{2,1,0:T(8,128)(2,1)}), bf16[64,24,128]{2,1,0:T(8,128)(2,1)S(1)}, u32[]{:S(2)}, u32[]{:S(2)}) %all-to-all-start.1) | async-done | bytes 393248 | tf_op jit(solution)/shard_map/all_to_all | solution.py:22
  100.5 1.4 fusion.47
  102.8 0.8 pad_maximum_fusion
  103.5 4.6 %all-to-all-start.2 = ((bf16[64,8,128]{2,1,0:T(8,128)(2,1)}), bf16[64,8,128]{2,1,0:T(8,128)(2,1)S(1)}, u32[]{:S(2)}, u32[]{:S(2)}) async-start(bf16[64,8,128]{2,1,0:T(8,128)(2,1)} %pad_maximum_fusion), calls=%async_computation.2 | async-start | bytes 262144 | tf_op jit(solution)/shard_map/all_to_all | solution.py:22
  108.4 11.4 %all-to-all-done.2 = bf16[64,8,128]{2,1,0:T(8,128)(2,1)S(1)} async-done(((bf16[64,8,128]{2,1,0:T(8,128)(2,1)}), bf16[64,8,128]{2,1,0:T(8,128)(2,1)S(1)}, u32[]{:S(2)}, u32[]{:S(2)}) %all-to-all-start.2) | async-done | bytes 131104 | tf_op jit(solution)/shard_map/all_to_all | solution.py:22
  119.9 0.8 broadcast_in_dim.35
  120.6 9.3 %all-to-all-start.3 = ((bf16[256,4,128]{2,1,0:T(4,128)(2,1)}), bf16[256,4,128]{2,1,0:T(4,128)(2,1)S(1)}, u32[]{:S(2)}, u32[]{:S(2)}) async-start(bf16[256,4,128]{2,1,0:T(4,128)(2,1)} %broadcast_in_dim.35), calls=%async_computation.3 | async-start | bytes 524288 | tf_op jit(solution)/shard_map/all_to_all | solution.py:22
  130.5 12.0 %all-to-all-done.3 = bf16[256,4,128]{2,1,0:T(4,128)(2,1)S(1)} async-done(((bf16[256,4,128]{2,1,0:T(4,128)(2,1)}), bf16[256,4,128]{2,1,0:T(4,128)(2,1)S(1)}, u32[]{:S(2)}, u32[]{:S(2)}) %all-to-all-start.3) | async-done | bytes 262176 | tf_op jit(solution)/shard_map/all_to_all | solution.py:22
  142.8 1.0 multiply_reduce_fusion
  144.4 9.9 %collective-permute-start = (bf16[32,256]{1,0:T(8,128)(2,1)S(1)}, bf16[32,256]{1,0:T(8,128)(2,1)S(1)}, u32[]{:S(2)}, u32[]{:S(2)}) collective-permute-start(bf16[32,256]{1,0:T(8,128)(2,1)S(1)} %constant_dynamic-slice_fusion), channel_id=1, source_target_pairs={{0,256},{256,0},{1,257},{257,1},{2,258},{258,2},{3,259},{259,3},{4... | collective-permute-start | bytes 49160 | tf_op jit(solution)/shard_map/ppermute | solution.py:142
  154.5 0.7 slice.89
  155.2 0.7 slice.91
  155.9 0.7 convert_add_fusion
  (109 shorter events, 9.6 us)
Async XLA Ops:
  7.2 94.8 %copy-start = (bf16[256,1536]{1,0:T(8,128)(2,1)S(1)}, bf16[256,1536]{1,0:T(8,128)(2,1)}, u32[]{:S(2)}) copy-start(bf16[256,1536]{1,0:T(8,128)(2,1)} %param.25) | copy-start | bytes 2359300
  10.3 1.0 copy-start.5
  10.9 1.0 copy-start.6
  13.8 17.3 %copy-start.4 = (bf16[24,1536]{1,0:T(8,128)(2,1)S(1)}, bf16[24,1536]{1,0:T(8,128)(2,1)}, u32[]{:S(2)}) copy-start(bf16[24,1536]{1,0:T(8,128)(2,1)} %param.20) | copy-start | bytes 221188
  13.8 18.5 %copy-start.9 = (s32[1,16]{1,0:T(1,128)S(1)}, s32[1,16]{1,0:T(1,128)}, u32[]{:S(2)}) copy-start(s32[1,16]{1,0:T(1,128)} %param.19) | copy-start | bytes 196
  13.8 38.5 %all-to-all-start = ((bf16[64,48,128]{2,1,0:T(8,128)(2,1)}), bf16[64,48,128]{2,1,0:T(8,128)(2,1)S(1)}, u32[]{:S(2)}, u32[]{:S(2)}) async-start(bf16[64,48,128]{2,1,0:T(8,128)(2,1)} %maximum_maximum_fusion), calls=%async_computation | async-start | bytes 1572864 | tf_op jit(solution)/shard_map/all_to_all | solution.py:22
  31.1 43.0 %all-gather.4.cloned.1.call-start = ((), (), s32[]{:S(2)}) async-start(), calls=%async_computation.4 | async-start | bytes 1327104 | tf_op jit(solution)/shard_map/all_gather | solution.py:163
  74.1 1.1 slice-start
  76.1 22.9 %all-to-all-start.1 = ((bf16[64,24,128]{2,1,0:T(8,128)(2,1)}), bf16[64,24,128]{2,1,0:T(8,128)(2,1)S(1)}, u32[]{:S(2)}, u32[]{:S(2)}) async-start(bf16[64,24,128]{2,1,0:T(8,128)(2,1)} %broadcast_in_dim.33), calls=%async_computation.1 | async-start | bytes 786432 | tf_op jit(solution)/shard_map/all_to_all | solution.py:22
  85.6 14.1 %copy-start.1 = (bf16[1,16,1536]{2,1,0:T(8,128)(2,1)S(1)}, bf16[1,16,1536]{2,1,0:T(8,128)(2,1)}, u32[]{:S(2)}) copy-start(bf16[1,16,1536]{2,1,0:T(8,128)(2,1)} %param.15) | copy-start | bytes 147460
  85.7 14.3 %copy-start.7 = (bf16[1536,16]{0,1:T(8,128)(2,1)S(1)}, bf16[1536,16]{0,1:T(8,128)(2,1)}, u32[]{:S(2)}) copy-start(bf16[1536,16]{0,1:T(8,128)(2,1)} %param.21) | copy-start | bytes 147460
  85.7 14.4 %copy-start.8 = (s32[1,16,2]{1,2,0:T(2,128)S(1)}, s32[1,16,2]{1,2,0:T(2,128)}, u32[]{:S(2)}) copy-start(s32[1,16,2]{1,2,0:T(2,128)} %param.22) | copy-start | bytes 388
  99.4 2.5 %copy-start.2 = (bf16[1536,256]{1,0:T(8,128)(2,1)S(1)}, bf16[1536,256]{1,0:T(8,128)(2,1)}, u32[]{:S(2)}) copy-start(bf16[1536,256]{1,0:T(8,128)(2,1)} %param.24) | copy-start | bytes 2359300
  102.7 27.3 %copy-start.10 = (f32[8]{0:T(128)S(1)}, f32[8]{0:T(128)}, u32[]{:S(2)}) copy-start(f32[8]{0:T(128)} %param.29) | copy-start | bytes 100
  102.7 27.3 %copy-start.11 = (s32[8]{0:T(128)S(1)}, s32[8]{0:T(128)}, u32[]{:S(2)}) copy-start(s32[8]{0:T(128)} %param.28) | copy-start | bytes 100
  102.7 27.5 %copy-start.12 = (s32[64]{0:T(128)S(1)}, s32[64]{0:T(128)}, u32[]{:S(2)}) copy-start(s32[64]{0:T(128)} %param.27) | copy-start | bytes 772
  103.5 16.2 %all-to-all-start.2 = ((bf16[64,8,128]{2,1,0:T(8,128)(2,1)}), bf16[64,8,128]{2,1,0:T(8,128)(2,1)S(1)}, u32[]{:S(2)}, u32[]{:S(2)}) async-start(bf16[64,8,128]{2,1,0:T(8,128)(2,1)} %pad_maximum_fusion), calls=%async_computation.2 | async-start | bytes 262144 | tf_op jit(solution)/shard_map/all_to_all | solution.py:22
  120.6 21.9 %all-to-all-start.3 = ((bf16[256,4,128]{2,1,0:T(4,128)(2,1)}), bf16[256,4,128]{2,1,0:T(4,128)(2,1)S(1)}, u32[]{:S(2)}, u32[]{:S(2)}) async-start(bf16[256,4,128]{2,1,0:T(4,128)(2,1)} %broadcast_in_dim.35), calls=%async_computation.3 | async-start | bytes 524288 | tf_op jit(solution)/shard_map/all_to_all | solution.py:22
  130.0 14.1 %copy-start.3 = (bf16[1536,256]{1,0:T(8,128)(2,1)S(1)}, bf16[1536,256]{1,0:T(8,128)(2,1)}, u32[]{:S(2)}) copy-start(bf16[1536,256]{1,0:T(8,128)(2,1)} %param.26) | copy-start | bytes 2359300
  144.4 11.5 %collective-permute-start = (bf16[32,256]{1,0:T(8,128)(2,1)S(1)}, bf16[32,256]{1,0:T(8,128)(2,1)S(1)}, u32[]{:S(2)}, u32[]{:S(2)}) collective-permute-start(bf16[32,256]{1,0:T(8,128)(2,1)S(1)} %constant_dynamic-slice_fusion), channel_id=1, source_target_pairs={{0,256},{256,0},{1,257},{257,1},{2,258},{258,2},{3,259},{259,3},{4... | collective-permute-start | bytes 49160 | tf_op jit(solution)/shard_map/ppermute | solution.py:142
Sparse Core Ops, SparseCore 0:
  34.0 39.9 all-gather.3

commit v3 on v2

--- a/solution.py
+++ b/solution.py
@@ -75,6 +75,7 @@
     kv = kv.reshape(blocks, pair * span, 2 * HEAD_DIM)
     fill = jnp.zeros((blocks, 4, 2 * HEAD_DIM), BF16)
     got = exchange(jnp.concatenate([kv, high, low, fill], axis=1), BLK)
+    got, head_w = lax.optimization_barrier((got, head_w))
 
     n_kv, n_l = pair * span, pair * group
     kv = got[:, :n_kv].reshape(blocks, pair, span, 2 * HEAD_DIM).transpose(1, 0, 2, 3)

time: 164 us -> 160 us (0.976)
  waiting for transfers between devices: 76.1 us -> 70.4 us
  starting transfers between devices: 50.7 us -> 52.5 us
    all_to_all x4, waiting for transfers between devices: 55.6 us -> 36.8 us  [exchange(): return lax.all_to_all(value, axes, 0, 0, tiled=True)]
    all_gather x1, waiting for transfers between devices: 20.5 us -> 33.6 us  [gathered_rows(): gathered = lax.all_gather(padded, 'z', axis=0, tiled=False)]
    all_to_all x4, starting transfers between devices: 40.7 us -> 44.3 us  [exchange(): return lax.all_to_all(value, axes, 0, 0, tiled=True)]
    ppermute x1, starting transfers between devices: 9.94 us -> 8.15 us  [local(): partner = lax.ppermute(sent, 'guide', [(0, 1), (1, 0)])]
  transfers between devices with their start and end apart: 6 -> 6, of which waited for: 5 -> 4; matrix products, arithmetic and copies ran while one was open for 4% -> 6% of each run, Pallas kernels for 0% -> 0%
where the time goes in v3:
time: 160 us; the launch traced here: 159 us
  waiting for transfers between devices  70.4 us (44%)
  starting transfers between devices  52.5 us (33%)
  between operations  14.5 us (9%)
  other arithmetic  10.4 us (6%)
  local copies, waits for them, and re-layouts  7.26 us (5%)
  matrix products  4.33 us (3%)
    all_to_all x4, starting transfers between devices, exchange(): return lax.all_to_all(value, axes, 0, 0, tiled=True)  44.3 us
    all_to_all x4, waiting for transfers between devices, exchange(): return lax.all_to_all(value, axes, 0, 0, tiled=True)  36.8 us
    all_gather x1, waiting for transfers between devices, gathered_rows(): gathered = lax.all_gather(padded, 'z', axis=0, tiled=False)  33.6 us
    ppermute x1, starting transfers between devices, local(): partner = lax.ppermute(sent, 'guide', [(0, 1), (1, 0)])  8.15 us
  transfers between devices with their start and end apart: 6, of which 4 were waited for; matrix products, arithmetic and copies ran while one was open for 6% of the time, Pallas kernels for 0%

profile of v3, /device:TPU:1, one launch (start us, length us, event | category | flops | bytes accessed | tf_op | source)
XLA Modules:
  0.0 159.5 jit_solution(11302114384441289766)
XLA Ops:
  7.2 1.7 %maximum_bitcast_fusion.2 = bf16[1,44,1536]{2,1,0:T(8,128)(2,1)} fusion(bf16[20,1536]{1,0:T(8,128)(2,1)} %bitcast.81, bf16[24,1536]{1,0:T(8,128)(2,1)} %param.20), kind=kLoop, calls=%fused_computation.26 | loop fusion | flops 270336 | bytes 270336
  8.9 0.8 convert_bitcast_fusion
  9.7 0.9 multiply_reduce_fusion.2
  10.7 1.1 fusion.29
  14.3 1.2 maximum_maximum_fusion
  15.5 17.3 %all-to-all-start = ((bf16[64,48,128]{2,1,0:T(8,128)(2,1)}), bf16[64,48,128]{2,1,0:T(8,128)(2,1)S(1)}, u32[]{:S(2)}, u32[]{:S(2)}) async-start(bf16[64,48,128]{2,1,0:T(8,128)(2,1)} %maximum_maximum_fusion), calls=%async_computation | async-start | bytes 1572864 | tf_op jit(solution)/shard_map/all_to_all | solution.py:22
  33.3 0.7 reduce.8
  34.3 33.6 %all-gather.4.cloned.1.call-done = bf16[8,44,1536]{2,1,0:T(8,128)(2,1)} async-done(((bf16[1,44,1536]{2,1,0:T(8,128)(2,1)}), bf16[8,44,1536]{2,1,0:T(8,128)(2,1)}) %all-gather.4.cloned.1.call-update) | async-done | bytes 1081360 | tf_op jit(solution)/shard_map/all_gather | solution.py:164
  69.4 0.8 broadcast_in_dim.33
  70.2 12.3 %all-to-all-start.1 = ((bf16[64,24,128]{2,1,0:T(8,128)(2,1)}), bf16[64,24,128]{2,1,0:T(8,128)(2,1)S(1)}, u32[]{:S(2)}, u32[]{:S(2)}) async-start(bf16[64,24,128]{2,1,0:T(8,128)(2,1)} %broadcast_in_dim.33), calls=%async_computation.1 | async-start | bytes 786432 | tf_op jit(solution)/shard_map/all_to_all | solution.py:22
  82.6 13.4 %all-to-all-done.1 = bf16[64,24,128]{2,1,0:T(8,128)(2,1)S(1)} async-done(((bf16[64,24,128]{2,1,0:T(8,128)(2,1)}), bf16[64,24,128]{2,1,0:T(8,128)(2,1)S(1)}, u32[]{:S(2)}, u32[]{:S(2)}) %all-to-all-start.1) | async-done | bytes 393248 | tf_op jit(solution)/shard_map/all_to_all | solution.py:22
  97.5 1.4 fusion.47
  99.0 0.6 fusion.2
  99.8 0.8 pad_maximum_fusion
  100.6 4.6 %all-to-all-start.2 = ((bf16[64,8,128]{2,1,0:T(8,128)(2,1)}), bf16[64,8,128]{2,1,0:T(8,128)(2,1)S(1)}, u32[]{:S(2)}, u32[]{:S(2)}) async-start(bf16[64,8,128]{2,1,0:T(8,128)(2,1)} %pad_maximum_fusion), calls=%async_computation.2 | async-start | bytes 262144 | tf_op jit(solution)/shard_map/all_to_all | solution.py:22
  105.4 11.4 %all-to-all-done.2 = bf16[64,8,128]{2,1,0:T(8,128)(2,1)S(1)} async-done(((bf16[64,8,128]{2,1,0:T(8,128)(2,1)}), bf16[64,8,128]{2,1,0:T(8,128)(2,1)S(1)}, u32[]{:S(2)}, u32[]{:S(2)}) %all-to-all-start.2) | async-done | bytes 131104 | tf_op jit(solution)/shard_map/all_to_all | solution.py:22
  116.9 0.8 broadcast_in_dim.35
  117.7 10.1 %all-to-all-start.3 = ((bf16[256,4,128]{2,1,0:T(4,128)(2,1)}), bf16[256,4,128]{2,1,0:T(4,128)(2,1)S(1)}, u32[]{:S(2)}, u32[]{:S(2)}) async-start(bf16[256,4,128]{2,1,0:T(4,128)(2,1)} %broadcast_in_dim.35), calls=%async_computation.3 | async-start | bytes 524288 | tf_op jit(solution)/shard_map/all_to_all | solution.py:22
  128.3 12.0 %all-to-all-done.3 = bf16[256,4,128]{2,1,0:T(4,128)(2,1)S(1)} async-done(((bf16[256,4,128]{2,1,0:T(4,128)(2,1)}), bf16[256,4,128]{2,1,0:T(4,128)(2,1)S(1)}, u32[]{:S(2)}, u32[]{:S(2)}) %all-to-all-start.3) | async-done | bytes 262176 | tf_op jit(solution)/shard_map/all_to_all | solution.py:22
  140.6 1.0 multiply_reduce_fusion
  142.2 8.2 %collective-permute-start = (bf16[32,256]{1,0:T(8,128)(2,1)S(1)}, bf16[32,256]{1,0:T(8,128)(2,1)S(1)}, u32[]{:S(2)}, u32[]{:S(2)}) collective-permute-start(bf16[32,256]{1,0:T(8,128)(2,1)S(1)} %constant_dynamic-slice_fusion), channel_id=1, source_target_pairs={{0,256},{256,0},{1,257},{257,1},{2,258},{258,2},{3,259},{259,3},{4... | collective-permute-start | bytes 49160 | tf_op jit(solution)/shard_map/ppermute | solution.py:143
  150.5 0.7 slice.89
  151.2 0.7 slice.91
  151.9 0.7 convert_add_fusion
  (107 shorter events, 8.3 us)
Async XLA Ops:
  7.2 91.8 %copy-start = (bf16[256,1536]{1,0:T(8,128)(2,1)S(1)}, bf16[256,1536]{1,0:T(8,128)(2,1)}, u32[]{:S(2)}) copy-start(bf16[256,1536]{1,0:T(8,128)(2,1)} %param.25) | copy-start | bytes 2359300
  7.2 60.7 %all-gather.4.cloned.1.call-start = ((), (), s32[]{:S(2)}) async-start(), calls=%async_computation.4 | async-start | bytes 1327104 | tf_op jit(solution)/shard_map/all_gather | solution.py:164
  12.0 1.0 copy-start.4
  12.5 1.0 copy-start.5
  15.5 17.8 %copy-start.8 = (s32[1,16]{1,0:T(1,128)S(1)}, s32[1,16]{1,0:T(1,128)}, u32[]{:S(2)}) copy-start(s32[1,16]{1,0:T(1,128)} %param.19) | copy-start | bytes 196
  15.5 52.4 %all-to-all-start = ((bf16[64,48,128]{2,1,0:T(8,128)(2,1)}), bf16[64,48,128]{2,1,0:T(8,128)(2,1)S(1)}, u32[]{:S(2)}, u32[]{:S(2)}) async-start(bf16[64,48,128]{2,1,0:T(8,128)(2,1)} %maximum_maximum_fusion), calls=%async_computation | async-start | bytes 1572864 | tf_op jit(solution)/shard_map/all_to_all | solution.py:22
  68.0 1.2 slice-start
  70.2 25.8 %all-to-all-start.1 = ((bf16[64,24,128]{2,1,0:T(8,128)(2,1)}), bf16[64,24,128]{2,1,0:T(8,128)(2,1)S(1)}, u32[]{:S(2)}, u32[]{:S(2)}) async-start(bf16[64,24,128]{2,1,0:T(8,128)(2,1)} %broadcast_in_dim.33), calls=%async_computation.1 | async-start | bytes 786432 | tf_op jit(solution)/shard_map/all_to_all | solution.py:22
  82.5 14.3 %copy-start.1 = (bf16[1,16,1536]{2,1,0:T(8,128)(2,1)S(1)}, bf16[1,16,1536]{2,1,0:T(8,128)(2,1)}, u32[]{:S(2)}) copy-start(bf16[1,16,1536]{2,1,0:T(8,128)(2,1)} %param.15) | copy-start | bytes 147460
  82.6 14.5 %copy-start.6 = (bf16[1536,16]{0,1:T(8,128)(2,1)S(1)}, bf16[1536,16]{0,1:T(8,128)(2,1)}, u32[]{:S(2)}) copy-start(bf16[1536,16]{0,1:T(8,128)(2,1)} %param.21) | copy-start | bytes 147460
  82.6 14.6 %copy-start.7 = (s32[1,16,2]{1,2,0:T(2,128)S(1)}, s32[1,16,2]{1,2,0:T(2,128)}, u32[]{:S(2)}) copy-start(s32[1,16,2]{1,2,0:T(2,128)} %param.22) | copy-start | bytes 388
  96.5 2.5 %copy-start.2 = (bf16[1536,256]{1,0:T(8,128)(2,1)S(1)}, bf16[1536,256]{1,0:T(8,128)(2,1)}, u32[]{:S(2)}) copy-start(bf16[1536,256]{1,0:T(8,128)(2,1)} %param.24) | copy-start | bytes 2359300
  99.7 28.2 %copy-start.9 = (f32[8]{0:T(128)S(1)}, f32[8]{0:T(128)}, u32[]{:S(2)}) copy-start(f32[8]{0:T(128)} %param.29) | copy-start | bytes 100
  99.7 28.2 %copy-start.10 = (s32[8]{0:T(128)S(1)}, s32[8]{0:T(128)}, u32[]{:S(2)}) copy-start(s32[8]{0:T(128)} %param.28) | copy-start | bytes 100
  99.7 28.3 %copy-start.11 = (s32[64]{0:T(128)S(1)}, s32[64]{0:T(128)}, u32[]{:S(2)}) copy-start(s32[64]{0:T(128)} %param.27) | copy-start | bytes 772
  100.6 16.3 %all-to-all-start.2 = ((bf16[64,8,128]{2,1,0:T(8,128)(2,1)}), bf16[64,8,128]{2,1,0:T(8,128)(2,1)S(1)}, u32[]{:S(2)}, u32[]{:S(2)}) async-start(bf16[64,8,128]{2,1,0:T(8,128)(2,1)} %pad_maximum_fusion), calls=%async_computation.2 | async-start | bytes 262144 | tf_op jit(solution)/shard_map/all_to_all | solution.py:22
  117.7 22.7 %all-to-all-start.3 = ((bf16[256,4,128]{2,1,0:T(4,128)(2,1)}), bf16[256,4,128]{2,1,0:T(4,128)(2,1)S(1)}, u32[]{:S(2)}, u32[]{:S(2)}) async-start(bf16[256,4,128]{2,1,0:T(4,128)(2,1)} %broadcast_in_dim.35), calls=%async_computation.3 | async-start | bytes 524288 | tf_op jit(solution)/shard_map/all_to_all | solution.py:22
  127.8 14.1 %copy-start.3 = (bf16[1536,256]{1,0:T(8,128)(2,1)S(1)}, bf16[1536,256]{1,0:T(8,128)(2,1)}, u32[]{:S(2)}) copy-start(bf16[1536,256]{1,0:T(8,128)(2,1)} %param.26) | copy-start | bytes 2359300
  142.2 9.7 %collective-permute-start = (bf16[32,256]{1,0:T(8,128)(2,1)S(1)}, bf16[32,256]{1,0:T(8,128)(2,1)S(1)}, u32[]{:S(2)}, u32[]{:S(2)}) collective-permute-start(bf16[32,256]{1,0:T(8,128)(2,1)S(1)} %constant_dynamic-slice_fusion), channel_id=1, source_target_pairs={{0,256},{256,0},{1,257},{257,1},{2,258},{258,2},{3,259},{259,3},{4... | collective-permute-start | bytes 49160 | tf_op jit(solution)/shard_map/ppermute | solution.py:143
Sparse Core Ops, SparseCore 0:
  10.1 57.7 all-gather.3

commit v4 on v1

--- a/solution.py
+++ b/solution.py
@@ -54,36 +54,38 @@
     width = hidden.shape[2]
     width_q = HEADS * HEAD_DIM
     width_k = KV_HEADS * HEAD_DIM
-    head_w = gathered_rows(w_out)
-
     x = hidden[0].astype(F32)
     normed = rms(x).astype(BF16)
     rows = w_qkv.shape[0]
     part = lax.dynamic_slice_in_dim(normed, block * rows, rows, 1)
     qkv = jnp.dot(part, w_qkv, preferred_element_type=F32)
-    q = qkv[:, :width_q].reshape(pair, nz, KV_HEADS, group, HEAD_DIM)
-    k = qkv[:, width_q : width_q + width_k].reshape(pair, nz, KV_HEADS, 1, HEAD_DIM)
-    v = qkv[:, width_q + width_k :].reshape(pair, nz, KV_HEADS, 1, HEAD_DIM)
-    upper = jnp.concatenate([k, v, jnp.zeros_like(k)], axis=3)
-    lines = jnp.concatenate([q, upper], axis=4).transpose(2, 1, 0, 3, 4)
-    lines = lines.reshape(blocks, pair * group, 2 * HEAD_DIM)
-    high, low = halves(lines)
+    q = qkv[:, :width_q].reshape(pair, nz, KV_HEADS, group * HEAD_DIM)
+    k = qkv[:, width_q : width_q + width_k].reshape(pair, nz, KV_HEADS, HEAD_DIM)
+    v = qkv[:, width_q + width_k :].reshape(pair, nz, KV_HEADS, HEAD_DIM)
+    lines = jnp.concatenate([q, k, v], axis=3).transpose(2, 1, 0, 3)
+    n_l = pair * (group + 2) * HEAD_DIM // 128
+    high, low = halves(lines.reshape(blocks, n_l, 128))
     span = key_cache.shape[2]
     kc = key_cache[0].reshape(pair, nz, span, KV_HEADS, HEAD_DIM)
     vc = value_cache[0].reshape(pair, nz, span, KV_HEADS, HEAD_DIM)
     kv = jnp.concatenate([kc, vc], axis=4).transpose(3, 1, 0, 2, 4)
     kv = kv.reshape(blocks, pair * span, 2 * HEAD_DIM)
-    fill = jnp.zeros((blocks, 4, 2 * HEAD_DIM), BF16)
-    got = exchange(jnp.concatenate([kv, high, low, fill], axis=1), BLK)
+    cols = width // blocks
+    w_rows = w_out.shape[0]
+    n_w = -(-w_rows * cols // 128)
+    w_blocks = w_out.reshape(w_rows, blocks, cols).transpose(1, 0, 2).reshape(blocks, w_rows * cols)
+    w_blocks = jnp.pad(w_blocks, ((0, 0), (0, n_w * 128 - w_rows * cols))).reshape(blocks, n_w, 128)
+    got = exchange(jnp.concatenate([kv, high, low, w_blocks], axis=1), BLK)
 
-    n_kv, n_l = pair * span, pair * group
+    n_kv = pair * span
+    w_cols = got[:, n_kv + 2 * n_l :].reshape(blocks, n_w * 128)[:, : w_rows * cols].reshape(-1, cols)
     kv = got[:, :n_kv].reshape(blocks, pair, span, 2 * HEAD_DIM).transpose(1, 0, 2, 3)
     kv = kv.reshape(pair, blocks * span, 2 * HEAD_DIM)
     sums = jnp.sum(
         got[:, n_kv : n_kv + n_l].astype(F32) + got[:, n_kv + n_l : n_kv + 2 * n_l].astype(F32), axis=0
     )
-    sums = sums.reshape(pair, group, 2 * HEAD_DIM).astype(BF16)
-    query, new_k, new_v = sums[:, :, :HEAD_DIM], sums[:, 0, HEAD_DIM:], sums[:, 1, HEAD_DIM:]
+    sums = sums.reshape(pair, group + 2, HEAD_DIM).astype(BF16)
+    query, new_k, new_v = sums[:, :group], sums[:, group], sums[:, group + 1]
     scale = HEAD_DIM ** (-0.5)
     scores = jnp.einsum("ihd,ipd->ihp", query, kv[:, :, :HEAD_DIM], preferred_element_type=F32) * scale
     own = jnp.sum(query.astype(F32) * new_k.astype(F32)[:, None, :], axis=-1) * scale
@@ -96,13 +98,23 @@
     acc = jnp.einsum("ihp,ipd->ihd", probs.astype(BF16), kv[:, :, HEAD_DIM:], preferred_element_type=F32)
     own_r = lax.reduce_precision(own_prob, 8, 7)
     acc = acc + own_r[..., None] * new_v.astype(F32)[:, None, :]
-    attn = (acc / total[..., None]).astype(BF16).reshape(pair, group * HEAD_DIM)
-    part = jnp.dot(attn, head_w, preferred_element_type=F32).astype(BF16)
-    part = part.reshape(pair * width // 128, 128)
-    got = exchange(jnp.broadcast_to(part[None], (blocks,) + part.shape), BLK)
+    attn = (acc / total[..., None]).astype(BF16)
+    attn = jnp.concatenate([attn, sums[:, group:]], axis=1).reshape(n_l, 128)
+    got = exchange(to_all(attn, blocks), BLK)
 
-    got = jnp.sum(got.reshape(ny, nz, pair, width).astype(F32), axis=0)
-    mixed = x + got.transpose(1, 0, 2).reshape(count, width)
+    got = got[:, :n_l].reshape(ny, nz, pair, (group + 2), HEAD_DIM).transpose(2, 1, 0, 3, 4)
+    got = got.reshape(count, KV_HEADS, group + 2, HEAD_DIM)
+    attn = got[:, :, :group].reshape(count, width_q)
+    fresh_k = got[:, :, group].reshape(count, width_k)
+    fresh_v = got[:, :, group + 1].reshape(count, width_k)
+    part = jnp.dot(attn, w_cols, preferred_element_type=F32)
+    own_lines = count * cols // 128
+    high, low = halves(part.reshape(own_lines, 128))
+    got = exchange(to_all(jnp.concatenate([high, low], axis=0), blocks), BLK)
+    part = got[:, :own_lines].astype(F32) + got[:, own_lines : 2 * own_lines].astype(F32)
+    part = part.reshape(blocks, count, cols).transpose(1, 0, 2).reshape(count, width)
+
+    mixed = x + part
     expert_in = rms(mixed).astype(BF16)
     choice_logits = jnp.dot(expert_in, router, preferred_element_type=F32)
     picks = (routes[0][:, :, None] == jnp.arange(EXPERTS)[None, None, :]).astype(F32)
@@ -118,31 +130,23 @@
     upper = jnp.dot(expert_in, w_up, preferred_element_type=F32)
     act = (jax.nn.silu(gate) * upper * unit_weight).astype(BF16)
     expert_out = jnp.dot(act, w_down, preferred_element_type=F32)
-    own_lines = count * width // blocks // 128
     high, low = halves(expert_out.reshape(blocks, own_lines, 128))
-    fresh = jnp.concatenate([new_k, new_v], axis=1)
-    fresh = jnp.broadcast_to(fresh[None], (blocks,) + fresh.shape)
-    got = exchange(jnp.concatenate([high, low, fresh], axis=1), BLK)
+    got = exchange(jnp.concatenate([high, low], axis=1), BLK)
 
     piece = jnp.sum(got[:, :own_lines].astype(F32) + got[:, own_lines : 2 * own_lines].astype(F32), axis=0)
     mixed_piece = lax.dynamic_index_in_dim(mixed.reshape(blocks, own_lines, 128), block, 0, False)
     piece = (mixed_piece + piece).astype(BF16)
     piece = jnp.concatenate([piece, jnp.zeros((1, 128), BF16)], axis=0)
     everyone = blocks * lax.axis_size("batch")
-    fresh = got[:, 2 * own_lines :].reshape(ny, nz, pair, 2, HEAD_DIM).transpose(3, 2, 1, 0, 4)
-    fresh = fresh.reshape(2, count, width_k)
     got = exchange(jnp.broadcast_to(piece[None], (everyone,) + piece.shape), ("batch",) + BLK)
     outgoing = got[:, :own_lines].reshape(-1, width).astype(F32)
     final_in = rms(outgoing).astype(BF16)
     stream_logits = jnp.dot(final_in, w_vocab, preferred_element_type=F32).astype(BF16)
     stream = lax.axis_index("guide")
     half_rows = stream_logits.shape[0] // 2
-    kept = lax.dynamic_slice_in_dim(stream_logits, stream * half_rows, half_rows, 0)
-    sent = lax.dynamic_slice_in_dim(stream_logits, (1 - stream) * half_rows, half_rows, 0)
-    partner = lax.ppermute(sent, "guide", [(0, 1), (1, 0)])
-    is_first = stream == 0
-    cond = jnp.where(is_first, kept, partner).astype(F32)
-    uncond = jnp.where(is_first, partner, kept).astype(F32)
+    both = lax.all_gather(stream_logits, "guide", axis=0, tiled=False)
+    both = lax.dynamic_slice_in_dim(both, stream * half_rows, half_rows, 1).astype(F32)
+    cond, uncond = both[0], both[1]
     group_count = weight_index.shape[0]
     level_count = guidance_levels.shape[0]
     in_group = (group_ids[:, None] == jnp.arange(group_count)[None, :]).astype(F32)
@@ -151,11 +155,13 @@
     request_weight = jnp.sum(in_group * group_weight[None, :], axis=1)
     weight_rows = lax.dynamic_slice_in_dim(request_weight, stream * half_rows, half_rows, 0)
     logits = uncond + weight_rows[:, None] * (cond - uncond)
-    return (logits, fresh[0][None], fresh[1][None])
+    return (logits, fresh_k[None], fresh_v[None])
 
 
-def gathered_rows(w_out):
-    return lax.all_gather(w_out, "z", axis=0, tiled=True)
+def to_all(lines, number):
+    fill = -lines.shape[0] % 8
+    lines = jnp.concatenate([lines, jnp.zeros((fill, lines.shape[1]), lines.dtype)], axis=0)
+    return jnp.broadcast_to(lines[None], (number,) + lines.shape)
 
 
 def solution(mesh):

time: 145 us -> 141 us (0.972)
  waiting for transfers between devices: 36.6 us -> 63.7 us
  blocking collectives: 32.8 us -> 6.93 us
  starting transfers between devices: 53.8 us -> 45.1 us
  local copies, waits for them, and re-layouts: 7.66 us -> 11.6 us
    all_to_all x4 -> x5, waiting for transfers between devices: 36.6 us -> 63.7 us  [exchange(): return lax.all_to_all(value, axes, 0, 0, tiled=True)]
    all_gather x1, blocking collectives: 32.8 us -> 6.93 us  [local(): both = lax.all_gather(stream_logits, 'guide', axis=0, tiled=False)]
    ppermute x1 -> x0, starting transfers between devices: 10.7 us -> none  [local(): partner = lax.ppermute(sent, 'guide', [(0, 1), (1, 0)])]
    reshape x6 -> x16, local copies, waits for them, and re-layouts: 0.55 us -> 2.82 us  [the longest x1 0.61 us: local(): w_out.reshape(w_rows, blocks, cols).transpose(1, 0, 2)]
    all_to_all x4 -> x5, starting transfers between devices: 43.1 us -> 45.1 us  [exchange(): return lax.all_to_all(value, axes, 0, 0, tiled=True)]
    slice x9 -> x8, local copies, waits for them, and re-layouts: 1.68 us -> 0.18 us  [the longest x2 0.06 us: local(): attn = got[:, :, :group].reshape(count, width_q)]
  transfers between devices with their start and end apart: 5 -> 5, of which waited for: 3 -> 5; matrix products, arithmetic and copies ran while one was open for 3% -> 3% of each run, Pallas kernels for 0% -> 0%
where the time goes in v4:
time: 141 us; the launch traced here: 140 us
  waiting for transfers between devices  63.7 us (45%)
  starting transfers between devices  45.1 us (32%)
  local copies, waits for them, and re-layouts  11.6 us (8%)
  other arithmetic  8.38 us (6%)
  blocking collectives  6.93 us (5%)
  matrix products  3.16 us (2%)
    all_to_all x5, waiting for transfers between devices, exchange(): return lax.all_to_all(value, axes, 0, 0, tiled=True)  63.7 us
    all_to_all x5, starting transfers between devices, exchange(): return lax.all_to_all(value, axes, 0, 0, tiled=True)  45.1 us
    all_gather x1, blocking collectives, local(): both = lax.all_gather(stream_logits, 'guide', axis=0, tiled=False)  6.93 us
  transfers between devices with their start and end apart: 5, of which 5 were waited for; matrix products, arithmetic and copies ran while one was open for 3% of the time, Pallas kernels for 0%

profile of v4, /device:TPU:1, one launch (start us, length us, event | category | flops | bytes accessed | tf_op | source)
XLA Modules:
  0.0 140.1 jit_solution(14672887086610147021)
XLA Ops:
  0.6 0.9 convert_bitcast_fusion
  1.5 0.9 multiply_reduce_fusion.3
  2.5 1.1 fusion.27
  6.0 0.8 copy-done.7
  7.8 1.1 pad_maximum_fusion
  8.8 17.3 %all-to-all-start = ((bf16[64,47,128]{2,1,0:T(8,128)(2,1)}), bf16[64,47,128]{2,1,0:T(8,128)(2,1)S(1)}, u32[]{:S(2)}, u32[]{:S(2)}) async-start(bf16[64,47,128]{2,1,0:T(8,128)(2,1)} %pad_maximum_fusion), calls=%async_computation | async-start | bytes 1572864 | tf_op jit(solution)/shard_map/all_to_all | solution.py:22
  26.6 0.7 reduce.8
  27.6 19.6 %all-to-all-done = bf16[64,47,128]{2,1,0:T(8,128)(2,1)S(1)} async-done(((bf16[64,47,128]{2,1,0:T(8,128)(2,1)}), bf16[64,47,128]{2,1,0:T(8,128)(2,1)S(1)}, u32[]{:S(2)}, u32[]{:S(2)}) %all-to-all-start) | async-done | bytes 770080 | tf_op jit(solution)/shard_map/all_to_all | solution.py:22
  48.6 0.7 broadcast_in_dim.26
  49.3 9.0 %all-to-all-start.1 = ((bf16[64,8,128]{2,1,0:T(8,128)(2,1)}), bf16[64,8,128]{2,1,0:T(8,128)(2,1)S(1)}, u32[]{:S(2)}, u32[]{:S(2)}) async-start(bf16[64,8,128]{2,1,0:T(8,128)(2,1)} %broadcast_in_dim.26), calls=%async_computation.1 | async-start | bytes 262144 | tf_op jit(solution)/shard_map/all_to_all | solution.py:22
  58.8 11.0 %all-to-all-done.1 = bf16[64,8,128]{2,1,0:T(8,128)(2,1)S(1)} async-done(((bf16[64,8,128]{2,1,0:T(8,128)(2,1)}), bf16[64,8,128]{2,1,0:T(8,128)(2,1)S(1)}, u32[]{:S(2)}, u32[]{:S(2)}) %all-to-all-start.1) | async-done | bytes 131104 | tf_op jit(solution)/shard_map/all_to_all | solution.py:22
  71.4 4.6 %all-to-all-start.2 = ((bf16[64,8,128]{2,1,0:T(8,128)(2,1)}), bf16[64,8,128]{2,1,0:T(8,128)(2,1)S(1)}, u32[]{:S(2)}, u32[]{:S(2)}) async-start(bf16[64,8,128]{2,1,0:T(8,128)(2,1)} %broadcast_in_dim.28), calls=%async_computation.2 | async-start | bytes 262144 | tf_op jit(solution)/shard_map/all_to_all | solution.py:22
  76.7 11.1 %all-to-all-done.2 = bf16[64,8,128]{2,1,0:T(8,128)(2,1)S(1)} async-done(((bf16[64,8,128]{2,1,0:T(8,128)(2,1)}), bf16[64,8,128]{2,1,0:T(8,128)(2,1)S(1)}, u32[]{:S(2)}, u32[]{:S(2)}) %all-to-all-start.2) | async-done | bytes 131104 | tf_op jit(solution)/shard_map/all_to_all | solution.py:22
  90.7 0.7 pad_maximum_fusion.1
  91.4 4.6 %all-to-all-start.3 = ((bf16[64,6,128]{2,1,0:T(8,128)(2,1)}), bf16[64,6,128]{2,1,0:T(8,128)(2,1)S(1)}, u32[]{:S(2)}, u32[]{:S(2)}) async-start(bf16[64,6,128]{2,1,0:T(8,128)(2,1)} %pad_maximum_fusion.1), calls=%async_computation.3 | async-start | bytes 262144 | tf_op jit(solution)/shard_map/all_to_all | solution.py:22
  96.4 11.2 %all-to-all-done.3 = bf16[64,6,128]{2,1,0:T(8,128)(2,1)S(1)} async-done(((bf16[64,6,128]{2,1,0:T(8,128)(2,1)}), bf16[64,6,128]{2,1,0:T(8,128)(2,1)S(1)}, u32[]{:S(2)}, u32[]{:S(2)}) %all-to-all-start.3) | async-done | bytes 98336 | tf_op jit(solution)/shard_map/all_to_all | solution.py:22
  107.7 0.8 broadcast_in_dim.29
  108.5 9.6 %all-to-all-start.4 = ((bf16[256,4,128]{2,1,0:T(4,128)(2,1)}), bf16[256,4,128]{2,1,0:T(4,128)(2,1)S(1)}, u32[]{:S(2)}, u32[]{:S(2)}) async-start(bf16[256,4,128]{2,1,0:T(4,128)(2,1)} %broadcast_in_dim.29), calls=%async_computation.4 | async-start | bytes 524288 | tf_op jit(solution)/shard_map/all_to_all | solution.py:22
  118.5 0.7 broadcast_in_dim_reshape_squeeze.6
  119.2 0.7 broadcast_in_dim_reshape_squeeze.7
  119.9 10.8 %all-to-all-done.4 = bf16[256,4,128]{2,1,0:T(4,128)(2,1)S(1)} async-done(((bf16[256,4,128]{2,1,0:T(4,128)(2,1)}), bf16[256,4,128]{2,1,0:T(4,128)(2,1)S(1)}, u32[]{:S(2)}, u32[]{:S(2)}) %all-to-all-start.4) | async-done | bytes 262176 | tf_op jit(solution)/shard_map/all_to_all | solution.py:22
  130.9 1.0 multiply_reduce_fusion
  132.5 6.9 %all-gather = bf16[128,256]{1,0:T(8,128)(2,1)S(1)} all-gather(bf16[64,256]{1,0:T(8,128)(2,1)S(1)} %convolution_convert_fusion), channel_id=2, replica_groups=mesh['guide'=2,'y'=8,'z'=8,'batch'=4] {'guide'}, dimensions={0}, use_global_device_ids=true | all-gather | bytes 98304 | tf_op jit(solution)/shard_map/all_gather | solution.py:147
  139.4 0.7 fusion.12
  (120 shorter events, 12.4 us)
Async XLA Ops:
  0.6 89.3 %copy-start = (bf16[256,1536]{1,0:T(8,128)(2,1)S(1)}, bf16[256,1536]{1,0:T(8,128)(2,1)}, u32[]{:S(2)}) copy-start(bf16[256,1536]{1,0:T(8,128)(2,1)} %param.25) | copy-start | bytes 2359300
  4.0 1.0 copy-start.5
  4.3 1.0 copy-start.6
  5.9 0.9 copy-start.7
  8.8 17.8 %copy-start.10 = (s32[1,16]{1,0:T(1,128)S(1)}, s32[1,16]{1,0:T(1,128)}, u32[]{:S(2)}) copy-start(s32[1,16]{1,0:T(1,128)} %param.19) | copy-start | bytes 196
  8.8 38.5 %all-to-all-start = ((bf16[64,47,128]{2,1,0:T(8,128)(2,1)}), bf16[64,47,128]{2,1,0:T(8,128)(2,1)S(1)}, u32[]{:S(2)}, u32[]{:S(2)}) async-start(bf16[64,47,128]{2,1,0:T(8,128)(2,1)} %pad_maximum_fusion), calls=%async_computation | async-start | bytes 1572864 | tf_op jit(solution)/shard_map/all_to_all | solution.py:22
  49.3 20.6 %all-to-all-start.1 = ((bf16[64,8,128]{2,1,0:T(8,128)(2,1)}), bf16[64,8,128]{2,1,0:T(8,128)(2,1)S(1)}, u32[]{:S(2)}, u32[]{:S(2)}) async-start(bf16[64,8,128]{2,1,0:T(8,128)(2,1)} %broadcast_in_dim.26), calls=%async_computation.1 | async-start | bytes 262144 | tf_op jit(solution)/shard_map/all_to_all | solution.py:22
  70.2 5.9 %copy-start.1 = (bf16[1,16,1536]{2,1,0:T(8,128)(2,1)S(1)}, bf16[1,16,1536]{2,1,0:T(8,128)(2,1)}, u32[]{:S(2)}) copy-start(bf16[1,16,1536]{2,1,0:T(8,128)(2,1)} %param.15) | copy-start | bytes 147460
  71.4 16.3 %all-to-all-start.2 = ((bf16[64,8,128]{2,1,0:T(8,128)(2,1)}), bf16[64,8,128]{2,1,0:T(8,128)(2,1)S(1)}, u32[]{:S(2)}, u32[]{:S(2)}) async-start(bf16[64,8,128]{2,1,0:T(8,128)(2,1)} %broadcast_in_dim.28), calls=%async_computation.2 | async-start | bytes 262144 | tf_op jit(solution)/shard_map/all_to_all | solution.py:22
  88.3 0.8 copy-start.8
  88.3 0.9 copy-start.9
  88.4 1.2 copy-start.4
  88.6 1.3 copy-start.2
  91.4 16.2 %all-to-all-start.3 = ((bf16[64,6,128]{2,1,0:T(8,128)(2,1)}), bf16[64,6,128]{2,1,0:T(8,128)(2,1)S(1)}, u32[]{:S(2)}, u32[]{:S(2)}) async-start(bf16[64,6,128]{2,1,0:T(8,128)(2,1)} %pad_maximum_fusion.1), calls=%async_computation.3 | async-start | bytes 262144 | tf_op jit(solution)/shard_map/all_to_all | solution.py:22
  96.1 22.0 %copy-start.11 = (f32[8]{0:T(128)S(1)}, f32[8]{0:T(128)}, u32[]{:S(2)}) copy-start(f32[8]{0:T(128)} %param.29) | copy-start | bytes 100
  96.1 22.0 %copy-start.12 = (s32[8]{0:T(128)S(1)}, s32[8]{0:T(128)}, u32[]{:S(2)}) copy-start(s32[8]{0:T(128)} %param.28) | copy-start | bytes 100
  96.1 22.2 %copy-start.13 = (s32[64]{0:T(128)S(1)}, s32[64]{0:T(128)}, u32[]{:S(2)}) copy-start(s32[64]{0:T(128)} %param.27) | copy-start | bytes 772
  108.5 22.1 %all-to-all-start.4 = ((bf16[256,4,128]{2,1,0:T(4,128)(2,1)}), bf16[256,4,128]{2,1,0:T(4,128)(2,1)S(1)}, u32[]{:S(2)}, u32[]{:S(2)}) async-start(bf16[256,4,128]{2,1,0:T(4,128)(2,1)} %broadcast_in_dim.29), calls=%async_computation.4 | async-start | bytes 524288 | tf_op jit(solution)/shard_map/all_to_all | solution.py:22
  130.7 1.5 %copy-start.3 = (bf16[1536,256]{1,0:T(8,128)(2,1)S(1)}, bf16[1536,256]{1,0:T(8,128)(2,1)}, u32[]{:S(2)}) copy-start(bf16[1536,256]{1,0:T(8,128)(2,1)} %param.26) | copy-start | bytes 2359300

commit v5 on v4

--- a/solution.py
+++ b/solution.py
@@ -1,6 +1,8 @@
 import jax
 import jax.numpy as jnp
 from jax import lax
+from jax.experimental import pallas as pl
+from jax.experimental.pallas import tpu as pltpu
 from jax.sharding import Mesh, PartitionSpec as P
 
 HEADS = 24
@@ -55,37 +57,22 @@
     width_q = HEADS * HEAD_DIM
     width_k = KV_HEADS * HEAD_DIM
     x = hidden[0].astype(F32)
-    normed = rms(x).astype(BF16)
-    rows = w_qkv.shape[0]
-    part = lax.dynamic_slice_in_dim(normed, block * rows, rows, 1)
-    qkv = jnp.dot(part, w_qkv, preferred_element_type=F32)
-    q = qkv[:, :width_q].reshape(pair, nz, KV_HEADS, group * HEAD_DIM)
-    k = qkv[:, width_q : width_q + width_k].reshape(pair, nz, KV_HEADS, HEAD_DIM)
-    v = qkv[:, width_q + width_k :].reshape(pair, nz, KV_HEADS, HEAD_DIM)
-    lines = jnp.concatenate([q, k, v], axis=3).transpose(2, 1, 0, 3)
-    n_l = pair * (group + 2) * HEAD_DIM // 128
-    high, low = halves(lines.reshape(blocks, n_l, 128))
     span = key_cache.shape[2]
-    kc = key_cache[0].reshape(pair, nz, span, KV_HEADS, HEAD_DIM)
-    vc = value_cache[0].reshape(pair, nz, span, KV_HEADS, HEAD_DIM)
-    kv = jnp.concatenate([kc, vc], axis=4).transpose(3, 1, 0, 2, 4)
-    kv = kv.reshape(blocks, pair * span, 2 * HEAD_DIM)
+    sent = first_payload(block, hidden[0], w_qkv, key_cache[0], value_cache[0], blocks)
+    got = exchange(sent, BLK)
     cols = width // blocks
     w_rows = w_out.shape[0]
     n_w = -(-w_rows * cols // 128)
     w_blocks = w_out.reshape(w_rows, blocks, cols).transpose(1, 0, 2).reshape(blocks, w_rows * cols)
     w_blocks = jnp.pad(w_blocks, ((0, 0), (0, n_w * 128 - w_rows * cols))).reshape(blocks, n_w, 128)
-    got = exchange(jnp.concatenate([kv, high, low, w_blocks], axis=1), BLK)
 
     n_kv = pair * span
-    w_cols = got[:, n_kv + 2 * n_l :].reshape(blocks, n_w * 128)[:, : w_rows * cols].reshape(-1, cols)
     kv = got[:, :n_kv].reshape(blocks, pair, span, 2 * HEAD_DIM).transpose(1, 0, 2, 3)
     kv = kv.reshape(pair, blocks * span, 2 * HEAD_DIM)
-    sums = jnp.sum(
-        got[:, n_kv : n_kv + n_l].astype(F32) + got[:, n_kv + n_l : n_kv + 2 * n_l].astype(F32), axis=0
-    )
-    sums = sums.reshape(pair, group + 2, HEAD_DIM).astype(BF16)
-    query, new_k, new_v = sums[:, :group], sums[:, group], sums[:, group + 1]
+    sums = jnp.sum(got[:, n_kv:].astype(F32), axis=0)
+    query = (sums[:group] + sums[group + 2 :]).reshape(group, pair, HEAD_DIM).transpose(1, 0, 2).astype(BF16)
+    fresh = sums[group : group + 2].astype(BF16)
+    new_k, new_v = fresh[0].reshape(pair, HEAD_DIM), fresh[1].reshape(pair, HEAD_DIM)
     scale = HEAD_DIM ** (-0.5)
     scores = jnp.einsum("ihd,ipd->ihp", query, kv[:, :, :HEAD_DIM], preferred_element_type=F32) * scale
     own = jnp.sum(query.astype(F32) * new_k.astype(F32)[:, None, :], axis=-1) * scale
@@ -99,20 +86,21 @@
     own_r = lax.reduce_precision(own_prob, 8, 7)
     acc = acc + own_r[..., None] * new_v.astype(F32)[:, None, :]
     attn = (acc / total[..., None]).astype(BF16)
-    attn = jnp.concatenate([attn, sums[:, group:]], axis=1).reshape(n_l, 128)
-    got = exchange(to_all(attn, blocks), BLK)
-
-    got = got[:, :n_l].reshape(ny, nz, pair, (group + 2), HEAD_DIM).transpose(2, 1, 0, 3, 4)
-    got = got.reshape(count, KV_HEADS, group + 2, HEAD_DIM)
-    attn = got[:, :, :group].reshape(count, width_q)
-    fresh_k = got[:, :, group].reshape(count, width_k)
-    fresh_v = got[:, :, group + 1].reshape(count, width_k)
+    n_a = pair * group * HEAD_DIM // 128
+    attn = jnp.broadcast_to(attn.reshape(1, n_a, 128), (blocks, n_a, 128))
+    got = exchange(jnp.concatenate([attn, w_blocks], axis=1), BLK)
+
+    w_cols = got[:, n_a:].reshape(blocks, n_w * 128)[:, : w_rows * cols].reshape(-1, cols)
+    attn = got[:, :n_a].reshape(ny, nz, pair, group * HEAD_DIM).transpose(2, 1, 0, 3).reshape(count, width_q)
     part = jnp.dot(attn, w_cols, preferred_element_type=F32)
     own_lines = count * cols // 128
     high, low = halves(part.reshape(own_lines, 128))
-    got = exchange(to_all(jnp.concatenate([high, low], axis=0), blocks), BLK)
+    got = exchange(to_all(jnp.concatenate([high, low, fresh], axis=0), blocks), BLK)
     part = got[:, :own_lines].astype(F32) + got[:, own_lines : 2 * own_lines].astype(F32)
     part = part.reshape(blocks, count, cols).transpose(1, 0, 2).reshape(count, width)
+
+    fresh = got[:, 2 * own_lines :].reshape(ny, nz, 2, pair, HEAD_DIM).transpose(2, 3, 1, 0, 4)
+    fresh = fresh.reshape(2, 1, count, width_k)
 
     mixed = x + part
     expert_in = rms(mixed).astype(BF16)
@@ -155,13 +143,62 @@
     request_weight = jnp.sum(in_group * group_weight[None, :], axis=1)
     weight_rows = lax.dynamic_slice_in_dim(request_weight, stream * half_rows, half_rows, 0)
     logits = uncond + weight_rows[:, None] * (cond - uncond)
-    return (logits, fresh_k[None], fresh_v[None])
+    return (logits, fresh[0], fresh[1])
 
 
 def to_all(lines, number):
     fill = -lines.shape[0] % 8
     lines = jnp.concatenate([lines, jnp.zeros((fill, lines.shape[1]), lines.dtype)], axis=0)
     return jnp.broadcast_to(lines[None], (number,) + lines.shape)
+
+
+def first_payload_kernel(block_ref, hidden_ref, w_ref, key_ref, value_ref, out_ref, lines):
+    count, width = hidden_ref.shape
+    rows, total = w_ref.shape
+    span, width_k = key_ref.shape[1:]
+    nz = 8
+    normed = rms(hidden_ref[...].astype(F32)).astype(BF16)
+    at = lax.broadcasted_iota(jnp.int32, (width, 128), 0) - block_ref[0] * rows
+    pick = jnp.where(at == lax.broadcasted_iota(jnp.int32, (width, 128), 1), 1.0, 0.0)
+    part = jnp.dot(normed, pick.astype(BF16), preferred_element_type=F32)[:, :rows].astype(BF16)
+    qkv = jnp.dot(part, w_ref[...], preferred_element_type=F32)
+    low_lane = lax.broadcasted_iota(jnp.int32, (nz, 128), 1) < 64
+    heads = (total - 2 * width_k) // 64
+    for v in range(total // 128):
+        first, second = qkv[:nz, 128 * v : 128 * v + 128], qkv[nz:, 128 * v : 128 * v + 128]
+        even = jnp.where(low_lane, first, pltpu.roll(second, 64, 1))
+        odd = jnp.where(low_lane, pltpu.roll(first, 64, 1), second)
+        for chunk, line in ((2 * v, even), (2 * v + 1, odd)):
+            if chunk < heads:
+                y, row = chunk // 3, chunk % 3
+                high = line.astype(BF16).astype(F32)
+                lines[nz * y : nz * y + nz, 5 + row, :] = line - high
+            else:
+                y, row = (chunk - heads) % 8, 3 + (chunk - heads) // 8
+                high = line
+            lines[nz * y : nz * y + nz, row, :] = high
+    out_ref[:, 2 * span :, :] = lines[...].astype(BF16)
+    low_lane = lax.broadcasted_iota(jnp.int32, (count, span, 128), 2) < 64
+    for m in range(width_k // 128):
+        keys = key_ref[:, :, 128 * m : 128 * m + 128].astype(F32)
+        values = value_ref[:, :, 128 * m : 128 * m + 128].astype(F32)
+        even = jnp.where(low_lane, keys, pltpu.roll(values, 64, 2)).astype(BF16)
+        odd = jnp.where(low_lane, pltpu.roll(keys, 64, 2), values).astype(BF16)
+        for y, pair in ((2 * m, even), (2 * m + 1, odd)):
+            for i in range(count // nz):
+                out_ref[nz * y : nz * y + nz, span * i : span * i + span, :] = pair[nz * i : nz * i + nz]
+
+def first_payload(block, hidden, w_qkv, keys, values, blocks):
+    span = keys.shape[1]
+    vmem = pl.BlockSpec(memory_space=pltpu.VMEM)
+    return pl.pallas_call(
+        first_payload_kernel,
+        out_shape=jax.ShapeDtypeStruct((blocks, 2 * span + 8, 128), BF16),
+        in_specs=[pl.BlockSpec(memory_space=pltpu.SMEM)] + [vmem] * 4,
+        out_specs=vmem,
+        scratch_shapes=[pltpu.VMEM((blocks, 8, 128), F32)],
+        compiler_params=pltpu.CompilerParams(vmem_limit_bytes=32 << 20),
+    )(block.reshape(1), hidden, w_qkv, keys, values)
 
 
 def solution(mesh):

time: 141 us -> 135 us (0.957)
  waiting for transfers between devices: 63.7 us -> 59.1 us
  other arithmetic: 8.38 us -> 5.6 us
  local copies, waits for them, and re-layouts: 11.6 us -> 13.4 us
  Pallas kernels: 0 us -> 1.5 us
    all_to_all x5, waiting for transfers between devices: 63.7 us -> 59.1 us  [exchange(): return lax.all_to_all(value, axes, 0, 0, tiled=True)]
    unnamed x32 -> x36, local copies, waits for them, and re-layouts: 2.3 us -> 5.96 us
    another operation x4 -> x0, local copies, waits for them, and re-layouts: 1.94 us -> none  [the longest x2 1.4 us: local(): return (logits, fresh_k[None], fresh_v[None])]
    pallas_call x0 -> x1, Pallas kernels: none -> 1.5 us  [first_payload(): pl.pallas_call(first_payload_kernel, out_shape=jax.ShapeDtypeStruct((bloc...]
  transfers between devices with their start and end apart: 5 -> 5, of which waited for: 5 -> 5; matrix products, arithmetic and copies ran while one was open for 3% -> 4% of each run, Pallas kernels for 0% -> 0%
where the time goes in v5:
time: 135 us
  waiting for transfers between devices  59.1 us (44%)
  starting transfers between devices  44.8 us (33%)
  local copies, waits for them, and re-layouts  13.4 us (10%)
  blocking collectives  6.97 us (5%)
  other arithmetic  5.6 us (4%)
  matrix products  2.05 us (2%)
  Pallas kernels  1.5 us (1%)
    all_to_all x5, waiting for transfers between devices, exchange(): return lax.all_to_all(value, axes, 0, 0, tiled=True)  59.1 us
    all_to_all x5, starting transfers between devices, exchange(): return lax.all_to_all(value, axes, 0, 0, tiled=True)  44.8 us
    all_gather x1, blocking collectives, local(): both = lax.all_gather(stream_logits, 'guide', axis=0, tiled=False)  6.97 us
    unnamed x36, local copies, waits for them, and re-layouts  5.96 us
  transfers between devices with their start and end apart: 5, of which 5 were waited for; matrix products, arithmetic and copies ran while one was open for 4% of the time, Pallas kernels for 0%

profile of v5, /device:TPU:1, one launch (start us, length us, event | category | flops | bytes accessed | tf_op | source)
XLA Modules:
  0.0 134.5 jit_solution(5999723859825185839)
XLA Ops:
  0.7 0.9 copy-done.1
  1.5 0.9 copy-done.3
  2.5 0.9 copy-done.4
  3.4 0.9 copy-done.5
  4.3 1.5 %shard_map.166 = bf16[64,40,128]{2,1,0:T(8,128)(2,1)} custom-call(s32[1]{0:T(128)} %bitcast.block_ref, bf16[16,1536]{1,0:T(8,128)(2,1)S(1)} %bitcast.66, bf16[24,2560]{1,0:T(8,128)(2,1)S(1)} %copy-done.5, bf16[16,16,512]{2,1,0:T(8,128)(2,1)S(1)} %bitcast.67, bf16[16,16,512]{2,1,0:T(8,128)(2,1)S(1)} %bitcast.68), custom_call_target="tpu_custom_call" | custom-call | tf_op jit(solution)/shard_map/pallas_call | solution.py:194
  5.8 17.3 %all-to-all-start = ((bf16[64,40,128]{2,1,0:T(8,128)(2,1)}), bf16[64,40,128]{2,1,0:T(8,128)(2,1)S(1)}, u32[]{:S(2)}, u32[]{:S(2)}) async-start(bf16[64,40,128]{2,1,0:T(8,128)(2,1)} %shard_map.166), calls=%async_computation | async-start | bytes 1310720 | tf_op jit(solution)/shard_map/all_to_all | solution.py:24
  23.8 0.7 reduce.16
  25.8 15.8 %all-to-all-done = bf16[64,40,128]{2,1,0:T(8,128)(2,1)S(1)} async-done(((bf16[64,40,128]{2,1,0:T(8,128)(2,1)}), bf16[64,40,128]{2,1,0:T(8,128)(2,1)S(1)}, u32[]{:S(2)}, u32[]{:S(2)}) %all-to-all-start) | async-done | bytes 655392 | tf_op jit(solution)/shard_map/all_to_all | solution.py:24
  43.2 0.7 pad_maximum_fusion
  43.9 8.8 %all-to-all-start.1 = ((bf16[64,8,128]{2,1,0:T(8,128)(2,1)}), bf16[64,8,128]{2,1,0:T(8,128)(2,1)S(1)}, u32[]{:S(2)}, u32[]{:S(2)}) async-start(bf16[64,8,128]{2,1,0:T(8,128)(2,1)} %pad_maximum_fusion), calls=%async_computation.1 | async-start | bytes 262144 | tf_op jit(solution)/shard_map/all_to_all | solution.py:24
  52.7 11.5 %all-to-all-done.1 = bf16[64,8,128]{2,1,0:T(8,128)(2,1)S(1)} async-done(((bf16[64,8,128]{2,1,0:T(8,128)(2,1)}), bf16[64,8,128]{2,1,0:T(8,128)(2,1)S(1)}, u32[]{:S(2)}, u32[]{:S(2)}) %all-to-all-start.1) | async-done | bytes 131104 | tf_op jit(solution)/shard_map/all_to_all | solution.py:24
  65.9 4.7 %all-to-all-start.2 = ((bf16[64,8,128]{2,1,0:T(8,128)(2,1)}), bf16[64,8,128]{2,1,0:T(8,128)(2,1)S(1)}, u32[]{:S(2)}, u32[]{:S(2)}) async-start(bf16[64,8,128]{2,1,0:T(8,128)(2,1)} %broadcast_in_dim.28), calls=%async_computation.2 | async-start | bytes 262144 | tf_op jit(solution)/shard_map/all_to_all | solution.py:24
  71.2 11.1 %all-to-all-done.2 = bf16[64,8,128]{2,1,0:T(8,128)(2,1)S(1)} async-done(((bf16[64,8,128]{2,1,0:T(8,128)(2,1)}), bf16[64,8,128]{2,1,0:T(8,128)(2,1)S(1)}, u32[]{:S(2)}, u32[]{:S(2)}) %all-to-all-start.2) | async-done | bytes 131104 | tf_op jit(solution)/shard_map/all_to_all | solution.py:24
  85.2 0.7 pad_maximum_fusion.1
  85.9 4.6 %all-to-all-start.3 = ((bf16[64,6,128]{2,1,0:T(8,128)(2,1)}), bf16[64,6,128]{2,1,0:T(8,128)(2,1)S(1)}, u32[]{:S(2)}, u32[]{:S(2)}) async-start(bf16[64,6,128]{2,1,0:T(8,128)(2,1)} %pad_maximum_fusion.1), calls=%async_computation.3 | async-start | bytes 262144 | tf_op jit(solution)/shard_map/all_to_all | solution.py:24
  91.0 11.2 %all-to-all-done.3 = bf16[64,6,128]{2,1,0:T(8,128)(2,1)S(1)} async-done(((bf16[64,6,128]{2,1,0:T(8,128)(2,1)}), bf16[64,6,128]{2,1,0:T(8,128)(2,1)S(1)}, u32[]{:S(2)}, u32[]{:S(2)}) %all-to-all-start.3) | async-done | bytes 98336 | tf_op jit(solution)/shard_map/all_to_all | solution.py:24
  102.3 0.8 broadcast_in_dim.29
  103.0 9.4 %all-to-all-start.4 = ((bf16[256,4,128]{2,1,0:T(4,128)(2,1)}), bf16[256,4,128]{2,1,0:T(4,128)(2,1)S(1)}, u32[]{:S(2)}, u32[]{:S(2)}) async-start(bf16[256,4,128]{2,1,0:T(4,128)(2,1)} %broadcast_in_dim.29), calls=%async_computation.4 | async-start | bytes 524288 | tf_op jit(solution)/shard_map/all_to_all | solution.py:24
  114.2 0.7 squeeze.36
  114.9 0.7 squeeze.37
  115.6 9.4 %all-to-all-done.4 = bf16[256,4,128]{2,1,0:T(4,128)(2,1)S(1)} async-done(((bf16[256,4,128]{2,1,0:T(4,128)(2,1)}), bf16[256,4,128]{2,1,0:T(4,128)(2,1)S(1)}, u32[]{:S(2)}, u32[]{:S(2)}) %all-to-all-start.4) | async-done | bytes 262176 | tf_op jit(solution)/shard_map/all_to_all | solution.py:24
  125.3 1.0 multiply_reduce_fusion
  126.9 7.0 %all-gather = bf16[128,256]{1,0:T(8,128)(2,1)S(1)} all-gather(bf16[64,256]{1,0:T(8,128)(2,1)S(1)} %convolution_convert_fusion), channel_id=2, replica_groups=mesh['guide'=2,'y'=8,'z'=8,'batch'=4] {'guide'}, dimensions={0}, use_global_device_ids=true | all-gather | bytes 98304 | tf_op jit(solution)/shard_map/all_gather | solution.py:135
  133.8 0.7 fusion.11
  (110 shorter events, 11.4 us)
Async XLA Ops:
  0.6 83.8 %copy-start = (bf16[256,1536]{1,0:T(8,128)(2,1)S(1)}, bf16[256,1536]{1,0:T(8,128)(2,1)}, u32[]{:S(2)}) copy-start(bf16[256,1536]{1,0:T(8,128)(2,1)} %param.25) | copy-start | bytes 2359300
  0.7 0.9 copy-start.1
  1.5 0.9 copy-start.3
  2.5 0.9 copy-start.4
  3.4 0.9 copy-start.5
  5.8 18.7 %copy-start.9 = (bf16[24,1536]{1,0:T(8,128)(2,1)S(1)}, bf16[24,1536]{1,0:T(8,128)(2,1)}, u32[]{:S(2)}) copy-start(bf16[24,1536]{1,0:T(8,128)(2,1)} %param.20) | copy-start | bytes 221188
  5.8 35.8 %all-to-all-start = ((bf16[64,40,128]{2,1,0:T(8,128)(2,1)}), bf16[64,40,128]{2,1,0:T(8,128)(2,1)S(1)}, u32[]{:S(2)}, u32[]{:S(2)}) async-start(bf16[64,40,128]{2,1,0:T(8,128)(2,1)} %shard_map.166), calls=%async_computation | async-start | bytes 1310720 | tf_op jit(solution)/shard_map/all_to_all | solution.py:24
  23.1 0.7 copy-start.12
  43.9 20.3 %all-to-all-start.1 = ((bf16[64,8,128]{2,1,0:T(8,128)(2,1)}), bf16[64,8,128]{2,1,0:T(8,128)(2,1)S(1)}, u32[]{:S(2)}, u32[]{:S(2)}) async-start(bf16[64,8,128]{2,1,0:T(8,128)(2,1)} %pad_maximum_fusion), calls=%async_computation.1 | async-start | bytes 262144 | tf_op jit(solution)/shard_map/all_to_all | solution.py:24
  65.9 4.8 %copy-start.2 = (bf16[1,16,1536]{2,1,0:T(8,128)(2,1)S(1)}, bf16[1,16,1536]{2,1,0:T(8,128)(2,1)}, u32[]{:S(2)}) copy-start(bf16[1,16,1536]{2,1,0:T(8,128)(2,1)} %param.15) | copy-start | bytes 147460
  65.9 16.5 %all-to-all-start.2 = ((bf16[64,8,128]{2,1,0:T(8,128)(2,1)}), bf16[64,8,128]{2,1,0:T(8,128)(2,1)S(1)}, u32[]{:S(2)}, u32[]{:S(2)}) async-start(bf16[64,8,128]{2,1,0:T(8,128)(2,1)} %broadcast_in_dim.28), calls=%async_computation.2 | async-start | bytes 262144 | tf_op jit(solution)/shard_map/all_to_all | solution.py:24
  82.9 0.8 copy-start.10
  82.9 0.9 copy-start.11
  82.9 1.2 copy-start.8
  83.1 1.3 copy-start.6
  85.9 16.2 %all-to-all-start.3 = ((bf16[64,6,128]{2,1,0:T(8,128)(2,1)}), bf16[64,6,128]{2,1,0:T(8,128)(2,1)S(1)}, u32[]{:S(2)}, u32[]{:S(2)}) async-start(bf16[64,6,128]{2,1,0:T(8,128)(2,1)} %pad_maximum_fusion.1), calls=%async_computation.3 | async-start | bytes 262144 | tf_op jit(solution)/shard_map/all_to_all | solution.py:24
  103.0 21.9 %all-to-all-start.4 = ((bf16[256,4,128]{2,1,0:T(4,128)(2,1)}), bf16[256,4,128]{2,1,0:T(4,128)(2,1)S(1)}, u32[]{:S(2)}, u32[]{:S(2)}) async-start(bf16[256,4,128]{2,1,0:T(4,128)(2,1)} %broadcast_in_dim.29), calls=%async_computation.4 | async-start | bytes 524288 | tf_op jit(solution)/shard_map/all_to_all | solution.py:24
  112.5 0.7 copy-start.13
  112.5 0.7 copy-start.14
  113.1 0.7 copy-start.15
  125.1 1.5 %copy-start.7 = (bf16[1536,256]{1,0:T(8,128)(2,1)S(1)}, bf16[1536,256]{1,0:T(8,128)(2,1)}, u32[]{:S(2)}) copy-start(bf16[1536,256]{1,0:T(8,128)(2,1)} %param.26) | copy-start | bytes 2359300

commit v6 on v5

--- a/solution.py
+++ b/solution.py
@@ -14,6 +14,9 @@
 F32 = jnp.float32
 BF16 = jnp.bfloat16
 BLK = ("y", "z")
+HBM = pl.BlockSpec(memory_space=pltpu.HBM)
+VMEM = pl.BlockSpec(memory_space=pltpu.VMEM)
+SMEM = pl.BlockSpec(memory_space=pltpu.SMEM)
 
 
 def rms(values):
@@ -56,7 +59,6 @@
     width = hidden.shape[2]
     width_q = HEADS * HEAD_DIM
     width_k = KV_HEADS * HEAD_DIM
-    x = hidden[0].astype(F32)
     span = key_cache.shape[2]
     sent = first_payload(block, hidden[0], w_qkv, key_cache[0], value_cache[0], blocks)
     got = exchange(sent, BLK)
@@ -102,24 +104,8 @@
     fresh = got[:, 2 * own_lines :].reshape(ny, nz, 2, pair, HEAD_DIM).transpose(2, 3, 1, 0, 4)
     fresh = fresh.reshape(2, 1, count, width_k)
 
-    mixed = x + part
-    expert_in = rms(mixed).astype(BF16)
-    choice_logits = jnp.dot(expert_in, router, preferred_element_type=F32)
-    picks = (routes[0][:, :, None] == jnp.arange(EXPERTS)[None, None, :]).astype(F32)
-    chosen = jnp.sum(picks * choice_logits[:, None, :], axis=-1)
-    first = jax.nn.sigmoid(chosen[:, 0] - chosen[:, 1])
-    shares = jnp.stack([first, 1.0 - first], axis=1)
-    per_expert = jnp.sum(picks * shares[:, :, None], axis=1)
-    units = w_gate.shape[1]
-    owner = (block * units + jnp.arange(units)) // EXPERT_UNITS
-    member = (owner[None, :] == jnp.arange(EXPERTS)[:, None]).astype(F32)
-    unit_weight = jnp.sum(per_expert[:, :, None] * member[None, :, :], axis=1)
-    gate = jnp.dot(expert_in, w_gate, preferred_element_type=F32)
-    upper = jnp.dot(expert_in, w_up, preferred_element_type=F32)
-    act = (jax.nn.silu(gate) * upper * unit_weight).astype(BF16)
-    expert_out = jnp.dot(act, w_down, preferred_element_type=F32)
-    high, low = halves(expert_out.reshape(blocks, own_lines, 128))
-    got = exchange(jnp.concatenate([high, low], axis=1), BLK)
+    sent, mixed = expert_payload(block, hidden[0], part, router, routes[0], w_gate, w_up, w_down)
+    got = exchange(sent.reshape(blocks, 2 * own_lines, 128), BLK)
 
     piece = jnp.sum(got[:, :own_lines].astype(F32) + got[:, own_lines : 2 * own_lines].astype(F32), axis=0)
     mixed_piece = lax.dynamic_index_in_dim(mixed.reshape(blocks, own_lines, 128), block, 0, False)
@@ -127,7 +113,7 @@
     piece = jnp.concatenate([piece, jnp.zeros((1, 128), BF16)], axis=0)
     everyone = blocks * lax.axis_size("batch")
     got = exchange(jnp.broadcast_to(piece[None], (everyone,) + piece.shape), ("batch",) + BLK)
-    outgoing = got[:, :own_lines].reshape(-1, width).astype(F32)
+    outgoing = lax.optimization_barrier(got[:, :own_lines].astype(F32).reshape(-1, width))
     final_in = rms(outgoing).astype(BF16)
     stream_logits = jnp.dot(final_in, w_vocab, preferred_element_type=F32).astype(BF16)
     stream = lax.axis_index("guide")
@@ -152,15 +138,27 @@
     return jnp.broadcast_to(lines[None], (number,) + lines.shape)
 
 
-def first_payload_kernel(block_ref, hidden_ref, w_ref, key_ref, value_ref, out_ref, lines):
+def first_payload_kernel(
+    block_ref, hidden_hbm, w_hbm, key_hbm, value_hbm, out_ref, hidden_ref, w_ref, key_ref, value_ref, lines, sems
+):
+    copies = [
+        pltpu.make_async_copy(source, target, sems.at[n])
+        for n, (source, target) in enumerate(
+            ((hidden_hbm, hidden_ref), (w_hbm, w_ref), (key_hbm, key_ref), (value_hbm, value_ref))
+        )
+    ]
+    for copy in copies:
+        copy.start()
     count, width = hidden_ref.shape
     rows, total = w_ref.shape
     span, width_k = key_ref.shape[1:]
-    nz = 8
+    nz = count // 2
+    at = lax.broadcasted_iota(jnp.int32, (width, 128), 0) - block_ref[0] * rows
+    pick = jnp.where(at == lax.broadcasted_iota(jnp.int32, (width, 128), 1), 1.0, 0.0).astype(BF16)
+    copies[0].wait()
     normed = rms(hidden_ref[...].astype(F32)).astype(BF16)
-    at = lax.broadcasted_iota(jnp.int32, (width, 128), 0) - block_ref[0] * rows
-    pick = jnp.where(at == lax.broadcasted_iota(jnp.int32, (width, 128), 1), 1.0, 0.0)
-    part = jnp.dot(normed, pick.astype(BF16), preferred_element_type=F32)[:, :rows].astype(BF16)
+    part = jnp.dot(normed, pick, preferred_element_type=F32)[:, :rows].astype(BF16)
+    copies[1].wait()
     qkv = jnp.dot(part, w_ref[...], preferred_element_type=F32)
     low_lane = lax.broadcasted_iota(jnp.int32, (nz, 128), 1) < 64
     heads = (total - 2 * width_k) // 64
@@ -178,6 +176,8 @@
                 high = line
             lines[nz * y : nz * y + nz, row, :] = high
     out_ref[:, 2 * span :, :] = lines[...].astype(BF16)
+    copies[2].wait()
+    copies[3].wait()
     low_lane = lax.broadcasted_iota(jnp.int32, (count, span, 128), 2) < 64
     for m in range(width_k // 128):
         keys = key_ref[:, :, 128 * m : 128 * m + 128].astype(F32)
@@ -188,17 +188,95 @@
             for i in range(count // nz):
                 out_ref[nz * y : nz * y + nz, span * i : span * i + span, :] = pair[nz * i : nz * i + nz]
 
+
 def first_payload(block, hidden, w_qkv, keys, values, blocks):
     span = keys.shape[1]
-    vmem = pl.BlockSpec(memory_space=pltpu.VMEM)
     return pl.pallas_call(
         first_payload_kernel,
         out_shape=jax.ShapeDtypeStruct((blocks, 2 * span + 8, 128), BF16),
-        in_specs=[pl.BlockSpec(memory_space=pltpu.SMEM)] + [vmem] * 4,
-        out_specs=vmem,
-        scratch_shapes=[pltpu.VMEM((blocks, 8, 128), F32)],
-        compiler_params=pltpu.CompilerParams(vmem_limit_bytes=32 << 20),
+        in_specs=[SMEM] + [HBM] * 4,
+        out_specs=VMEM,
+        scratch_shapes=[pltpu.VMEM(a.shape, a.dtype) for a in (hidden, w_qkv, keys, values)]
+        + [pltpu.VMEM((blocks, 8, 128), F32), pltpu.SemaphoreType.DMA((4,))],
+        compiler_params=pltpu.CompilerParams(vmem_limit_bytes=60 << 20),
     )(block.reshape(1), hidden, w_qkv, keys, values)
+
+
+def expert_kernel(
+    block_ref,
+    hidden_ref,
+    part_ref,
+    router_ref,
+    routes_ref,
+    gate_hbm,
+    up_hbm,
+    down_hbm,
+    out_ref,
+    mixed_ref,
+    gate_ref,
+    up_ref,
+    down_ref,
+    lines,
+    sems,
+):
+    copies = [
+        pltpu.make_async_copy(source, target, sems.at[n])
+        for n, (source, target) in enumerate(((gate_hbm, gate_ref), (up_hbm, up_ref), (down_hbm, down_ref)))
+    ]
+    for copy in copies:
+        copy.start()
+    count, width = hidden_ref.shape
+    mixed = hidden_ref[...].astype(F32) + part_ref[...]
+    expert_in = rms(mixed).astype(BF16)
+    choice = lax.dot_general(
+        router_ref[...], expert_in, (((1,), (1,)), ((), ())), preferred_element_type=F32
+    )
+    experts = lax.broadcasted_iota(jnp.int32, choice.shape, 0)
+    routes = routes_ref[...]
+    e1, e2 = routes[0:1], routes[1:2]
+    zero = jnp.zeros_like(choice)
+    c1 = jnp.sum(jnp.where(experts == e1, choice, zero), axis=0, keepdims=True)
+    c2 = jnp.sum(jnp.where(experts == e2, choice, zero), axis=0, keepdims=True)
+    first = 1.0 / (1.0 + jnp.exp(c2 - c1))
+    mine = block_ref[0] * gate_ref.shape[1] // EXPERT_UNITS
+    share = jnp.where(e1 == mine, first, jnp.where(e2 == mine, 1.0 - first, 0.0))
+    row = lax.broadcasted_iota(jnp.int32, (count, count), 0)
+    column = lax.broadcasted_iota(jnp.int32, (count, count), 1)
+    share = jnp.sum(jnp.where(row == column, share, 0.0), axis=1, keepdims=True)
+    copies[0].wait()
+    gate = jnp.dot(expert_in, gate_ref[...], preferred_element_type=F32)
+    copies[1].wait()
+    upper = jnp.dot(expert_in, up_ref[...], preferred_element_type=F32)
+    act = (gate / (1.0 + jnp.exp(-gate)) * upper * share).astype(BF16)
+    copies[2].wait()
+    out = jnp.dot(act, down_ref[...], preferred_element_type=F32)
+    parts = width // 384
+    for j in range(parts):
+        for i in range(3):
+            lanes = slice(128 * (3 * j + i), 128 * (3 * j + i) + 128)
+            line = out[:, lanes]
+            high = line.astype(BF16).astype(F32)
+            lines[:, j, i, :] = high
+            lines[:, j, 3 + i, :] = line - high
+            mixed_ref[:, j, i, :] = mixed[:, lanes]
+    out_ref[...] = lines[...].astype(BF16)
+
+
+def expert_payload(block, hidden, part, router, routes, w_gate, w_up, w_down):
+    count, width = hidden.shape
+    parts = width // 384
+    return pl.pallas_call(
+        expert_kernel,
+        out_shape=(
+            jax.ShapeDtypeStruct((count, parts, 6, 128), BF16),
+            jax.ShapeDtypeStruct((count, parts, 3, 128), F32),
+        ),
+        in_specs=[SMEM] + [VMEM] * 4 + [HBM] * 3,
+        out_specs=(VMEM, VMEM),
+        scratch_shapes=[pltpu.VMEM(a.shape, a.dtype) for a in (w_gate, w_up, w_down)]
+        + [pltpu.VMEM((count, parts, 6, 128), F32), pltpu.SemaphoreType.DMA((3,))],
+        compiler_params=pltpu.CompilerParams(vmem_limit_bytes=60 << 20),
+    )(block.reshape(1), hidden, part, router.T, routes.T, w_gate, w_up, w_down)
 
 
 def solution(mesh):

time: 135 us -> 132 us (0.978)
  blocking collectives: 6.97 us -> 22.5 us
  waiting for transfers between devices: 59.1 us -> 48.4 us
  local copies, waits for them, and re-layouts: 13.4 us -> 8.36 us
  Pallas kernels: 1.5 us -> 6.31 us
  starting transfers between devices: 44.8 us -> 40.1 us
  other arithmetic: 5.6 us -> 3.8 us
    all_to_all x0 -> x1, blocking collectives: none -> 15.5 us  [exchange(): return lax.all_to_all(value, axes, 0, 0, tiled=True)]
    all_to_all x5 -> x4, waiting for transfers between devices: 59.1 us -> 48.4 us  [exchange(): return lax.all_to_all(value, axes, 0, 0, tiled=True)]
    all_to_all x5 -> x4, starting transfers between devices: 44.8 us -> 40.1 us  [exchange(): return lax.all_to_all(value, axes, 0, 0, tiled=True)]
    unnamed x36 -> x16, local copies, waits for them, and re-layouts: 5.96 us -> 2.08 us
    pallas_call x0 -> x1, Pallas kernels: none -> 3.73 us  [expert_payload(): pl.pallas_call(expert_kernel, out_shape=(jax.ShapeDtypeStruct((count, par...]
  transfers between devices with their start and end apart: 5 -> 4, of which waited for: 5 -> 4; matrix products, arithmetic and copies ran while one was open for 4% -> 3% of each run, Pallas kernels for 0% -> 0%
where the time goes in v6:
time: 132 us
  waiting for transfers between devices  48.4 us (37%)
  starting transfers between devices  40.1 us (30%)
  blocking collectives  22.5 us (17%)
  local copies, waits for them, and re-layouts  8.36 us (6%)
  Pallas kernels  6.31 us (5%)
  other arithmetic  3.8 us (3%)
    all_to_all x4, waiting for transfers between devices, exchange(): return lax.all_to_all(value, axes, 0, 0, tiled=True)  48.4 us
    all_to_all x4, starting transfers between devices, exchange(): return lax.all_to_all(value, axes, 0, 0, tiled=True)  40.1 us
    all_to_all x1, blocking collectives, exchange(): return lax.all_to_all(value, axes, 0, 0, tiled=True)  15.5 us
    all_gather x1, blocking collectives, local(): both = lax.all_gather(stream_logits, 'guide', axis=0, tiled=False)  6.99 us
    pallas_call x1, Pallas kernels, expert_payload(): pl.pallas_call(expert_kernel, out_shape=(jax.ShapeDtypeStruct((count, par...  3.73 us
  transfers between devices with their start and end apart: 4, of which 4 were waited for; matrix products, arithmetic and copies ran while one was open for 3% of the time, Pallas kernels for 0%

profile of v6, /device:TPU:1, one launch (start us, length us, event | category | flops | bytes accessed | tf_op | source)
XLA Modules:
  0.0 131.5 jit_solution(9324086752608900523)
XLA Ops:
  0.7 2.6 %shard_map.166 = bf16[64,40,128]{2,1,0:T(8,128)(2,1)} custom-call(s32[1]{0:T(128)} %bitcast.block_ref, bf16[16,1536]{1,0:T(8,128)(2,1)} %bitcast.74, bf16[24,2560]{1,0:T(8,128)(2,1)} %w_hbm.1, bf16[16,16,512]{2,1,0:T(8,128)(2,1)} %bitcast.70, bf16[16,16,512]{2,1,0:T(8,128)(2,1)} %bitcast.71), custom_call_target="tpu_custom_call" | custom-call | tf_op jit(solution)/shard_map/pallas_call | solution.py:194
  3.3 17.3 %all-to-all-start = ((bf16[64,40,128]{2,1,0:T(8,128)(2,1)}), bf16[64,40,128]{2,1,0:T(8,128)(2,1)S(1)}, u32[]{:S(2)}, u32[]{:S(2)}) async-start(bf16[64,40,128]{2,1,0:T(8,128)(2,1)} %shard_map.166), calls=%async_computation | async-start | bytes 1310720 | tf_op jit(solution)/shard_map/all_to_all | solution.py:27
  20.6 0.6 reshape.140
  21.6 0.5 broadcast.75
  22.2 0.7 reduce.13
  23.2 15.8 %all-to-all-done = bf16[64,40,128]{2,1,0:T(8,128)(2,1)S(1)} async-done(((bf16[64,40,128]{2,1,0:T(8,128)(2,1)}), bf16[64,40,128]{2,1,0:T(8,128)(2,1)S(1)}, u32[]{:S(2)}, u32[]{:S(2)}) %all-to-all-start) | async-done | bytes 655392 | tf_op jit(solution)/shard_map/all_to_all | solution.py:27
  40.6 0.7 pad_maximum_fusion
  41.3 8.8 %all-to-all-start.1 = ((bf16[64,8,128]{2,1,0:T(8,128)(2,1)}), bf16[64,8,128]{2,1,0:T(8,128)(2,1)S(1)}, u32[]{:S(2)}, u32[]{:S(2)}) async-start(bf16[64,8,128]{2,1,0:T(8,128)(2,1)} %pad_maximum_fusion), calls=%async_computation.1 | async-start | bytes 262144 | tf_op jit(solution)/shard_map/all_to_all | solution.py:27
  50.1 11.5 %all-to-all-done.1 = bf16[64,8,128]{2,1,0:T(8,128)(2,1)S(1)} async-done(((bf16[64,8,128]{2,1,0:T(8,128)(2,1)}), bf16[64,8,128]{2,1,0:T(8,128)(2,1)S(1)}, u32[]{:S(2)}, u32[]{:S(2)}) %all-to-all-start.1) | async-done | bytes 131104 | tf_op jit(solution)/shard_map/all_to_all | solution.py:27
  62.7 15.5 %all_to_all.25 = bf16[64,8,128]{2,1,0:T(8,128)(2,1)S(1)} all-to-all(bf16[64,8,128]{2,1,0:T(8,128)(2,1)S(1)} %broadcast_in_dim.28), channel_id=1, replica_groups=mesh['guide'=2,'y'=8,'z'=8,'batch'=4] {'y','z'}, dimensions={0} | all-to-all | bytes 262144 | tf_op jit(solution)/shard_map/all_to_all | solution.py:27
  78.7 0.9 reshape.149.part_ref
  79.7 3.7 %shard_map.167 = (bf16[16,4,6,128]{3,2,1,0:T(8,128)(2,1)}, f32[16,4,3,128]{3,2,1,0:T(4,128)}) custom-call(s32[1]{0:T(128)} %bitcast.block_ref, bf16[16,1536]{1,0:T(8,128)(2,1)} %bitcast.75, f32[16,1536]{1,0:T(8,128)} %reshape.149.part_ref, bf16[16,1536]{1,0:T(8,128)(2,1)} %bitcast.78, s32[2,16]{1,0:T(2,128)} %bitcast.79, bf16[1536,256]{1,0:T(8,128)(2,1)} %gate_hbm.1, ...), custom_call_target="tpu_custom_call" | custom-call | tf_op jit(solution)/shard_map/pallas_call | solution.py:268
  83.4 4.6 %all-to-all-start.3 = ((bf16[64,6,128]{2,1,0:T(8,128)(2,1)}), bf16[64,6,128]{2,1,0:T(8,128)(2,1)S(1)}, u32[]{:S(2)}, u32[]{:S(2)}) async-start(bf16[64,6,128]{2,1,0:T(8,128)(2,1)} %bitcast.77), calls=%async_computation.3 | async-start | bytes 262144 | tf_op jit(solution)/shard_map/all_to_all | solution.py:27
  88.0 11.6 %all-to-all-done.3 = bf16[64,6,128]{2,1,0:T(8,128)(2,1)S(1)} async-done(((bf16[64,6,128]{2,1,0:T(8,128)(2,1)}), bf16[64,6,128]{2,1,0:T(8,128)(2,1)S(1)}, u32[]{:S(2)}, u32[]{:S(2)}) %all-to-all-start.3) | async-done | bytes 98336 | tf_op jit(solution)/shard_map/all_to_all | solution.py:27
  99.7 0.7 fusion.15
  100.4 0.8 broadcast_in_dim.29
  101.2 9.4 %all-to-all-start.4 = ((bf16[256,4,128]{2,1,0:T(4,128)(2,1)}), bf16[256,4,128]{2,1,0:T(4,128)(2,1)S(1)}, u32[]{:S(2)}, u32[]{:S(2)}) async-start(bf16[256,4,128]{2,1,0:T(4,128)(2,1)} %broadcast_in_dim.29), calls=%async_computation.4 | async-start | bytes 524288 | tf_op jit(solution)/shard_map/all_to_all | solution.py:27
  110.6 0.6 copy-done.3
  111.5 0.5 copy-done.5
  112.3 0.7 squeeze.38
  113.0 0.7 squeeze.39
  113.7 9.4 %all-to-all-done.4 = bf16[256,4,128]{2,1,0:T(4,128)(2,1)S(1)} async-done(((bf16[256,4,128]{2,1,0:T(4,128)(2,1)}), bf16[256,4,128]{2,1,0:T(4,128)(2,1)S(1)}, u32[]{:S(2)}, u32[]{:S(2)}) %all-to-all-start.4) | async-done | bytes 262176 | tf_op jit(solution)/shard_map/all_to_all | solution.py:27
  123.8 7.0 %all-gather = bf16[128,256]{1,0:T(8,128)(2,1)S(1)} all-gather(bf16[64,256]{1,0:T(8,128)(2,1)S(1)} %convolution_convert_fusion), channel_id=2, replica_groups=mesh['guide'=2,'y'=8,'z'=8,'batch'=4] {'guide'}, dimensions={0}, use_global_device_ids=true | all-gather | bytes 98304 | tf_op jit(solution)/shard_map/all_gather | solution.py:121
  130.8 0.7 fusion.7
  (68 shorter events, 5.2 us)
Async XLA Ops:
  0.6 122.9 %copy-start = (bf16[1536,256]{1,0:T(8,128)(2,1)S(1)}, bf16[1536,256]{1,0:T(8,128)(2,1)}, u32[]{:S(2)}) copy-start(bf16[1536,256]{1,0:T(8,128)(2,1)} %param.26) | copy-start | bytes 2359300
  3.2 17.3 %copy-start.1 = (bf16[24,1536]{1,0:T(8,128)(2,1)S(1)}, bf16[24,1536]{1,0:T(8,128)(2,1)}, u32[]{:S(2)}) copy-start(bf16[24,1536]{1,0:T(8,128)(2,1)} %param.20) | copy-start | bytes 221188
  3.3 35.8 %all-to-all-start = ((bf16[64,40,128]{2,1,0:T(8,128)(2,1)}), bf16[64,40,128]{2,1,0:T(8,128)(2,1)S(1)}, u32[]{:S(2)}, u32[]{:S(2)}) async-start(bf16[64,40,128]{2,1,0:T(8,128)(2,1)} %shard_map.166), calls=%async_computation | async-start | bytes 1310720 | tf_op jit(solution)/shard_map/all_to_all | solution.py:27
  21.6 0.7 copy-start.2
  41.3 20.3 %all-to-all-start.1 = ((bf16[64,8,128]{2,1,0:T(8,128)(2,1)}), bf16[64,8,128]{2,1,0:T(8,128)(2,1)S(1)}, u32[]{:S(2)}, u32[]{:S(2)}) async-start(bf16[64,8,128]{2,1,0:T(8,128)(2,1)} %pad_maximum_fusion), calls=%async_computation.1 | async-start | bytes 262144 | tf_op jit(solution)/shard_map/all_to_all | solution.py:27
  83.4 16.3 %all-to-all-start.3 = ((bf16[64,6,128]{2,1,0:T(8,128)(2,1)}), bf16[64,6,128]{2,1,0:T(8,128)(2,1)S(1)}, u32[]{:S(2)}, u32[]{:S(2)}) async-start(bf16[64,6,128]{2,1,0:T(8,128)(2,1)} %bitcast.77), calls=%async_computation.3 | async-start | bytes 262144 | tf_op jit(solution)/shard_map/all_to_all | solution.py:27
  101.2 21.9 %all-to-all-start.4 = ((bf16[256,4,128]{2,1,0:T(4,128)(2,1)}), bf16[256,4,128]{2,1,0:T(4,128)(2,1)S(1)}, u32[]{:S(2)}, u32[]{:S(2)}) async-start(bf16[256,4,128]{2,1,0:T(4,128)(2,1)} %broadcast_in_dim.29), calls=%async_computation.4 | async-start | bytes 524288 | tf_op jit(solution)/shard_map/all_to_all | solution.py:27
  110.6 0.7 copy-start.3
  110.6 0.7 copy-start.4
  111.3 0.7 copy-start.5

commit v7 on v6

--- a/solution.py
+++ b/solution.py
@@ -65,7 +65,8 @@
     cols = width // blocks
     w_rows = w_out.shape[0]
     n_w = -(-w_rows * cols // 128)
-    w_blocks = w_out.reshape(w_rows, blocks, cols).transpose(1, 0, 2).reshape(blocks, w_rows * cols)
+    w_blocks = w_out.reshape(w_rows, blocks // count, cols // 8, count, 8).transpose(1, 3, 0, 2, 4)
+    w_blocks = w_blocks.reshape(blocks, w_rows * cols)
     w_blocks = jnp.pad(w_blocks, ((0, 0), (0, n_w * 128 - w_rows * cols))).reshape(blocks, n_w, 128)
 
     n_kv = pair * span
@@ -96,19 +97,20 @@
     attn = got[:, :n_a].reshape(ny, nz, pair, group * HEAD_DIM).transpose(2, 1, 0, 3).reshape(count, width_q)
     part = jnp.dot(attn, w_cols, preferred_element_type=F32)
     own_lines = count * cols // 128
+    part = part.reshape(count, own_lines, 8).transpose(1, 0, 2)
     high, low = halves(part.reshape(own_lines, 128))
     got = exchange(to_all(jnp.concatenate([high, low, fresh], axis=0), blocks), BLK)
-    part = got[:, :own_lines].astype(F32) + got[:, own_lines : 2 * own_lines].astype(F32)
-    part = part.reshape(blocks, count, cols).transpose(1, 0, 2).reshape(count, width)
-
     fresh = got[:, 2 * own_lines :].reshape(ny, nz, 2, pair, HEAD_DIM).transpose(2, 3, 1, 0, 4)
     fresh = fresh.reshape(2, 1, count, width_k)
 
-    sent, mixed = expert_payload(block, hidden[0], part, router, routes[0], w_gate, w_up, w_down)
+    expert = block * w_gate.shape[1] // EXPERT_UNITS
+    expert_in, share, mixed = routed(expert, got, hidden[0], router.T, routes[0].T)
+    sent = expert_payload(expert_in, share, w_gate, w_up, w_down)
     got = exchange(sent.reshape(blocks, 2 * own_lines, 128), BLK)
 
     piece = jnp.sum(got[:, :own_lines].astype(F32) + got[:, own_lines : 2 * own_lines].astype(F32), axis=0)
     mixed_piece = lax.dynamic_index_in_dim(mixed.reshape(blocks, own_lines, 128), block, 0, False)
+    mixed_piece = lax.optimization_barrier(mixed_piece)
     piece = (mixed_piece + piece).astype(BF16)
     piece = jnp.concatenate([piece, jnp.zeros((1, 128), BF16)], axis=0)
     everyone = blocks * lax.axis_size("batch")
@@ -202,81 +204,92 @@
     )(block.reshape(1), hidden, w_qkv, keys, values)
 
 
-def expert_kernel(
-    block_ref,
-    hidden_ref,
-    part_ref,
-    router_ref,
-    routes_ref,
-    gate_hbm,
-    up_hbm,
-    down_hbm,
-    out_ref,
-    mixed_ref,
-    gate_ref,
-    up_ref,
-    down_ref,
-    lines,
-    sems,
+def route_kernel(
+    expert_ref, got_ref, hidden_ref, router_ref, routes_ref, in_ref, share_ref, mixed_ref, held, lines
 ):
-    copies = [
-        pltpu.make_async_copy(source, target, sems.at[n])
-        for n, (source, target) in enumerate(((gate_hbm, gate_ref), (up_hbm, up_ref), (down_hbm, down_ref)))
-    ]
-    for copy in copies:
-        copy.start()
     count, width = hidden_ref.shape
-    mixed = hidden_ref[...].astype(F32) + part_ref[...]
-    expert_in = rms(mixed).astype(BF16)
+    got = got_ref[...].astype(F32)
+    held[...] = got[:, :3] + got[:, 3:6]
+    parts = width // 384
+    blocks = [held[count * m : count * m + count, i, :] for m in range(parts) for i in range(3)]
+    part = jnp.stack(blocks, axis=0)
+    row = lax.broadcasted_iota(jnp.int32, part.shape, 1)
+    lane = lax.broadcasted_iota(jnp.int32, part.shape, 2) // 8
+    step = 1
+    while step < count:
+        down = pltpu.roll(pltpu.roll(part, count - step, 1), 8 * step, 2)
+        back = pltpu.roll(pltpu.roll(part, step, 1), 128 - 8 * step, 2)
+        low_row, low_lane = (row & step) == 0, (lane & step) == 0
+        part = jnp.where(low_row == low_lane, part, jnp.where(low_row, down, back))
+        step *= 2
+    hidden = hidden_ref[...].astype(F32)
+    total = jnp.zeros((count, 1), F32)
+    for n in range(3 * parts):
+        block = hidden[:, 128 * n : 128 * n + 128] + part[n]
+        total = total + jnp.sum(block * block, axis=1, keepdims=True)
+        mixed_ref[:, n // 3, n % 3, :] = block
+        lines[:, 128 * n : 128 * n + 128] = block
+    expert_in = (lines[...] * lax.rsqrt(total / width + EPS)).astype(BF16)
+    in_ref[...] = expert_in
     choice = lax.dot_general(
         router_ref[...], expert_in, (((1,), (1,)), ((), ())), preferred_element_type=F32
     )
     experts = lax.broadcasted_iota(jnp.int32, choice.shape, 0)
     routes = routes_ref[...]
     e1, e2 = routes[0:1], routes[1:2]
-    zero = jnp.zeros_like(choice)
-    c1 = jnp.sum(jnp.where(experts == e1, choice, zero), axis=0, keepdims=True)
-    c2 = jnp.sum(jnp.where(experts == e2, choice, zero), axis=0, keepdims=True)
+    c1 = jnp.sum(jnp.where(experts == e1, choice, 0.0), axis=0, keepdims=True)
+    c2 = jnp.sum(jnp.where(experts == e2, choice, 0.0), axis=0, keepdims=True)
     first = 1.0 / (1.0 + jnp.exp(c2 - c1))
-    mine = block_ref[0] * gate_ref.shape[1] // EXPERT_UNITS
-    share = jnp.where(e1 == mine, first, jnp.where(e2 == mine, 1.0 - first, 0.0))
+    share = jnp.where(e1 == expert_ref[0], first, jnp.where(e2 == expert_ref[0], 1.0 - first, 0.0))
     row = lax.broadcasted_iota(jnp.int32, (count, count), 0)
     column = lax.broadcasted_iota(jnp.int32, (count, count), 1)
     share = jnp.sum(jnp.where(row == column, share, 0.0), axis=1, keepdims=True)
-    copies[0].wait()
-    gate = jnp.dot(expert_in, gate_ref[...], preferred_element_type=F32)
-    copies[1].wait()
-    upper = jnp.dot(expert_in, up_ref[...], preferred_element_type=F32)
-    act = (gate / (1.0 + jnp.exp(-gate)) * upper * share).astype(BF16)
-    copies[2].wait()
-    out = jnp.dot(act, down_ref[...], preferred_element_type=F32)
-    parts = width // 384
-    for j in range(parts):
-        for i in range(3):
-            lanes = slice(128 * (3 * j + i), 128 * (3 * j + i) + 128)
-            line = out[:, lanes]
-            high = line.astype(BF16).astype(F32)
-            lines[:, j, i, :] = high
-            lines[:, j, 3 + i, :] = line - high
-            mixed_ref[:, j, i, :] = mixed[:, lanes]
-    out_ref[...] = lines[...].astype(BF16)
-
-
-def expert_payload(block, hidden, part, router, routes, w_gate, w_up, w_down):
+    share_ref[...] = jnp.broadcast_to(share, share_ref.shape)
+
+
+def routed(expert, got, hidden, router, routes):
     count, width = hidden.shape
     parts = width // 384
     return pl.pallas_call(
-        expert_kernel,
+        route_kernel,
         out_shape=(
-            jax.ShapeDtypeStruct((count, parts, 6, 128), BF16),
+            jax.ShapeDtypeStruct((count, width), BF16),
+            jax.ShapeDtypeStruct((count, 128), F32),
             jax.ShapeDtypeStruct((count, parts, 3, 128), F32),
         ),
-        in_specs=[SMEM] + [VMEM] * 4 + [HBM] * 3,
-        out_specs=(VMEM, VMEM),
-        scratch_shapes=[pltpu.VMEM(a.shape, a.dtype) for a in (w_gate, w_up, w_down)]
-        + [pltpu.VMEM((count, parts, 6, 128), F32), pltpu.SemaphoreType.DMA((3,))],
-        compiler_params=pltpu.CompilerParams(vmem_limit_bytes=60 << 20),
-    )(block.reshape(1), hidden, part, router.T, routes.T, w_gate, w_up, w_down)
+        in_specs=[SMEM] + [VMEM] * 4,
+        out_specs=(VMEM, VMEM, VMEM),
+        scratch_shapes=[pltpu.VMEM((got.shape[0], 3, 128), F32), pltpu.VMEM((count, width), F32)],
+        compiler_params=pltpu.CompilerParams(vmem_limit_bytes=16 << 20),
+    )(expert.reshape(1), got, hidden, router, routes)
+
+
+def expert_kernel(in_ref, share_ref, gate_ref, up_ref, down_ref, out_ref, lines):
+    expert_in = in_ref[...]
+    width = expert_in.shape[1]
+    gate = jnp.dot(expert_in, gate_ref[...], preferred_element_type=F32)
+    upper = jnp.dot(expert_in, up_ref[...], preferred_element_type=F32)
+    act = (gate / (1.0 + jnp.exp(-gate)) * upper * share_ref[:, 0:1]).astype(BF16)
+    out = jnp.dot(act, down_ref[...], preferred_element_type=F32)
+    for n in range(width // 128):
+        line = out[:, 128 * n : 128 * n + 128]
+        high = line.astype(BF16).astype(F32)
+        lines[:, n // 3, n % 3, :] = high
+        lines[:, n // 3, 3 + n % 3, :] = line - high
+    out_ref[...] = lines[...].astype(BF16)
+
+
+def expert_payload(expert_in, share, w_gate, w_up, w_down):
+    count, width = expert_in.shape
+    shape = (count, width // 384, 6, 128)
+    return pl.pallas_call(
+        expert_kernel,
+        out_shape=jax.ShapeDtypeStruct(shape, BF16),
+        in_specs=[VMEM] * 5,
+        out_specs=VMEM,
+        scratch_shapes=[pltpu.VMEM(shape, F32)],
+        compiler_params=pltpu.CompilerParams(vmem_limit_bytes=16 << 20),
+    )(expert_in, share, w_gate, w_up, w_down)
 
 
 def solution(mesh):

time: 132 us -> 130 us (0.985)
  blocking collectives: 22.5 us -> 6.97 us
  waiting for transfers between devices: 48.4 us -> 59.3 us
  starting transfers between devices: 40.1 us -> 44.7 us
  Pallas kernels: 6.31 us -> 4.57 us
    all_to_all x1 -> x0, blocking collectives: 15.5 us -> none  [exchange(): return lax.all_to_all(value, axes, 0, 0, tiled=True)]
    all_to_all x4 -> x5, waiting for transfers between devices: 48.4 us -> 59.3 us  [exchange(): return lax.all_to_all(value, axes, 0, 0, tiled=True)]
    all_to_all x4 -> x5, starting transfers between devices: 40.1 us -> 44.7 us  [exchange(): return lax.all_to_all(value, axes, 0, 0, tiled=True)]
    pallas_call x1 -> x2, Pallas kernels: 3.73 us -> 1.99 us  [the longest x1 1.29 us: expert_payload(): pl.pallas_call(expert_kernel, out_shape=jax.ShapeDtypeStruct(shape, BF16)...]
  transfers between devices with their start and end apart: 4 -> 5, of which waited for: 4 -> 5; matrix products, arithmetic and copies ran while one was open for 3% -> 4% of each run, Pallas kernels for 0% -> 0%
where the time goes in v7:
time: 130 us; the launch traced here: 129 us
  waiting for transfers between devices  59.3 us (46%)
  starting transfers between devices  44.7 us (34%)
  local copies, waits for them, and re-layouts  8.64 us (7%)
  blocking collectives  6.97 us (5%)
  Pallas kernels  4.57 us (4%)
  other arithmetic  3.11 us (2%)
    all_to_all x5, waiting for transfers between devices, exchange(): return lax.all_to_all(value, axes, 0, 0, tiled=True)  59.3 us
    all_to_all x5, starting transfers between devices, exchange(): return lax.all_to_all(value, axes, 0, 0, tiled=True)  44.7 us
    all_gather x1, blocking collectives, local(): both = lax.all_gather(stream_logits, 'guide', axis=0, tiled=False)  6.97 us
  transfers between devices with their start and end apart: 5, of which 5 were waited for; matrix products, arithmetic and copies ran while one was open for 4% of the time, Pallas kernels for 0%

profile of v7, /device:TPU:1, one launch (start us, length us, event | category | flops | bytes accessed | tf_op | source)
XLA Modules:
  0.0 129.4 jit_solution(14883799610706819495)
XLA Ops:
  0.7 2.6 %shard_map.166 = bf16[64,40,128]{2,1,0:T(8,128)(2,1)} custom-call(s32[1]{0:T(128)} %bitcast.1.block_ref, bf16[16,1536]{1,0:T(8,128)(2,1)} %bitcast.63, bf16[24,2560]{1,0:T(8,128)(2,1)} %w_hbm.1, bf16[16,16,512]{2,1,0:T(8,128)(2,1)} %bitcast.76, bf16[16,16,512]{2,1,0:T(8,128)(2,1)} %bitcast.77), custom_call_target="tpu_custom_call" | custom-call | tf_op jit(solution)/shard_map/pallas_call | solution.py:196
  3.3 17.3 %all-to-all-start = ((bf16[64,40,128]{2,1,0:T(8,128)(2,1)}), bf16[64,40,128]{2,1,0:T(8,128)(2,1)S(1)}, u32[]{:S(2)}, u32[]{:S(2)}) async-start(bf16[64,40,128]{2,1,0:T(8,128)(2,1)} %shard_map.166), calls=%async_computation | async-start | bytes 1310720 | tf_op jit(solution)/shard_map/all_to_all | solution.py:27
  20.6 0.5 broadcast.76
  21.2 0.7 reduce.13
  22.2 1.1 copy.39
  24.0 15.0 %all-to-all-done = bf16[64,40,128]{2,1,0:T(8,128)(2,1)S(1)} async-done(((bf16[64,40,128]{2,1,0:T(8,128)(2,1)}), bf16[64,40,128]{2,1,0:T(8,128)(2,1)S(1)}, u32[]{:S(2)}, u32[]{:S(2)}) %all-to-all-start) | async-done | bytes 655392 | tf_op jit(solution)/shard_map/all_to_all | solution.py:27
  40.6 0.7 pad_maximum_fusion
  41.3 8.8 %all-to-all-start.1 = ((bf16[64,8,128]{2,1,0:T(8,128)(2,1)}), bf16[64,8,128]{2,1,0:T(8,128)(2,1)S(1)}, u32[]{:S(2)}, u32[]{:S(2)}) async-start(bf16[64,8,128]{2,1,0:T(8,128)(2,1)} %pad_maximum_fusion), calls=%async_computation.1 | async-start | bytes 262144 | tf_op jit(solution)/shard_map/all_to_all | solution.py:27
  50.1 11.5 %all-to-all-done.1 = bf16[64,8,128]{2,1,0:T(8,128)(2,1)S(1)} async-done(((bf16[64,8,128]{2,1,0:T(8,128)(2,1)}), bf16[64,8,128]{2,1,0:T(8,128)(2,1)S(1)}, u32[]{:S(2)}, u32[]{:S(2)}) %all-to-all-start.1) | async-done | bytes 131104 | tf_op jit(solution)/shard_map/all_to_all | solution.py:27
  62.9 0.7 broadcast_in_dim.28
  63.6 4.6 %all-to-all-start.2 = ((bf16[64,8,128]{2,1,0:T(8,128)(2,1)}), bf16[64,8,128]{2,1,0:T(8,128)(2,1)S(1)}, u32[]{:S(2)}, u32[]{:S(2)}) async-start(bf16[64,8,128]{2,1,0:T(8,128)(2,1)} %broadcast_in_dim.28), calls=%async_computation.2 | async-start | bytes 262144 | tf_op jit(solution)/shard_map/all_to_all | solution.py:27
  68.2 11.7 %all-to-all-done.2.got_ref = bf16[64,8,128]{2,1,0:T(8,128)(2,1)S(1)} async-done(((bf16[64,8,128]{2,1,0:T(8,128)(2,1)}), bf16[64,8,128]{2,1,0:T(8,128)(2,1)S(1)}, u32[]{:S(2)}, u32[]{:S(2)}) %all-to-all-start.2) | async-done | bytes 131104 | tf_op jit(solution)/shard_map/all_to_all | solution.py:27
  79.9 0.7 shard_map.167
  80.6 1.3 shard_map.168
  81.9 4.6 %all-to-all-start.3 = ((bf16[64,6,128]{2,1,0:T(8,128)(2,1)}), bf16[64,6,128]{2,1,0:T(8,128)(2,1)S(1)}, u32[]{:S(2)}, u32[]{:S(2)}) async-start(bf16[64,6,128]{2,1,0:T(8,128)(2,1)} %bitcast.22), calls=%async_computation.3 | async-start | bytes 262144 | tf_op jit(solution)/shard_map/all_to_all | solution.py:27
  86.6 11.6 %all-to-all-done.3 = bf16[64,6,128]{2,1,0:T(8,128)(2,1)S(1)} async-done(((bf16[64,6,128]{2,1,0:T(8,128)(2,1)}), bf16[64,6,128]{2,1,0:T(8,128)(2,1)S(1)}, u32[]{:S(2)}, u32[]{:S(2)}) %all-to-all-start.3) | async-done | bytes 98336 | tf_op jit(solution)/shard_map/all_to_all | solution.py:27
  98.3 0.8 broadcast_in_dim.29
  99.0 9.4 %all-to-all-start.4 = ((bf16[256,4,128]{2,1,0:T(4,128)(2,1)}), bf16[256,4,128]{2,1,0:T(4,128)(2,1)S(1)}, u32[]{:S(2)}, u32[]{:S(2)}) async-start(bf16[256,4,128]{2,1,0:T(4,128)(2,1)} %broadcast_in_dim.29), calls=%async_computation.4 | async-start | bytes 524288 | tf_op jit(solution)/shard_map/all_to_all | solution.py:27
  108.5 0.6 copy-done.9
  110.1 0.7 squeeze.38
  110.9 0.7 squeeze.39
  111.6 9.4 %all-to-all-done.4 = bf16[256,4,128]{2,1,0:T(4,128)(2,1)S(1)} async-done(((bf16[256,4,128]{2,1,0:T(4,128)(2,1)}), bf16[256,4,128]{2,1,0:T(4,128)(2,1)S(1)}, u32[]{:S(2)}, u32[]{:S(2)}) %all-to-all-start.4) | async-done | bytes 262176 | tf_op jit(solution)/shard_map/all_to_all | solution.py:27
  121.7 7.0 %all-gather = bf16[128,256]{1,0:T(8,128)(2,1)S(1)} all-gather(bf16[64,256]{1,0:T(8,128)(2,1)S(1)} %convolution_convert_fusion), channel_id=2, replica_groups=mesh['guide'=2,'y'=8,'z'=8,'batch'=4] {'guide'}, dimensions={0}, use_global_device_ids=true | all-gather | bytes 98304 | tf_op jit(solution)/shard_map/all_gather | solution.py:123
  128.7 0.7 fusion.8
  (79 shorter events, 5.7 us)
Async XLA Ops:
  0.6 120.8 %copy-start = (bf16[1536,256]{1,0:T(8,128)(2,1)S(1)}, bf16[1536,256]{1,0:T(8,128)(2,1)}, u32[]{:S(2)}) copy-start(bf16[1536,256]{1,0:T(8,128)(2,1)} %param.26) | copy-start | bytes 2359300
  3.2 18.7 %copy-start.7 = (bf16[24,1536]{1,0:T(8,128)(2,1)S(1)}, bf16[24,1536]{1,0:T(8,128)(2,1)}, u32[]{:S(2)}) copy-start(bf16[24,1536]{1,0:T(8,128)(2,1)} %param.20) | copy-start | bytes 221188
  3.3 35.8 %all-to-all-start = ((bf16[64,40,128]{2,1,0:T(8,128)(2,1)}), bf16[64,40,128]{2,1,0:T(8,128)(2,1)S(1)}, u32[]{:S(2)}, u32[]{:S(2)}) async-start(bf16[64,40,128]{2,1,0:T(8,128)(2,1)} %shard_map.166), calls=%async_computation | async-start | bytes 1310720 | tf_op jit(solution)/shard_map/all_to_all | solution.py:27
  20.5 0.7 copy-start.8
  41.3 20.3 %all-to-all-start.1 = ((bf16[64,8,128]{2,1,0:T(8,128)(2,1)}), bf16[64,8,128]{2,1,0:T(8,128)(2,1)S(1)}, u32[]{:S(2)}, u32[]{:S(2)}) async-start(bf16[64,8,128]{2,1,0:T(8,128)(2,1)} %pad_maximum_fusion), calls=%async_computation.1 | async-start | bytes 262144 | tf_op jit(solution)/shard_map/all_to_all | solution.py:27
  61.7 18.9 %copy-start.3 = (bf16[256,1536]{1,0:T(8,128)(2,1)S(1)}, bf16[256,1536]{1,0:T(8,128)(2,1)}, u32[]{:S(2)}) copy-start(bf16[256,1536]{1,0:T(8,128)(2,1)} %down_ref.1) | copy-start | bytes 2359300
  62.1 17.8 %copy-start.4 = (bf16[1,16,1536]{2,1,0:T(8,128)(2,1)S(1)}, bf16[1,16,1536]{2,1,0:T(8,128)(2,1)}, u32[]{:S(2)}) copy-start(bf16[1,16,1536]{2,1,0:T(8,128)(2,1)} %param.15) | copy-start | bytes 147460
  62.1 17.8 %copy-start.5 = (bf16[1536,16]{0,1:T(8,128)(2,1)S(1)}, bf16[1536,16]{0,1:T(8,128)(2,1)}, u32[]{:S(2)}) copy-start(bf16[1536,16]{0,1:T(8,128)(2,1)} %param.21) | copy-start | bytes 147460
  62.1 17.8 %copy-start.6 = (s32[1,16,2]{1,2,0:T(2,128)S(1)}, s32[1,16,2]{1,2,0:T(2,128)}, u32[]{:S(2)}) copy-start(s32[1,16,2]{1,2,0:T(2,128)} %param.22) | copy-start | bytes 388
  62.1 18.5 %copy-start.2 = (bf16[1536,256]{1,0:T(8,128)(2,1)S(1)}, bf16[1536,256]{1,0:T(8,128)(2,1)}, u32[]{:S(2)}) copy-start(bf16[1536,256]{1,0:T(8,128)(2,1)} %up_ref.1) | copy-start | bytes 2359300
  62.3 18.3 %copy-start.1 = (bf16[1536,256]{1,0:T(8,128)(2,1)S(1)}, bf16[1536,256]{1,0:T(8,128)(2,1)}, u32[]{:S(2)}) copy-start(bf16[1536,256]{1,0:T(8,128)(2,1)} %gate_ref.1) | copy-start | bytes 2359300
  63.6 16.3 %all-to-all-start.2 = ((bf16[64,8,128]{2,1,0:T(8,128)(2,1)}), bf16[64,8,128]{2,1,0:T(8,128)(2,1)S(1)}, u32[]{:S(2)}, u32[]{:S(2)}) async-start(bf16[64,8,128]{2,1,0:T(8,128)(2,1)} %broadcast_in_dim.28), calls=%async_computation.2 | async-start | bytes 262144 | tf_op jit(solution)/shard_map/all_to_all | solution.py:27
  81.9 16.2 %all-to-all-start.3 = ((bf16[64,6,128]{2,1,0:T(8,128)(2,1)}), bf16[64,6,128]{2,1,0:T(8,128)(2,1)S(1)}, u32[]{:S(2)}, u32[]{:S(2)}) async-start(bf16[64,6,128]{2,1,0:T(8,128)(2,1)} %bitcast.22), calls=%async_computation.3 | async-start | bytes 262144 | tf_op jit(solution)/shard_map/all_to_all | solution.py:27
  99.0 21.9 %all-to-all-start.4 = ((bf16[256,4,128]{2,1,0:T(4,128)(2,1)}), bf16[256,4,128]{2,1,0:T(4,128)(2,1)S(1)}, u32[]{:S(2)}, u32[]{:S(2)}) async-start(bf16[256,4,128]{2,1,0:T(4,128)(2,1)} %broadcast_in_dim.29), calls=%async_computation.4 | async-start | bytes 524288 | tf_op jit(solution)/shard_map/all_to_all | solution.py:27
  108.4 0.7 copy-start.9
  108.5 0.7 copy-start.10
  109.1 0.7 copy-start.11

commit v8 on v7

--- a/solution.py
+++ b/solution.py
@@ -91,7 +91,13 @@
     attn = (acc / total[..., None]).astype(BF16)
     n_a = pair * group * HEAD_DIM // 128
     attn = jnp.broadcast_to(attn.reshape(1, n_a, 128), (blocks, n_a, 128))
-    got = exchange(jnp.concatenate([attn, w_blocks], axis=1), BLK)
+    half_rows = group_ids.shape[0] // 2
+    start = lax.axis_index("guide").astype(jnp.uint32) * half_rows
+    weight_rows = request_weights(group_ids, weight_index, guidance_levels)
+    weight_rows = lax.dynamic_slice(weight_rows, (start,), (half_rows,))
+    sent = jnp.concatenate([attn, w_blocks], axis=1)
+    sent, fresh, weight_rows, start = lax.optimization_barrier((sent, fresh, weight_rows, start))
+    got = exchange(sent, BLK)
 
     w_cols = got[:, n_a:].reshape(blocks, n_w * 128)[:, : w_rows * cols].reshape(-1, cols)
     attn = got[:, :n_a].reshape(ny, nz, pair, group * HEAD_DIM).transpose(2, 1, 0, 3).reshape(count, width_q)
@@ -100,17 +106,16 @@
     part = part.reshape(count, own_lines, 8).transpose(1, 0, 2)
     high, low = halves(part.reshape(own_lines, 128))
     got = exchange(to_all(jnp.concatenate([high, low, fresh], axis=0), blocks), BLK)
-    fresh = got[:, 2 * own_lines :].reshape(ny, nz, 2, pair, HEAD_DIM).transpose(2, 3, 1, 0, 4)
-    fresh = fresh.reshape(2, 1, count, width_k)
-
-    expert = block * w_gate.shape[1] // EXPERT_UNITS
-    expert_in, share, mixed = routed(expert, got, hidden[0], router.T, routes[0].T)
+    parts = width // (own_lines * 128)
+    expert = lax.div(block * w_gate.shape[1], EXPERT_UNITS)
+    where = jnp.stack([expert, lax.div(block, parts), lax.rem(block, parts)])
+    expert_in, share, mixed_piece, fresh_k, fresh_v = routed(
+        where, got, hidden[0], router.T, routes[0].T, width_k
+    )
     sent = expert_payload(expert_in, share, w_gate, w_up, w_down)
     got = exchange(sent.reshape(blocks, 2 * own_lines, 128), BLK)
 
     piece = jnp.sum(got[:, :own_lines].astype(F32) + got[:, own_lines : 2 * own_lines].astype(F32), axis=0)
-    mixed_piece = lax.dynamic_index_in_dim(mixed.reshape(blocks, own_lines, 128), block, 0, False)
-    mixed_piece = lax.optimization_barrier(mixed_piece)
     piece = (mixed_piece + piece).astype(BF16)
     piece = jnp.concatenate([piece, jnp.zeros((1, 128), BF16)], axis=0)
     everyone = blocks * lax.axis_size("batch")
@@ -118,20 +123,21 @@
     outgoing = lax.optimization_barrier(got[:, :own_lines].astype(F32).reshape(-1, width))
     final_in = rms(outgoing).astype(BF16)
     stream_logits = jnp.dot(final_in, w_vocab, preferred_element_type=F32).astype(BF16)
-    stream = lax.axis_index("guide")
-    half_rows = stream_logits.shape[0] // 2
     both = lax.all_gather(stream_logits, "guide", axis=0, tiled=False)
-    both = lax.dynamic_slice_in_dim(both, stream * half_rows, half_rows, 1).astype(F32)
+    zero = jnp.zeros((), start.dtype)
+    both = lax.dynamic_slice(both, (zero, start, zero), (2, half_rows, both.shape[2])).astype(F32)
     cond, uncond = both[0], both[1]
+    logits = uncond + weight_rows[:, None] * (cond - uncond)
+    return (logits, fresh_k[None], fresh_v[None])
+
+
+def request_weights(group_ids, weight_index, guidance_levels):
     group_count = weight_index.shape[0]
     level_count = guidance_levels.shape[0]
     in_group = (group_ids[:, None] == jnp.arange(group_count)[None, :]).astype(F32)
     level_pick = (weight_index[:, None] == jnp.arange(level_count)[None, :]).astype(F32)
     group_weight = jnp.sum(level_pick * guidance_levels[None, :], axis=1)
-    request_weight = jnp.sum(in_group * group_weight[None, :], axis=1)
-    weight_rows = lax.dynamic_slice_in_dim(request_weight, stream * half_rows, half_rows, 0)
-    logits = uncond + weight_rows[:, None] * (cond - uncond)
-    return (logits, fresh[0], fresh[1])
+    return jnp.sum(in_group * group_weight[None, :], axis=1)
 
 
 def to_all(lines, number):
@@ -205,11 +211,34 @@
 
 
 def route_kernel(
-    expert_ref, got_ref, hidden_ref, router_ref, routes_ref, in_ref, share_ref, mixed_ref, held, lines
+    where_ref,
+    got_ref,
+    hidden_ref,
+    router_ref,
+    routes_ref,
+    in_ref,
+    share_ref,
+    piece_ref,
+    key_ref,
+    value_ref,
+    held,
+    lines,
+    mixed_ref,
 ):
     count, width = hidden_ref.shape
     got = got_ref[...].astype(F32)
-    held[...] = got[:, :3] + got[:, 3:6]
+    held[:, :3, :] = got[:, :3] + got[:, 3:6]
+    held[:, 3:, :] = got[:, 6:]
+    half = count // 2
+    low_lane = lax.broadcasted_iota(jnp.int32, (half, 128), 1) < 64
+    for n, out_ref in ((3, key_ref), (4, value_ref)):
+        for v in range(out_ref.shape[1] // 128):
+            even = held[2 * half * v : 2 * half * v + half, n, :]
+            odd = held[2 * half * v + half : 2 * half * v + 2 * half, n, :]
+            first = jnp.where(low_lane, even, pltpu.roll(odd, 64, 1))
+            second = jnp.where(low_lane, pltpu.roll(even, 64, 1), odd)
+            both = jnp.concatenate([first, second], axis=0)
+            out_ref[:, 128 * v : 128 * v + 128] = both.astype(BF16)
     parts = width // 384
     blocks = [held[count * m : count * m + count, i, :] for m in range(parts) for i in range(3)]
     part = jnp.stack(blocks, axis=0)
@@ -231,6 +260,7 @@
         lines[:, 128 * n : 128 * n + 128] = block
     expert_in = (lines[...] * lax.rsqrt(total / width + EPS)).astype(BF16)
     in_ref[...] = expert_in
+    piece_ref[...] = mixed_ref[where_ref[1], where_ref[2]]
     choice = lax.dot_general(
         router_ref[...], expert_in, (((1,), (1,)), ((), ())), preferred_element_type=F32
     )
@@ -240,14 +270,14 @@
     c1 = jnp.sum(jnp.where(experts == e1, choice, 0.0), axis=0, keepdims=True)
     c2 = jnp.sum(jnp.where(experts == e2, choice, 0.0), axis=0, keepdims=True)
     first = 1.0 / (1.0 + jnp.exp(c2 - c1))
-    share = jnp.where(e1 == expert_ref[0], first, jnp.where(e2 == expert_ref[0], 1.0 - first, 0.0))
+    share = jnp.where(e1 == where_ref[0], first, jnp.where(e2 == where_ref[0], 1.0 - first, 0.0))
     row = lax.broadcasted_iota(jnp.int32, (count, count), 0)
     column = lax.broadcasted_iota(jnp.int32, (count, count), 1)
     share = jnp.sum(jnp.where(row == column, share, 0.0), axis=1, keepdims=True)
     share_ref[...] = jnp.broadcast_to(share, share_ref.shape)
 
 
-def routed(expert, got, hidden, router, routes):
+def routed(where, got, hidden, router, routes, width_k):
     count, width = hidden.shape
     parts = width // 384
     return pl.pallas_call(
@@ -255,13 +285,19 @@
         out_shape=(
             jax.ShapeDtypeStruct((count, width), BF16),
             jax.ShapeDtypeStruct((count, 128), F32),
-            jax.ShapeDtypeStruct((count, parts, 3, 128), F32),
+            jax.ShapeDtypeStruct((3, 128), F32),
+            jax.ShapeDtypeStruct((count, width_k), BF16),
+            jax.ShapeDtypeStruct((count, width_k), BF16),
         ),
         in_specs=[SMEM] + [VMEM] * 4,
-        out_specs=(VMEM, VMEM, VMEM),
-        scratch_shapes=[pltpu.VMEM((got.shape[0], 3, 128), F32), pltpu.VMEM((count, width), F32)],
+        out_specs=(VMEM,) * 5,
+        scratch_shapes=[
+            pltpu.VMEM((got.shape[0], 5, 128), F32),
+            pltpu.VMEM((count, width), F32),
+            pltpu.VMEM((count, parts, 3, 128), F32),
+        ],
         compiler_params=pltpu.CompilerParams(vmem_limit_bytes=16 << 20),
-    )(expert.reshape(1), got, hidden, router, routes)
+    )(where, got, hidden, router, routes)
 
 
 def expert_kernel(in_ref, share_ref, gate_ref, up_ref, down_ref, out_ref, lines):

time: 130 us -> 128 us (0.985)
  blocking collectives: 6.97 us -> 64.3 us
  waiting for transfers between devices: 59.3 us -> 25.2 us
  starting transfers between devices: 44.7 us -> 21.9 us
  local copies, waits for them, and re-layouts: 8.64 us -> 6.35 us
    all_to_all x0 -> x3, blocking collectives: none -> 57.3 us  [exchange(): return lax.all_to_all(value, axes, 0, 0, tiled=True)]
    all_to_all x5 -> x2, waiting for transfers between devices: 59.3 us -> 25.2 us  [exchange(): return lax.all_to_all(value, axes, 0, 0, tiled=True)]
    all_to_all x5 -> x2, starting transfers between devices: 44.7 us -> 21.9 us  [exchange(): return lax.all_to_all(value, axes, 0, 0, tiled=True)]
    squeeze x3 -> x0, local copies, waits for them, and re-layouts: 1.41 us -> none  [the longest x2 1.4 us: local(): return (logits, fresh[0], fresh[1])]
  transfers between devices with their start and end apart: 5 -> 2, of which waited for: 5 -> 2; matrix products, arithmetic and copies ran while one was open for 4% -> 3% of each run, Pallas kernels for 0% -> 0%
where the time goes in v8:
time: 128 us; the launch traced here: 127 us
  blocking collectives  64.3 us (50%)
  waiting for transfers between devices  25.2 us (20%)
  starting transfers between devices  21.9 us (17%)
  local copies, waits for them, and re-layouts  6.35 us (5%)
  Pallas kernels  5.09 us (4%)
  other arithmetic  2.55 us (2%)
    all_to_all x3, blocking collectives, exchange(): return lax.all_to_all(value, axes, 0, 0, tiled=True)  57.3 us
    all_to_all x2, waiting for transfers between devices, exchange(): return lax.all_to_all(value, axes, 0, 0, tiled=True)  25.2 us
    all_to_all x2, starting transfers between devices, exchange(): return lax.all_to_all(value, axes, 0, 0, tiled=True)  21.9 us
    all_gather x1, blocking collectives, local(): both = lax.all_gather(stream_logits, 'guide', axis=0, tiled=False)  6.97 us
    pallas_call x1, Pallas kernels, first_payload(): pl.pallas_call(first_payload_kernel, out_shape=jax.ShapeDtypeStruct((bloc...  2.58 us
  transfers between devices with their start and end apart: 2, of which 2 were waited for; matrix products, arithmetic and copies ran while one was open for 3% of the time, Pallas kernels for 0%

profile of v8, /device:TPU:1, one launch (start us, length us, event | category | flops | bytes accessed | tf_op | source)
XLA Modules:
  0.0 127.3 jit_solution(3339328702049005545)
XLA Ops:
  0.7 2.6 %shard_map.166 = bf16[64,40,128]{2,1,0:T(8,128)(2,1)} custom-call(s32[1]{0:T(128)} %bitcast.3.block_ref, bf16[16,1536]{1,0:T(8,128)(2,1)} %bitcast.60, bf16[24,2560]{1,0:T(8,128)(2,1)} %w_hbm.1, bf16[16,16,512]{2,1,0:T(8,128)(2,1)} %bitcast.72, bf16[16,16,512]{2,1,0:T(8,128)(2,1)} %bitcast.73), custom_call_target="tpu_custom_call" | custom-call | tf_op jit(solution)/shard_map/pallas_call | solution.py:202
  3.3 17.3 %all-to-all-start = ((bf16[64,40,128]{2,1,0:T(8,128)(2,1)}), bf16[64,40,128]{2,1,0:T(8,128)(2,1)S(1)}, u32[]{:S(2)}, u32[]{:S(2)}) async-start(bf16[64,40,128]{2,1,0:T(8,128)(2,1)} %shard_map.166), calls=%async_computation | async-start | bytes 1310720 | tf_op jit(solution)/shard_map/all_to_all | solution.py:27
  20.6 0.5 broadcast.76
  21.2 0.7 reduce.13
  22.0 0.2 copy.34
  22.2 1.1 copy.35
  23.2 0.3 reshape.125
  24.0 0.6 copy-done.9
  24.8 0.5 copy-done.11
  25.5 13.5 %all-to-all-done = bf16[64,40,128]{2,1,0:T(8,128)(2,1)S(1)} async-done(((bf16[64,40,128]{2,1,0:T(8,128)(2,1)}), bf16[64,40,128]{2,1,0:T(8,128)(2,1)S(1)}, u32[]{:S(2)}, u32[]{:S(2)}) %all-to-all-start) | async-done | bytes 655392 | tf_op jit(solution)/shard_map/all_to_all | solution.py:27
  39.5 0.3 select_reduce_fusion
  40.1 0.3 fusion.1
  40.7 20.1 %all_to_all.25 = bf16[64,8,128]{2,1,0:T(8,128)(2,1)S(1)} all-to-all(bf16[64,8,128]{2,1,0:T(8,128)(2,1)S(1)} %pad_maximum_fusion), channel_id=1, replica_groups=mesh['guide'=2,'y'=8,'z'=8,'batch'=4] {'y','z'}, dimensions={0} | all-to-all | bytes 262144 | tf_op jit(solution)/shard_map/all_to_all | solution.py:27
  60.9 0.3 reshape.130
  62.1 0.7 broadcast_in_dim.32
  62.7 4.6 %all-to-all-start.2 = ((bf16[64,8,128]{2,1,0:T(8,128)(2,1)}), bf16[64,8,128]{2,1,0:T(8,128)(2,1)S(1)}, u32[]{:S(2)}, u32[]{:S(2)}) async-start(bf16[64,8,128]{2,1,0:T(8,128)(2,1)} %broadcast_in_dim.32), calls=%async_computation.2 | async-start | bytes 262144 | tf_op jit(solution)/shard_map/all_to_all | solution.py:27
  67.4 11.6 %all-to-all-done.2.got_ref = bf16[64,8,128]{2,1,0:T(8,128)(2,1)S(1)} async-done(((bf16[64,8,128]{2,1,0:T(8,128)(2,1)}), bf16[64,8,128]{2,1,0:T(8,128)(2,1)S(1)}, u32[]{:S(2)}, u32[]{:S(2)}) %all-to-all-start.2) | async-done | bytes 131104 | tf_op jit(solution)/shard_map/all_to_all | solution.py:27
  79.1 1.9 %shard_map.167 = (bf16[16,1536]{1,0:T(8,128)(2,1)S(1)}, f32[16,128]{1,0:T(8,128)S(1)}, f32[3,128]{1,0:T(4,128)S(1)}, bf16[16,512]{1,0:T(8,128)(2,1)}, bf16[16,512]{1,0:T(8,128)(2,1)}) custom-call(s32[3]{0:T(128)S(1)} %pad_add_fusion.where_ref, bf16[64,8,128]{2,1,0:T(8,128)(2,1)S(1)} %all-to-all-done.2.got_ref, bf16[16,1536]{1,0:T(8,128)(2,1)S(1)} %bitcast.61, ...), custom_call_target="tpu_custom_call" | custom-call | tf_op jit(solution)/shard_map/pallas_call | solution.py:283
  81.0 0.6 shard_map.168
  81.6 15.4 %all_to_all.26 = bf16[64,6,128]{2,1,0:T(8,128)(2,1)S(1)} all-to-all(bf16[64,6,128]{2,1,0:T(8,128)(2,1)S(1)} %bitcast.59), channel_id=1, replica_groups=mesh['guide'=2,'y'=8,'z'=8,'batch'=4] {'y','z'}, dimensions={0} | all-to-all | bytes 196608 | tf_op jit(solution)/shard_map/all_to_all | solution.py:27
  97.2 21.7 %all_to_all.27 = bf16[256,4,128]{2,1,0:T(4,128)(2,1)S(1)} all-to-all(bf16[256,4,128]{2,1,0:T(4,128)(2,1)S(1)} %broadcast_in_dim.33), channel_id=1, replica_groups=mesh['guide'=2,'y'=8,'z'=8,'batch'=4] {'batch','y','z'}, dimensions={0} | all-to-all | bytes 524288 | tf_op jit(solution)/shard_map/all_to_all | solution.py:27
  119.4 0.3 convolution_convert_fusion
  119.7 7.0 %all-gather = bf16[128,256]{1,0:T(8,128)(2,1)S(1)} all-gather(bf16[64,256]{1,0:T(8,128)(2,1)S(1)} %convolution_convert_fusion), channel_id=2, replica_groups=mesh['guide'=2,'y'=8,'z'=8,'batch'=4] {'guide'}, dimensions={0}, use_global_device_ids=true | all-gather | bytes 98304 | tf_op jit(solution)/shard_map/all_gather | solution.py:126
  126.6 0.7 fusion.8
  (69 shorter events, 3.5 us)
Async XLA Ops:
  0.6 118.7 %copy-start = (bf16[1536,256]{1,0:T(8,128)(2,1)S(1)}, bf16[1536,256]{1,0:T(8,128)(2,1)}, u32[]{:S(2)}) copy-start(bf16[1536,256]{1,0:T(8,128)(2,1)} %param.26) | copy-start | bytes 2359300
  3.2 18.7 %copy-start.7 = (bf16[24,1536]{1,0:T(8,128)(2,1)S(1)}, bf16[24,1536]{1,0:T(8,128)(2,1)}, u32[]{:S(2)}) copy-start(bf16[24,1536]{1,0:T(8,128)(2,1)} %param.20) | copy-start | bytes 221188
  3.3 35.8 %all-to-all-start = ((bf16[64,40,128]{2,1,0:T(8,128)(2,1)}), bf16[64,40,128]{2,1,0:T(8,128)(2,1)S(1)}, u32[]{:S(2)}, u32[]{:S(2)}) async-start(bf16[64,40,128]{2,1,0:T(8,128)(2,1)} %shard_map.166), calls=%async_computation | async-start | bytes 1310720 | tf_op jit(solution)/shard_map/all_to_all | solution.py:27
  20.5 0.7 copy-start.8
  24.0 0.7 copy-start.9
  24.0 0.7 copy-start.10
  24.6 0.7 copy-start.11
  60.9 20.1 %copy-start.3 = (bf16[256,1536]{1,0:T(8,128)(2,1)S(1)}, bf16[256,1536]{1,0:T(8,128)(2,1)}, u32[]{:S(2)}) copy-start(bf16[256,1536]{1,0:T(8,128)(2,1)} %down_ref.1) | copy-start | bytes 2359300
  61.2 17.8 %copy-start.4 = (bf16[1,16,1536]{2,1,0:T(8,128)(2,1)S(1)}, bf16[1,16,1536]{2,1,0:T(8,128)(2,1)}, u32[]{:S(2)}) copy-start(bf16[1,16,1536]{2,1,0:T(8,128)(2,1)} %param.15) | copy-start | bytes 147460
  61.3 17.8 %copy-start.5 = (bf16[1536,16]{0,1:T(8,128)(2,1)S(1)}, bf16[1536,16]{0,1:T(8,128)(2,1)}, u32[]{:S(2)}) copy-start(bf16[1536,16]{0,1:T(8,128)(2,1)} %param.21) | copy-start | bytes 147460
  61.3 17.8 %copy-start.6 = (s32[1,16,2]{1,2,0:T(2,128)S(1)}, s32[1,16,2]{1,2,0:T(2,128)}, u32[]{:S(2)}) copy-start(s32[1,16,2]{1,2,0:T(2,128)} %param.22) | copy-start | bytes 388
  61.3 19.7 %copy-start.2 = (bf16[1536,256]{1,0:T(8,128)(2,1)S(1)}, bf16[1536,256]{1,0:T(8,128)(2,1)}, u32[]{:S(2)}) copy-start(bf16[1536,256]{1,0:T(8,128)(2,1)} %up_ref.1) | copy-start | bytes 2359300
  61.4 19.5 %copy-start.1 = (bf16[1536,256]{1,0:T(8,128)(2,1)S(1)}, bf16[1536,256]{1,0:T(8,128)(2,1)}, u32[]{:S(2)}) copy-start(bf16[1536,256]{1,0:T(8,128)(2,1)} %gate_ref.1) | copy-start | bytes 2359300
  62.7 16.3 %all-to-all-start.2 = ((bf16[64,8,128]{2,1,0:T(8,128)(2,1)}), bf16[64,8,128]{2,1,0:T(8,128)(2,1)S(1)}, u32[]{:S(2)}, u32[]{:S(2)}) async-start(bf16[64,8,128]{2,1,0:T(8,128)(2,1)} %broadcast_in_dim.32), calls=%async_computation.2 | async-start | bytes 262144 | tf_op jit(solution)/shard_map/all_to_all | solution.py:27

commit v9 on v8

--- a/solution.py
+++ b/solution.py
@@ -92,11 +92,15 @@
     n_a = pair * group * HEAD_DIM // 128
     attn = jnp.broadcast_to(attn.reshape(1, n_a, 128), (blocks, n_a, 128))
     half_rows = group_ids.shape[0] // 2
-    start = lax.axis_index("guide").astype(jnp.uint32) * half_rows
+    stream = lax.axis_index("guide")
     weight_rows = request_weights(group_ids, weight_index, guidance_levels)
-    weight_rows = lax.dynamic_slice(weight_rows, (start,), (half_rows,))
+    weight_rows = lax.dynamic_slice(weight_rows, (stream.astype(jnp.uint32) * half_rows,), (half_rows,))
+    weight_rows = jnp.broadcast_to(weight_rows[:, None], (half_rows, w_vocab.shape[1]))
+    parts = width // 384
+    expert = lax.div(block * w_gate.shape[1], EXPERT_UNITS)
+    where = jnp.stack([expert, lax.div(block, parts), lax.rem(block, parts)])
     sent = jnp.concatenate([attn, w_blocks], axis=1)
-    sent, fresh, weight_rows, start = lax.optimization_barrier((sent, fresh, weight_rows, start))
+    sent, fresh, weight_rows, stream, where = lax.optimization_barrier((sent, fresh, weight_rows, stream, where))
     got = exchange(sent, BLK)
 
     w_cols = got[:, n_a:].reshape(blocks, n_w * 128)[:, : w_rows * cols].reshape(-1, cols)
@@ -106,9 +110,6 @@
     part = part.reshape(count, own_lines, 8).transpose(1, 0, 2)
     high, low = halves(part.reshape(own_lines, 128))
     got = exchange(to_all(jnp.concatenate([high, low, fresh], axis=0), blocks), BLK)
-    parts = width // (own_lines * 128)
-    expert = lax.div(block * w_gate.shape[1], EXPERT_UNITS)
-    where = jnp.stack([expert, lax.div(block, parts), lax.rem(block, parts)])
     expert_in, share, mixed_piece, fresh_k, fresh_v = routed(
         where, got, hidden[0], router.T, routes[0].T, width_k
     )
@@ -124,11 +125,32 @@
     final_in = rms(outgoing).astype(BF16)
     stream_logits = jnp.dot(final_in, w_vocab, preferred_element_type=F32).astype(BF16)
     both = lax.all_gather(stream_logits, "guide", axis=0, tiled=False)
-    zero = jnp.zeros((), start.dtype)
-    both = lax.dynamic_slice(both, (zero, start, zero), (2, half_rows, both.shape[2])).astype(F32)
-    cond, uncond = both[0], both[1]
-    logits = uncond + weight_rows[:, None] * (cond - uncond)
-    return (logits, fresh_k[None], fresh_v[None])
+    return last_outputs(stream, both, weight_rows, fresh_k, fresh_v)
+
+
+def last_kernel(stream_ref, both_ref, weight_ref, key_in, value_in, logits_ref, key_ref, value_ref):
+    half_rows = logits_ref.shape[0]
+    first = stream_ref[0] == 0
+    cond = jnp.where(first, both_ref[0, :half_rows], both_ref[0, half_rows:]).astype(F32)
+    uncond = jnp.where(first, both_ref[1, :half_rows], both_ref[1, half_rows:]).astype(F32)
+    logits_ref[...] = uncond + weight_ref[...] * (cond - uncond)
+    key_ref[0] = key_in[...].astype(BF16)
+    value_ref[0] = value_in[...].astype(BF16)
+
+
+def last_outputs(stream, both, weight_rows, fresh_k, fresh_v):
+    shape = weight_rows.shape
+    return pl.pallas_call(
+        last_kernel,
+        out_shape=(
+            jax.ShapeDtypeStruct(shape, F32),
+            jax.ShapeDtypeStruct((1,) + fresh_k.shape, BF16),
+            jax.ShapeDtypeStruct((1,) + fresh_v.shape, BF16),
+        ),
+        in_specs=[SMEM] + [VMEM] * 4,
+        out_specs=(VMEM,) * 3,
+        compiler_params=pltpu.CompilerParams(vmem_limit_bytes=16 << 20),
+    )(stream.reshape(1), both, weight_rows, fresh_k, fresh_v)
 
 
 def request_weights(group_ids, weight_index, guidance_levels):
@@ -237,8 +259,7 @@
             odd = held[2 * half * v + half : 2 * half * v + 2 * half, n, :]
             first = jnp.where(low_lane, even, pltpu.roll(odd, 64, 1))
             second = jnp.where(low_lane, pltpu.roll(even, 64, 1), odd)
-            both = jnp.concatenate([first, second], axis=0)
-            out_ref[:, 128 * v : 128 * v + 128] = both.astype(BF16)
+            out_ref[:, 128 * v : 128 * v + 128] = jnp.concatenate([first, second], axis=0)
     parts = width // 384
     blocks = [held[count * m : count * m + count, i, :] for m in range(parts) for i in range(3)]
     part = jnp.stack(blocks, axis=0)
@@ -286,8 +307,8 @@
             jax.ShapeDtypeStruct((count, width), BF16),
             jax.ShapeDtypeStruct((count, 128), F32),
             jax.ShapeDtypeStruct((3, 128), F32),
-            jax.ShapeDtypeStruct((count, width_k), BF16),
-            jax.ShapeDtypeStruct((count, width_k), BF16),
+            jax.ShapeDtypeStruct((count, width_k), F32),
+            jax.ShapeDtypeStruct((count, width_k), F32),
         ),
         in_specs=[SMEM] + [VMEM] * 4,
         out_specs=(VMEM,) * 5,

time: 128 us -> 127 us (level)
  blocking collectives: 64.3 us -> 79.8 us
  waiting for transfers between devices: 25.2 us -> 13.4 us
  starting transfers between devices: 21.9 us -> 17.3 us
    all_to_all x3 -> x4, blocking collectives: 57.3 us -> 72.8 us  [exchange(): return lax.all_to_all(value, axes, 0, 0, tiled=True)]
    all_to_all x2 -> x1, waiting for transfers between devices: 25.2 us -> 13.4 us  [exchange(): return lax.all_to_all(value, axes, 0, 0, tiled=True)]
    all_to_all x2 -> x1, starting transfers between devices: 21.9 us -> 17.3 us  [exchange(): return lax.all_to_all(value, axes, 0, 0, tiled=True)]
  transfers between devices with their start and end apart: 2 -> 1, of which waited for: 2 -> 1; matrix products, arithmetic and copies ran while one was open for 3% -> 3% of each run, Pallas kernels for 0% -> 0%
where the time goes in v9:
time: 127 us; the launch traced here: 126 us
  blocking collectives  79.8 us (63%)
  starting transfers between devices  17.3 us (14%)
  waiting for transfers between devices  13.4 us (11%)
  local copies, waits for them, and re-layouts  6.33 us (5%)
  Pallas kernels  5.1 us (4%)
  other arithmetic  2.51 us (2%)
    all_to_all x4, blocking collectives, exchange(): return lax.all_to_all(value, axes, 0, 0, tiled=True)  72.8 us
    all_to_all x1, starting transfers between devices, exchange(): return lax.all_to_all(value, axes, 0, 0, tiled=True)  17.3 us
    all_to_all x1, waiting for transfers between devices, exchange(): return lax.all_to_all(value, axes, 0, 0, tiled=True)  13.4 us
    all_gather x1, blocking collectives, local(): both = lax.all_gather(stream_logits, 'guide', axis=0, tiled=False)  6.97 us
    pallas_call x1, Pallas kernels, first_payload(): pl.pallas_call(first_payload_kernel, out_shape=jax.ShapeDtypeStruct((bloc...  2.58 us
  transfers between devices with their start and end apart: 1, of which 1 were waited for; matrix products, arithmetic and copies ran while one was open for 3% of the time, Pallas kernels for 0%

profile of v9, /device:TPU:1, one launch (start us, length us, event | category | flops | bytes accessed | tf_op | source)
XLA Modules:
  0.0 126.4 jit_solution(12322487748760319981)
XLA Ops:
  0.7 2.6 %shard_map.166 = bf16[64,40,128]{2,1,0:T(8,128)(2,1)} custom-call(s32[1]{0:T(128)} %bitcast.block_ref, bf16[16,1536]{1,0:T(8,128)(2,1)} %bitcast.48, bf16[24,2560]{1,0:T(8,128)(2,1)} %w_hbm.1, bf16[16,16,512]{2,1,0:T(8,128)(2,1)} %bitcast.60, bf16[16,16,512]{2,1,0:T(8,128)(2,1)} %bitcast.61), custom_call_target="tpu_custom_call" | custom-call | tf_op jit(solution)/shard_map/pallas_call | solution.py:224
  3.3 17.3 %all-to-all-start = ((bf16[64,40,128]{2,1,0:T(8,128)(2,1)}), bf16[64,40,128]{2,1,0:T(8,128)(2,1)S(1)}, u32[]{:S(2)}, u32[]{:S(2)}) async-start(bf16[64,40,128]{2,1,0:T(8,128)(2,1)} %shard_map.166), calls=%async_computation | async-start | bytes 1310720 | tf_op jit(solution)/shard_map/all_to_all | solution.py:27
  20.6 0.5 broadcast.76
  21.2 0.7 reduce.13
  22.0 0.2 copy.34
  22.2 1.1 copy.35
  23.3 0.3 reshape.128
  24.0 0.6 copy-done.9
  24.8 0.5 copy-done.11
  25.6 13.4 %all-to-all-done = bf16[64,40,128]{2,1,0:T(8,128)(2,1)S(1)} async-done(((bf16[64,40,128]{2,1,0:T(8,128)(2,1)}), bf16[64,40,128]{2,1,0:T(8,128)(2,1)S(1)}, u32[]{:S(2)}, u32[]{:S(2)}) %all-to-all-start) | async-done | bytes 655392 | tf_op jit(solution)/shard_map/all_to_all | solution.py:27
  39.2 0.5 slice.56
  40.0 0.3 select_reduce_fusion
  40.6 0.3 fusion.1
  41.3 20.1 %all_to_all.25 = bf16[64,8,128]{2,1,0:T(8,128)(2,1)S(1)} all-to-all(bf16[64,8,128]{2,1,0:T(8,128)(2,1)S(1)} %pad_maximum_fusion), channel_id=1, replica_groups=mesh['guide'=2,'y'=8,'z'=8,'batch'=4] {'y','z'}, dimensions={0} | all-to-all | bytes 262144 | tf_op jit(solution)/shard_map/all_to_all | solution.py:27
  61.5 0.3 reshape.134
  62.6 0.7 pad_maximum_fusion.1
  63.3 15.5 %all_to_all.26.got_ref = bf16[64,8,128]{2,1,0:T(8,128)(2,1)S(1)} all-to-all(bf16[64,8,128]{2,1,0:T(8,128)(2,1)S(1)} %broadcast_in_dim.31), channel_id=1, replica_groups=mesh['guide'=2,'y'=8,'z'=8,'batch'=4] {'y','z'}, dimensions={0} | all-to-all | bytes 262144 | tf_op jit(solution)/shard_map/all_to_all | solution.py:27
  78.8 1.3 shard_map.167
  80.1 0.6 shard_map.168
  80.8 15.4 %all_to_all.27 = bf16[64,6,128]{2,1,0:T(8,128)(2,1)S(1)} all-to-all(bf16[64,6,128]{2,1,0:T(8,128)(2,1)S(1)} %bitcast.46), channel_id=1, replica_groups=mesh['guide'=2,'y'=8,'z'=8,'batch'=4] {'y','z'}, dimensions={0} | all-to-all | bytes 196608 | tf_op jit(solution)/shard_map/all_to_all | solution.py:27
  96.3 21.7 %all_to_all.28 = bf16[256,4,128]{2,1,0:T(4,128)(2,1)S(1)} all-to-all(bf16[256,4,128]{2,1,0:T(4,128)(2,1)S(1)} %broadcast_in_dim.32), channel_id=1, replica_groups=mesh['guide'=2,'y'=8,'z'=8,'batch'=4] {'batch','y','z'}, dimensions={0} | all-to-all | bytes 524288 | tf_op jit(solution)/shard_map/all_to_all | solution.py:27
  118.5 0.3 convolution_convert_fusion
  118.8 7.0 %all-gather = bf16[128,256]{1,0:T(8,128)(2,1)S(1)} all-gather(bf16[64,256]{1,0:T(8,128)(2,1)S(1)} %convolution_convert_fusion), channel_id=2, replica_groups=mesh['guide'=2,'y'=8,'z'=8,'batch'=4] {'guide'}, dimensions={0}, use_global_device_ids=true | all-gather | bytes 98304 | tf_op jit(solution)/shard_map/all_gather | solution.py:127
  125.8 0.6 shard_map.169
  (68 shorter events, 3.5 us)
Async XLA Ops:
  0.6 117.9 %copy-start = (bf16[1536,256]{1,0:T(8,128)(2,1)S(1)}, bf16[1536,256]{1,0:T(8,128)(2,1)}, u32[]{:S(2)}) copy-start(bf16[1536,256]{1,0:T(8,128)(2,1)} %param.26) | copy-start | bytes 2359300
  3.2 18.7 %copy-start.7 = (bf16[24,1536]{1,0:T(8,128)(2,1)S(1)}, bf16[24,1536]{1,0:T(8,128)(2,1)}, u32[]{:S(2)}) copy-start(bf16[24,1536]{1,0:T(8,128)(2,1)} %param.20) | copy-start | bytes 221188
  3.3 35.8 %all-to-all-start = ((bf16[64,40,128]{2,1,0:T(8,128)(2,1)}), bf16[64,40,128]{2,1,0:T(8,128)(2,1)S(1)}, u32[]{:S(2)}, u32[]{:S(2)}) async-start(bf16[64,40,128]{2,1,0:T(8,128)(2,1)} %shard_map.166), calls=%async_computation | async-start | bytes 1310720 | tf_op jit(solution)/shard_map/all_to_all | solution.py:27
  20.5 0.7 copy-start.8
  24.0 0.7 copy-start.9
  24.0 0.7 copy-start.10
  24.7 0.7 copy-start.11
  61.4 18.7 %copy-start.3 = (bf16[256,1536]{1,0:T(8,128)(2,1)S(1)}, bf16[256,1536]{1,0:T(8,128)(2,1)}, u32[]{:S(2)}) copy-start(bf16[256,1536]{1,0:T(8,128)(2,1)} %down_ref.1) | copy-start | bytes 2359300
  61.8 17.0 %copy-start.4 = (bf16[1,16,1536]{2,1,0:T(8,128)(2,1)S(1)}, bf16[1,16,1536]{2,1,0:T(8,128)(2,1)}, u32[]{:S(2)}) copy-start(bf16[1,16,1536]{2,1,0:T(8,128)(2,1)} %param.15) | copy-start | bytes 147460
  61.8 17.0 %copy-start.5 = (bf16[1536,16]{0,1:T(8,128)(2,1)S(1)}, bf16[1536,16]{0,1:T(8,128)(2,1)}, u32[]{:S(2)}) copy-start(bf16[1536,16]{0,1:T(8,128)(2,1)} %param.21) | copy-start | bytes 147460
  61.8 17.0 %copy-start.6 = (s32[1,16,2]{1,2,0:T(2,128)S(1)}, s32[1,16,2]{1,2,0:T(2,128)}, u32[]{:S(2)}) copy-start(s32[1,16,2]{1,2,0:T(2,128)} %param.22) | copy-start | bytes 388
  61.8 18.3 %copy-start.2 = (bf16[1536,256]{1,0:T(8,128)(2,1)S(1)}, bf16[1536,256]{1,0:T(8,128)(2,1)}, u32[]{:S(2)}) copy-start(bf16[1536,256]{1,0:T(8,128)(2,1)} %up_ref.1) | copy-start | bytes 2359300
  62.0 18.1 %copy-start.1 = (bf16[1536,256]{1,0:T(8,128)(2,1)S(1)}, bf16[1536,256]{1,0:T(8,128)(2,1)}, u32[]{:S(2)}) copy-start(bf16[1536,256]{1,0:T(8,128)(2,1)} %gate_ref.1) | copy-start | bytes 2359300

commit v10 on v9

--- a/solution.py
+++ b/solution.py
@@ -69,28 +69,7 @@
     w_blocks = w_blocks.reshape(blocks, w_rows * cols)
     w_blocks = jnp.pad(w_blocks, ((0, 0), (0, n_w * 128 - w_rows * cols))).reshape(blocks, n_w, 128)
 
-    n_kv = pair * span
-    kv = got[:, :n_kv].reshape(blocks, pair, span, 2 * HEAD_DIM).transpose(1, 0, 2, 3)
-    kv = kv.reshape(pair, blocks * span, 2 * HEAD_DIM)
-    sums = jnp.sum(got[:, n_kv:].astype(F32), axis=0)
-    query = (sums[:group] + sums[group + 2 :]).reshape(group, pair, HEAD_DIM).transpose(1, 0, 2).astype(BF16)
-    fresh = sums[group : group + 2].astype(BF16)
-    new_k, new_v = fresh[0].reshape(pair, HEAD_DIM), fresh[1].reshape(pair, HEAD_DIM)
-    scale = HEAD_DIM ** (-0.5)
-    scores = jnp.einsum("ihd,ipd->ihp", query, kv[:, :, :HEAD_DIM], preferred_element_type=F32) * scale
-    own = jnp.sum(query.astype(F32) * new_k.astype(F32)[:, None, :], axis=-1) * scale
-    lens = lax.dynamic_index_in_dim(lengths[0].reshape(pair, nz), z, 1, False)
-    valid = (jnp.arange(blocks * span)[None, :] < lens[:, None])[:, None, :]
-    top = jnp.maximum(jnp.max(jnp.where(valid, scores, -1e30), axis=-1), own)
-    probs = jnp.exp(jnp.where(valid, scores - top[..., None], -1e30))
-    own_prob = jnp.exp(own - top)
-    total = jnp.sum(probs, axis=-1) + own_prob
-    acc = jnp.einsum("ihp,ipd->ihd", probs.astype(BF16), kv[:, :, HEAD_DIM:], preferred_element_type=F32)
-    own_r = lax.reduce_precision(own_prob, 8, 7)
-    acc = acc + own_r[..., None] * new_v.astype(F32)[:, None, :]
-    attn = (acc / total[..., None]).astype(BF16)
     n_a = pair * group * HEAD_DIM // 128
-    attn = jnp.broadcast_to(attn.reshape(1, n_a, 128), (blocks, n_a, 128))
     half_rows = group_ids.shape[0] // 2
     stream = lax.axis_index("guide")
     weight_rows = request_weights(group_ids, weight_index, guidance_levels)
@@ -98,23 +77,23 @@
     weight_rows = jnp.broadcast_to(weight_rows[:, None], (half_rows, w_vocab.shape[1]))
     parts = width // 384
     expert = lax.div(block * w_gate.shape[1], EXPERT_UNITS)
-    where = jnp.stack([expert, lax.div(block, parts), lax.rem(block, parts)])
-    sent = jnp.concatenate([attn, w_blocks], axis=1)
-    sent, fresh, weight_rows, stream, where = lax.optimization_barrier((sent, fresh, weight_rows, stream, where))
+    where = jnp.stack([expert, lax.div(block, parts), lax.rem(block, parts), z])
+    where = jnp.concatenate([where, lengths.reshape(count)])
+    got, weight_rows, stream, where = lax.optimization_barrier((got, weight_rows, stream, where))
+    sent, fresh = attended(where, got, w_blocks)
     got = exchange(sent, BLK)
 
     w_cols = got[:, n_a:].reshape(blocks, n_w * 128)[:, : w_rows * cols].reshape(-1, cols)
-    attn = got[:, :n_a].reshape(ny, nz, pair, group * HEAD_DIM).transpose(2, 1, 0, 3).reshape(count, width_q)
+    attn = got[:, :n_a].reshape(ny, nz, group, pair, HEAD_DIM).transpose(3, 1, 0, 2, 4).reshape(count, width_q)
     part = jnp.dot(attn, w_cols, preferred_element_type=F32)
     own_lines = count * cols // 128
     part = part.reshape(count, own_lines, 8).transpose(1, 0, 2)
     high, low = halves(part.reshape(own_lines, 128))
-    got = exchange(to_all(jnp.concatenate([high, low, fresh], axis=0), blocks), BLK)
-    expert_in, share, mixed_piece, fresh_k, fresh_v = routed(
-        where, got, hidden[0], router.T, routes[0].T, width_k
-    )
-    sent = expert_payload(expert_in, share, w_gate, w_up, w_down)
-    got = exchange(sent.reshape(blocks, 2 * own_lines, 128), BLK)
+    got = exchange(to_all(jnp.concatenate([high, low], axis=0), blocks), BLK)
+    expert_in, share, mixed_piece = routed(where, got, hidden[0], router.T, routes[0].T)
+    sent = expert_payload(expert_in, share, fresh, w_gate, w_up, w_down)
+    got = exchange(sent.reshape(blocks, 2 * own_lines + 2, 128), BLK)
+    fresh = got
 
     piece = jnp.sum(got[:, :own_lines].astype(F32) + got[:, own_lines : 2 * own_lines].astype(F32), axis=0)
     piece = (mixed_piece + piece).astype(BF16)
@@ -125,32 +104,96 @@
     final_in = rms(outgoing).astype(BF16)
     stream_logits = jnp.dot(final_in, w_vocab, preferred_element_type=F32).astype(BF16)
     both = lax.all_gather(stream_logits, "guide", axis=0, tiled=False)
-    return last_outputs(stream, both, weight_rows, fresh_k, fresh_v)
-
-
-def last_kernel(stream_ref, both_ref, weight_ref, key_in, value_in, logits_ref, key_ref, value_ref):
+    return last_outputs(stream, both, weight_rows, fresh, count, width_k)
+
+
+def last_kernel(stream_ref, both_ref, weight_ref, fresh_ref, logits_ref, key_ref, value_ref, held):
     half_rows = logits_ref.shape[0]
     first = stream_ref[0] == 0
     cond = jnp.where(first, both_ref[0, :half_rows], both_ref[0, half_rows:]).astype(F32)
     uncond = jnp.where(first, both_ref[1, :half_rows], both_ref[1, half_rows:]).astype(F32)
     logits_ref[...] = uncond + weight_ref[...] * (cond - uncond)
-    key_ref[0] = key_in[...].astype(BF16)
-    value_ref[0] = value_in[...].astype(BF16)
-
-
-def last_outputs(stream, both, weight_rows, fresh_k, fresh_v):
-    shape = weight_rows.shape
+    held[...] = fresh_ref[:, 6:, :].astype(F32)
+    half = key_ref.shape[1] // 2
+    low_lane = lax.broadcasted_iota(jnp.int32, (half, 128), 1) < 64
+    for n, out_ref in ((0, key_ref), (1, value_ref)):
+        for v in range(out_ref.shape[2] // 128):
+            even = held[2 * half * v : 2 * half * v + half, n, :]
+            odd = held[2 * half * v + half : 2 * half * v + 2 * half, n, :]
+            first = jnp.where(low_lane, even, pltpu.roll(odd, 64, 1))
+            second = jnp.where(low_lane, pltpu.roll(even, 64, 1), odd)
+            both = jnp.concatenate([first, second], axis=0)
+            out_ref[0, :, 128 * v : 128 * v + 128] = both.astype(BF16)
+
+
+def last_outputs(stream, both, weight_rows, fresh, count, width_k):
     return pl.pallas_call(
         last_kernel,
         out_shape=(
-            jax.ShapeDtypeStruct(shape, F32),
-            jax.ShapeDtypeStruct((1,) + fresh_k.shape, BF16),
-            jax.ShapeDtypeStruct((1,) + fresh_v.shape, BF16),
+            jax.ShapeDtypeStruct(weight_rows.shape, F32),
+            jax.ShapeDtypeStruct((1, count, width_k), BF16),
+            jax.ShapeDtypeStruct((1, count, width_k), BF16),
         ),
-        in_specs=[SMEM] + [VMEM] * 4,
+        in_specs=[SMEM] + [VMEM] * 3,
         out_specs=(VMEM,) * 3,
+        scratch_shapes=[pltpu.VMEM((fresh.shape[0], 2, 128), F32)],
         compiler_params=pltpu.CompilerParams(vmem_limit_bytes=16 << 20),
-    )(stream.reshape(1), both, weight_rows, fresh_k, fresh_v)
+    )(stream.reshape(1), both, weight_rows, fresh)
+
+
+def attention_kernel(where_ref, got_ref, w_ref, out_ref, fresh_ref, lines):
+    blocks, rows, lanes = got_ref.shape
+    span = (rows - 8) // 2
+    sums = jnp.sum(got_ref[:, 2 * span :, :].astype(F32), axis=0)
+    fresh = sums[3:5].astype(BF16)
+    fresh_ref[...] = fresh
+    fresh = fresh.astype(F32)
+    group = HEADS // KV_HEADS
+    query = (sums[:group] + sums[group + 2 :]).astype(BF16).astype(F32)
+    query = jnp.concatenate([query, jnp.zeros((8 - group, lanes), F32)], axis=0)
+    low = lax.broadcasted_iota(jnp.int32, (8, lanes), 1) < HEAD_DIM
+    position = lax.broadcasted_iota(jnp.int32, (8, blocks * span), 1)
+    scale = HEAD_DIM ** (-0.5)
+    results = []
+    for i in range(2):
+        cache = got_ref[:, span * i : span * i + span, :].reshape(blocks * span, lanes)
+        here = jnp.where(low, query if i == 0 else pltpu.roll(query, HEAD_DIM, 1), 0.0)
+        flipped = jnp.concatenate([fresh, jnp.zeros((6, lanes), F32)], axis=0)
+        flipped = pltpu.roll(flipped, HEAD_DIM, 1)
+        new_k = fresh[0:1] if i == 0 else flipped[0:1]
+        new_v = flipped[1:2] if i == 0 else fresh[1:2]
+        scores = lax.dot_general(
+            here.astype(BF16), cache, (((1,), (1,)), ((), ())), preferred_element_type=F32
+        )
+        scores = scores * scale
+        own = jnp.sum(here * new_k, axis=1, keepdims=True) * scale
+        valid = position < where_ref[4 + where_ref[3] + 8 * i]
+        top = jnp.maximum(jnp.max(jnp.where(valid, scores, -1e30), axis=1, keepdims=True), own)
+        probs = jnp.exp(jnp.where(valid, scores - top, -1e30))
+        own_prob = jnp.exp(own - top)
+        total = jnp.sum(probs, axis=1, keepdims=True) + own_prob
+        acc = jnp.dot(probs.astype(BF16), cache, preferred_element_type=F32)
+        acc = acc + own_prob.astype(BF16).astype(F32) * new_v
+        results.append(acc / total)
+    attn = jnp.where(low, pltpu.roll(results[0], HEAD_DIM, 1), results[1])
+    lines[:, :group, :] = jnp.broadcast_to(attn[None, :group], (blocks, group, lanes))
+    lines[:, group:, :] = w_ref[...].astype(F32)
+    out_ref[...] = lines[...].astype(BF16)
+
+
+def attended(where, got, w_blocks):
+    blocks = got.shape[0]
+    return pl.pallas_call(
+        attention_kernel,
+        out_shape=(
+            jax.ShapeDtypeStruct((blocks, 8, 128), BF16),
+            jax.ShapeDtypeStruct((2, 128), BF16),
+        ),
+        in_specs=[SMEM] + [VMEM] * 2,
+        out_specs=(VMEM,) * 2,
+        scratch_shapes=[pltpu.VMEM((blocks, 8, 128), F32)],
+        compiler_params=pltpu.CompilerParams(vmem_limit_bytes=16 << 20),
+    )(where, got, w_blocks)
 
 
 def request_weights(group_ids, weight_index, guidance_levels):
@@ -163,8 +206,6 @@
 
 
 def to_all(lines, number):
-    fill = -lines.shape[0] % 8
-    lines = jnp.concatenate([lines, jnp.zeros((fill, lines.shape[1]), lines.dtype)], axis=0)
     return jnp.broadcast_to(lines[None], (number,) + lines.shape)
 
 
@@ -241,25 +282,13 @@
     in_ref,
     share_ref,
     piece_ref,
-    key_ref,
-    value_ref,
     held,
     lines,
     mixed_ref,
 ):
     count, width = hidden_ref.shape
     got = got_ref[...].astype(F32)
-    held[:, :3, :] = got[:, :3] + got[:, 3:6]
-    held[:, 3:, :] = got[:, 6:]
-    half = count // 2
-    low_lane = lax.broadcasted_iota(jnp.int32, (half, 128), 1) < 64
-    for n, out_ref in ((3, key_ref), (4, value_ref)):
-        for v in range(out_ref.shape[1] // 128):
-            even = held[2 * half * v : 2 * half * v + half, n, :]
-            odd = held[2 * half * v + half : 2 * half * v + 2 * half, n, :]
-            first = jnp.where(low_lane, even, pltpu.roll(odd, 64, 1))
-            second = jnp.where(low_lane, pltpu.roll(even, 64, 1), odd)
-            out_ref[:, 128 * v : 128 * v + 128] = jnp.concatenate([first, second], axis=0)
+    held[...] = got[:, :3] + got[:, 3:6]
     parts = width // 384
     blocks = [held[count * m : count * m + count, i, :] for m in range(parts) for i in range(3)]
     part = jnp.stack(blocks, axis=0)
@@ -298,7 +327,7 @@
     share_ref[...] = jnp.broadcast_to(share, share_ref.shape)
 
 
-def routed(where, got, hidden, router, routes, width_k):
+def routed(where, got, hidden, router, routes):
     count, width = hidden.shape
     parts = width // 384
     return pl.pallas_call(
@@ -307,13 +336,11 @@
             jax.ShapeDtypeStruct((count, width), BF16),
             jax.ShapeDtypeStruct((count, 128), F32),
             jax.ShapeDtypeStruct((3, 128), F32),
-            jax.ShapeDtypeStruct((count, width_k), F32),
-            jax.ShapeDtypeStruct((count, width_k), F32),
         ),
         in_specs=[SMEM] + [VMEM] * 4,
-        out_specs=(VMEM,) * 5,
+        out_specs=(VMEM,) * 3,
         scratch_shapes=[
-            pltpu.VMEM((got.shape[0], 5, 128), F32),
+            pltpu.VMEM((got.shape[0], 3, 128), F32),
             pltpu.VMEM((count, width), F32),
             pltpu.VMEM((count, parts, 3, 128), F32),
         ],
@@ -321,7 +348,7 @@
     )(where, got, hidden, router, routes)
 
 
-def expert_kernel(in_ref, share_ref, gate_ref, up_ref, down_ref, out_ref, lines):
+def expert_kernel(in_ref, share_ref, fresh_ref, gate_ref, up_ref, down_ref, out_ref, lines):
     expert_in = in_ref[...]
     width = expert_in.shape[1]
     gate = jnp.dot(expert_in, gate_ref[...], preferred_element_type=F32)
@@ -333,20 +360,22 @@
         high = line.astype(BF16).astype(F32)
         lines[:, n // 3, n % 3, :] = high
         lines[:, n // 3, 3 + n % 3, :] = line - high
+    fresh = fresh_ref[...].astype(F32)
+    lines[:, :, 6:, :] = jnp.broadcast_to(fresh[None, None], lines.shape[:2] + fresh.shape)
     out_ref[...] = lines[...].astype(BF16)
 
 
-def expert_payload(expert_in, share, w_gate, w_up, w_down):
+def expert_payload(expert_in, share, fresh, w_gate, w_up, w_down):
     count, width = expert_in.shape
-    shape = (count, width // 384, 6, 128)
+    shape = (count, width // 384, 8, 128)
     return pl.pallas_call(
         expert_kernel,
         out_shape=jax.ShapeDtypeStruct(shape, BF16),
-        in_specs=[VMEM] * 5,
+        in_specs=[VMEM] * 6,
         out_specs=VMEM,
         scratch_shapes=[pltpu.VMEM(shape, F32)],
         compiler_params=pltpu.CompilerParams(vmem_limit_bytes=16 << 20),
-    )(expert_in, share, w_gate, w_up, w_down)
+    )(expert_in, share, fresh, w_gate, w_up, w_down)
 
 
 def solution(mesh):

time: 127 us -> 127 us (level)
  other arithmetic: 2.51 us -> 0.56 us
  Pallas kernels: 5.1 us -> 6.51 us
    pallas_call x1 -> x2, Pallas kernels: 0.64 us -> 2.05 us  [the longest x1 1.31 us: attended(): pl.pallas_call(attention_kernel, out_shape=(jax.ShapeDtypeStruct((blocks,...]
  transfers between devices with their start and end apart: 1 -> 1, of which waited for: 1 -> 1; matrix products, arithmetic and copies ran while one was open for 3% -> 2% of each run, Pallas kernels for 0% -> 0%
where the time goes in v10:
time: 127 us
  blocking collectives  79.8 us (63%)
  starting transfers between devices  17.3 us (14%)
  waiting for transfers between devices  14.5 us (11%)
  local copies, waits for them, and re-layouts  7.02 us (6%)
  Pallas kernels  6.51 us (5%)
    all_to_all x4, blocking collectives, exchange(): return lax.all_to_all(value, axes, 0, 0, tiled=True)  72.8 us
    all_to_all x1, starting transfers between devices, exchange(): return lax.all_to_all(value, axes, 0, 0, tiled=True)  17.3 us
    all_to_all x1, waiting for transfers between devices, exchange(): return lax.all_to_all(value, axes, 0, 0, tiled=True)  14.5 us
    all_gather x1, blocking collectives, local(): both = lax.all_gather(stream_logits, 'guide', axis=0, tiled=False)  6.97 us
    pallas_call x1, Pallas kernels, first_payload(): pl.pallas_call(first_payload_kernel, out_shape=jax.ShapeDtypeStruct((bloc...  2.58 us
  transfers between devices with their start and end apart: 1, of which 1 were waited for; matrix products, arithmetic and copies ran while one was open for 2% of the time, Pallas kernels for 0%

profile of v10, /device:TPU:1, one launch (start us, length us, event | category | flops | bytes accessed | tf_op | source)
XLA Modules:
  0.0 127.0 jit_solution(13521194852364091125)
XLA Ops:
  0.7 2.6 %shard_map.166 = bf16[64,40,128]{2,1,0:T(8,128)(2,1)} custom-call(s32[1]{0:T(128)} %bitcast.block_ref, bf16[16,1536]{1,0:T(8,128)(2,1)} %bitcast.40, bf16[24,2560]{1,0:T(8,128)(2,1)} %w_hbm.1, bf16[16,16,512]{2,1,0:T(8,128)(2,1)} %bitcast.50, bf16[16,16,512]{2,1,0:T(8,128)(2,1)} %bitcast.51), custom_call_target="tpu_custom_call" | custom-call | tf_op jit(solution)/shard_map/pallas_call | solution.py:265
  3.3 17.3 %all-to-all-start = ((bf16[64,40,128]{2,1,0:T(8,128)(2,1)}), bf16[64,40,128]{2,1,0:T(8,128)(2,1)S(1)}, u32[]{:S(2)}, u32[]{:S(2)}) async-start(bf16[64,40,128]{2,1,0:T(8,128)(2,1)} %shard_map.166), calls=%async_computation | async-start | bytes 1310720 | tf_op jit(solution)/shard_map/all_to_all | solution.py:27
  20.6 0.2 copy.28
  20.8 1.1 copy.29
  21.9 0.3 reshape.69
  22.4 0.6 copy-done.9
  23.1 0.2 select_reduce_fusion.1
  23.2 0.5 copy-done.11
  23.9 0.7 copy-done.8
  24.6 14.5 %all-to-all-done.got_ref = bf16[64,40,128]{2,1,0:T(8,128)(2,1)S(1)} async-done(((bf16[64,40,128]{2,1,0:T(8,128)(2,1)}), bf16[64,40,128]{2,1,0:T(8,128)(2,1)S(1)}, u32[]{:S(2)}, u32[]{:S(2)}) %all-to-all-start) | async-done | bytes 655392 | tf_op jit(solution)/shard_map/all_to_all | solution.py:27
  39.2 1.3 %shard_map.167 = (bf16[64,8,128]{2,1,0:T(8,128)(2,1)S(1)}, bf16[2,128]{1,0:T(2,128)(2,1)S(1)}) custom-call(s32[20]{0:T(128)S(1)} %concatenate.9.where_ref, bf16[64,40,128]{2,1,0:T(8,128)(2,1)S(1)} %all-to-all-done.got_ref, bf16[64,5,128]{2,1,0:T(8,128)(2,1)S(1)} %copy.35.w_ref), custom_call_target="tpu_custom_call" | custom-call | tf_op jit(solution)/shard_map/pallas_call | solution.py:186
  40.5 20.1 %all_to_all.25 = bf16[64,8,128]{2,1,0:T(8,128)(2,1)S(1)} all-to-all(bf16[64,8,128]{2,1,0:T(8,128)(2,1)S(1)} %get-tuple-element.15), channel_id=1, replica_groups=mesh['guide'=2,'y'=8,'z'=8,'batch'=4] {'y','z'}, dimensions={0} | all-to-all | bytes 262144 | tf_op jit(solution)/shard_map/all_to_all | solution.py:27
  61.0 0.2 reshape.82
  61.2 1.1 reshape.74
  62.2 1.1 copy.33
  63.8 15.5 %all_to_all.26.got_ref = bf16[64,6,128]{2,1,0:T(8,128)(2,1)S(1)} all-to-all(bf16[64,6,128]{2,1,0:T(8,128)(2,1)S(1)} %broadcast_in_dim.7), channel_id=1, replica_groups=mesh['guide'=2,'y'=8,'z'=8,'batch'=4] {'y','z'}, dimensions={0} | all-to-all | bytes 196608 | tf_op jit(solution)/shard_map/all_to_all | solution.py:27
  79.3 1.2 shard_map.168
  80.6 0.6 shard_map.169
  81.2 15.4 %all_to_all.27.fresh_ref = bf16[64,8,128]{2,1,0:T(8,128)(2,1)S(1)} all-to-all(bf16[64,8,128]{2,1,0:T(8,128)(2,1)S(1)} %bitcast.38), channel_id=1, replica_groups=mesh['guide'=2,'y'=8,'z'=8,'batch'=4] {'y','z'}, dimensions={0} | all-to-all | bytes 262144 | tf_op jit(solution)/shard_map/all_to_all | solution.py:27
  96.8 21.7 %all_to_all.28 = bf16[256,4,128]{2,1,0:T(4,128)(2,1)S(1)} all-to-all(bf16[256,4,128]{2,1,0:T(4,128)(2,1)S(1)} %broadcast_in_dim.8), channel_id=1, replica_groups=mesh['guide'=2,'y'=8,'z'=8,'batch'=4] {'batch','y','z'}, dimensions={0} | all-to-all | bytes 524288 | tf_op jit(solution)/shard_map/all_to_all | solution.py:27
  118.6 0.2 reshape.80
  118.9 0.3 convolution_convert_fusion
  119.2 7.0 %all-gather = bf16[128,256]{1,0:T(8,128)(2,1)S(1)} all-gather(bf16[64,256]{1,0:T(8,128)(2,1)S(1)} %convolution_convert_fusion), channel_id=2, replica_groups=mesh['guide'=2,'y'=8,'z'=8,'batch'=4] {'guide'}, dimensions={0}, use_global_device_ids=true | all-gather | bytes 98304 | tf_op jit(solution)/shard_map/all_gather | solution.py:106
  126.2 0.7 shard_map.170
  (46 shorter events, 1.6 us)
Async XLA Ops:
  0.6 118.3 %copy-start = (bf16[1536,256]{1,0:T(8,128)(2,1)S(1)}, bf16[1536,256]{1,0:T(8,128)(2,1)}, u32[]{:S(2)}) copy-start(bf16[1536,256]{1,0:T(8,128)(2,1)} %param.26) | copy-start | bytes 2359300
  3.2 17.3 %copy-start.7 = (bf16[24,1536]{1,0:T(8,128)(2,1)S(1)}, bf16[24,1536]{1,0:T(8,128)(2,1)}, u32[]{:S(2)}) copy-start(bf16[24,1536]{1,0:T(8,128)(2,1)} %param.20) | copy-start | bytes 221188
  3.3 35.8 %all-to-all-start = ((bf16[64,40,128]{2,1,0:T(8,128)(2,1)}), bf16[64,40,128]{2,1,0:T(8,128)(2,1)S(1)}, u32[]{:S(2)}, u32[]{:S(2)}) async-start(bf16[64,40,128]{2,1,0:T(8,128)(2,1)} %shard_map.166), calls=%async_computation | async-start | bytes 1310720 | tf_op jit(solution)/shard_map/all_to_all | solution.py:27
  22.4 0.7 copy-start.9
  22.4 0.7 copy-start.10
  23.1 0.7 copy-start.11
  23.9 0.7 copy-start.8
  60.7 19.8 %copy-start.3 = (bf16[256,1536]{1,0:T(8,128)(2,1)S(1)}, bf16[256,1536]{1,0:T(8,128)(2,1)}, u32[]{:S(2)}) copy-start(bf16[256,1536]{1,0:T(8,128)(2,1)} %down_ref.1) | copy-start | bytes 2359300
  60.9 18.4 %copy-start.4 = (bf16[1,16,1536]{2,1,0:T(8,128)(2,1)S(1)}, bf16[1,16,1536]{2,1,0:T(8,128)(2,1)}, u32[]{:S(2)}) copy-start(bf16[1,16,1536]{2,1,0:T(8,128)(2,1)} %param.15) | copy-start | bytes 147460
  60.9 18.3 %copy-start.5 = (bf16[1536,16]{0,1:T(8,128)(2,1)S(1)}, bf16[1536,16]{0,1:T(8,128)(2,1)}, u32[]{:S(2)}) copy-start(bf16[1536,16]{0,1:T(8,128)(2,1)} %param.21) | copy-start | bytes 147460
  60.9 18.3 %copy-start.6 = (s32[1,16,2]{1,2,0:T(2,128)S(1)}, s32[1,16,2]{1,2,0:T(2,128)}, u32[]{:S(2)}) copy-start(s32[1,16,2]{1,2,0:T(2,128)} %param.22) | copy-start | bytes 388
  61.1 19.4 %copy-start.1 = (bf16[1536,256]{1,0:T(8,128)(2,1)S(1)}, bf16[1536,256]{1,0:T(8,128)(2,1)}, u32[]{:S(2)}) copy-start(bf16[1536,256]{1,0:T(8,128)(2,1)} %gate_ref.1) | copy-start | bytes 2359300
  61.1 19.4 %copy-start.2 = (bf16[1536,256]{1,0:T(8,128)(2,1)S(1)}, bf16[1536,256]{1,0:T(8,128)(2,1)}, u32[]{:S(2)}) copy-start(bf16[1536,256]{1,0:T(8,128)(2,1)} %up_ref.1) | copy-start | bytes 2359300

commit v11 on v10

--- a/solution.py
+++ b/solution.py
@@ -64,12 +64,10 @@
     got = exchange(sent, BLK)
     cols = width // blocks
     w_rows = w_out.shape[0]
-    n_w = -(-w_rows * cols // 128)
-    w_blocks = w_out.reshape(w_rows, blocks // count, cols // 8, count, 8).transpose(1, 3, 0, 2, 4)
-    w_blocks = w_blocks.reshape(blocks, w_rows * cols)
-    w_blocks = jnp.pad(w_blocks, ((0, 0), (0, n_w * 128 - w_rows * cols))).reshape(blocks, n_w, 128)
-
-    n_a = pair * group * HEAD_DIM // 128
+    w_blocks = jnp.pad(w_out, ((0, 25 - w_rows), (0, 0)))
+    w_blocks = w_blocks.reshape(5, 5, blocks // count, cols // 8, count, 8).transpose(2, 4, 1, 0, 3, 5)
+    w_blocks = jnp.pad(w_blocks.reshape(blocks, 5, 5 * cols), ((0, 0), (0, 0), (0, 128 - 5 * cols)))
+
     half_rows = group_ids.shape[0] // 2
     stream = lax.axis_index("guide")
     weight_rows = request_weights(group_ids, weight_index, guidance_levels)
@@ -83,13 +81,9 @@
     sent, fresh = attended(where, got, w_blocks)
     got = exchange(sent, BLK)
 
-    w_cols = got[:, n_a:].reshape(blocks, n_w * 128)[:, : w_rows * cols].reshape(-1, cols)
-    attn = got[:, :n_a].reshape(ny, nz, group, pair, HEAD_DIM).transpose(3, 1, 0, 2, 4).reshape(count, width_q)
-    part = jnp.dot(attn, w_cols, preferred_element_type=F32)
     own_lines = count * cols // 128
-    part = part.reshape(count, own_lines, 8).transpose(1, 0, 2)
-    high, low = halves(part.reshape(own_lines, 128))
-    got = exchange(to_all(jnp.concatenate([high, low], axis=0), blocks), BLK)
+    got = exchange(projected(got, count, w_rows, width_q), BLK)
+
     expert_in, share, mixed_piece = routed(where, got, hidden[0], router.T, routes[0].T)
     sent = expert_payload(expert_in, share, fresh, w_gate, w_up, w_down)
     got = exchange(sent.reshape(blocks, 2 * own_lines + 2, 128), BLK)
@@ -139,6 +133,56 @@
         scratch_shapes=[pltpu.VMEM((fresh.shape[0], 2, 128), F32)],
         compiler_params=pltpu.CompilerParams(vmem_limit_bytes=16 << 20),
     )(stream.reshape(1), both, weight_rows, fresh)
+
+
+def project_kernel(got_ref, out_ref, held, rows_ref, attn_ref):
+    held[...] = got_ref[...].astype(F32)
+    rows = rows_ref.shape[1]
+    w = held[:, 3:, :]
+    for g in range(5):
+        here = min(5, rows - 5 * g)
+        turned = w if g == 0 else pltpu.roll(w, 128 - 24 * g, 2)
+        rows_ref[:, 5 * g : 5 * g + here, :] = turned[:, :here, :]
+    half = attn_ref.shape[0] // 2
+    low = lax.broadcasted_iota(jnp.int32, (half, 128), 1) < 64
+    for v in range(attn_ref.shape[1] // 128):
+        (y, h), (y2, h2) = divmod(2 * v, 3), divmod(2 * v + 1, 3)
+        even = held[8 * y : 8 * y + 8, h, :]
+        odd = held[8 * y2 : 8 * y2 + 8, h2, :]
+        attn_ref[:half, 128 * v : 128 * v + 128] = jnp.where(low, even, pltpu.roll(odd, 64, 1))
+        attn_ref[half:, 128 * v : 128 * v + 128] = jnp.where(low, pltpu.roll(even, 64, 1), odd)
+    w = rows_ref[...].reshape(-1, 128).astype(BF16)
+    part = jnp.dot(attn_ref[...].astype(BF16), w, preferred_element_type=F32)
+    row = lax.broadcasted_iota(jnp.int32, part.shape, 0)
+    lane = lax.broadcasted_iota(jnp.int32, part.shape, 1)
+    highs, lows = [], []
+    for i in range(3):
+        group = part if i == 0 else pltpu.roll(part, 128 - 8 * i, 1)
+        group = jnp.where(lane < 8, group, 0.0)
+        for shift in (8, 16, 32, 64):
+            group = group + pltpu.roll(group, shift, 1)
+        line = jnp.sum(jnp.where(lane // 8 == row, group, 0.0), axis=0, keepdims=True)
+        high = line.astype(BF16).astype(F32)
+        highs.append(high)
+        lows.append(line - high)
+    lines = jnp.concatenate(highs + lows, axis=0)
+    out_ref[...] = jnp.broadcast_to(lines[None], out_ref.shape).astype(BF16)
+
+
+def projected(got, count, w_rows, width_q):
+    blocks = got.shape[0]
+    return pl.pallas_call(
+        project_kernel,
+        out_shape=jax.ShapeDtypeStruct((blocks, 6, 128), BF16),
+        in_specs=[VMEM],
+        out_specs=VMEM,
+        scratch_shapes=[
+            pltpu.VMEM((blocks, 8, 128), F32),
+            pltpu.VMEM((blocks, w_rows, 128), F32),
+            pltpu.VMEM((count, width_q), F32),
+        ],
+        compiler_params=pltpu.CompilerParams(vmem_limit_bytes=16 << 20),
+    )(got)
 
 
 def attention_kernel(where_ref, got_ref, w_ref, out_ref, fresh_ref, lines):
@@ -203,10 +247,6 @@
     level_pick = (weight_index[:, None] == jnp.arange(level_count)[None, :]).astype(F32)
     group_weight = jnp.sum(level_pick * guidance_levels[None, :], axis=1)
     return jnp.sum(in_group * group_weight[None, :], axis=1)
-
-
-def to_all(lines, number):
-    return jnp.broadcast_to(lines[None], (number,) + lines.shape)
 
 
 def first_payload_kernel(

time: 127 us -> 125 us (0.984)
  local copies, waits for them, and re-layouts: 7.02 us -> 5.45 us
  waiting for transfers between devices: 14.5 us -> 13.1 us
    unnamed x26 -> x24, local copies, waits for them, and re-layouts: 2.07 us -> 0.07 us
    all_to_all x1, waiting for transfers between devices: 14.5 us -> 13.1 us  [exchange(): return lax.all_to_all(value, axes, 0, 0, tiled=True)]
    reshape x6 -> x3, local copies, waits for them, and re-layouts: 1.94 us -> 3.07 us  [the longest x2 1.63 us: local(): w_blocks.reshape(blocks, 5, 5 * cols)]
  transfers between devices with their start and end apart: 1 -> 1, of which waited for: 1 -> 1; matrix products, arithmetic and copies ran while one was open for 2% -> 4% of each run, Pallas kernels for 0% -> 0%
where the time goes in v11:
time: 125 us; the launch traced here: 124 us
  blocking collectives  79.8 us (64%)
  starting transfers between devices  17.1 us (14%)
  waiting for transfers between devices  13.1 us (10%)
  Pallas kernels  7.34 us (6%)
  local copies, waits for them, and re-layouts  5.45 us (4%)
    all_to_all x4, blocking collectives, exchange(): return lax.all_to_all(value, axes, 0, 0, tiled=True)  72.8 us
    all_to_all x1, starting transfers between devices, exchange(): return lax.all_to_all(value, axes, 0, 0, tiled=True)  17.1 us
    all_to_all x1, waiting for transfers between devices, exchange(): return lax.all_to_all(value, axes, 0, 0, tiled=True)  13.1 us
    all_gather x1, blocking collectives, local(): both = lax.all_gather(stream_logits, 'guide', axis=0, tiled=False)  6.97 us
    pallas_call x1, Pallas kernels, first_payload(): pl.pallas_call(first_payload_kernel, out_shape=jax.ShapeDtypeStruct((bloc...  2.61 us
  transfers between devices with their start and end apart: 1, of which 1 were waited for; matrix products, arithmetic and copies ran while one was open for 4% of the time, Pallas kernels for 0%

profile of v11, /device:TPU:1, one launch (start us, length us, event | category | flops | bytes accessed | tf_op | source)
XLA Modules:
  0.0 124.5 jit_solution(18151794660871479562)
XLA Ops:
  0.7 2.6 %shard_map.166 = bf16[64,40,128]{2,1,0:T(8,128)(2,1)} custom-call(s32[1]{0:T(128)} %bitcast.block_ref, bf16[16,1536]{1,0:T(8,128)(2,1)} %bitcast.22, bf16[24,2560]{1,0:T(8,128)(2,1)} %w_hbm.1, bf16[16,16,512]{2,1,0:T(8,128)(2,1)} %bitcast.27, bf16[16,16,512]{2,1,0:T(8,128)(2,1)} %bitcast.28), custom_call_target="tpu_custom_call" | custom-call | tf_op jit(solution)/shard_map/pallas_call | solution.py:305
  3.3 17.1 %all-to-all-start = ((bf16[64,40,128]{2,1,0:T(8,128)(2,1)}), bf16[64,40,128]{2,1,0:T(8,128)(2,1)S(1)}, u32[]{:S(2)}, u32[]{:S(2)}) async-start(bf16[64,40,128]{2,1,0:T(8,128)(2,1)} %shard_map.166), calls=%async_computation | async-start | bytes 1310720 | tf_op jit(solution)/shard_map/all_to_all | solution.py:27
  20.5 1.4 %reshape.47 = bf16[5,5,4,3,16,8]{5,4,3,2,1,0:T(8,128)(2,1)S(1)} reshape(bf16[25,1536]{1,0:T(8,128)(2,1)S(1)} %pad.9) | data formatting | bytes 153600 | tf_op jit(solution)/shard_map/reshape | solution.py:68
  22.0 1.7 %copy.21 = bf16[4,16,5,5,3,8]{1,0,5,4,3,2:T(4,128)(2,1)} copy(bf16[4,16,5,5,3,8]{5,1,4,0,2,3:T(8,128)(2,1)S(1)} %bitcast.26) | data formatting | bytes 153600 | tf_op jit(solution)/shard_map/transpose | solution.py:68
  23.7 1.5 %reshape.48 = bf16[64,5,120]{0,2,1:T(8,128)(2,1)S(1)} reshape(bf16[4,16,5,5,3,8]{1,0,5,4,3,2:T(4,128)(2,1)} %copy.21) | data formatting | bytes 153600 | tf_op jit(solution)/shard_map/reshape | solution.py:69
  25.2 0.2 copy.22
  25.5 0.2 select_reduce_fusion.1
  25.7 0.1 select_reduce_fusion
  25.8 0.1 concatenate.6.where_ref
  25.9 13.1 %all-to-all-done.got_ref = bf16[64,40,128]{2,1,0:T(8,128)(2,1)S(1)} async-done(((bf16[64,40,128]{2,1,0:T(8,128)(2,1)}), bf16[64,40,128]{2,1,0:T(8,128)(2,1)S(1)}, u32[]{:S(2)}, u32[]{:S(2)}) %all-to-all-start) | async-done | bytes 655392 | tf_op jit(solution)/shard_map/all_to_all | solution.py:27
  39.0 1.3 %shard_map.167 = (bf16[64,8,128]{2,1,0:T(8,128)(2,1)S(1)}, bf16[2,128]{1,0:T(2,128)(2,1)S(1)}) custom-call(s32[20]{0:T(128)S(1)} %concatenate.6.where_ref, bf16[64,40,128]{2,1,0:T(8,128)(2,1)S(1)} %all-to-all-done.got_ref, bf16[64,5,128]{2,1,0:T(8,128)(2,1)S(1)} %pad.10.w_ref), custom_call_target="tpu_custom_call" | custom-call | tf_op jit(solution)/shard_map/pallas_call | solution.py:230
  40.4 20.1 %all_to_all.25.got_ref = bf16[64,8,128]{2,1,0:T(8,128)(2,1)S(1)} all-to-all(bf16[64,8,128]{2,1,0:T(8,128)(2,1)S(1)} %get-tuple-element.15), channel_id=1, replica_groups=mesh['guide'=2,'y'=8,'z'=8,'batch'=4] {'y','z'}, dimensions={0} | all-to-all | bytes 262144 | tf_op jit(solution)/shard_map/all_to_all | solution.py:27
  60.5 0.8 shard_map.168
  61.3 15.5 %all_to_all.26.got_ref = bf16[64,6,128]{2,1,0:T(8,128)(2,1)S(1)} all-to-all(bf16[64,6,128]{2,1,0:T(8,128)(2,1)S(1)} %shard_map.168), channel_id=1, replica_groups=mesh['guide'=2,'y'=8,'z'=8,'batch'=4] {'y','z'}, dimensions={0} | all-to-all | bytes 196608 | tf_op jit(solution)/shard_map/all_to_all | solution.py:27
  76.8 1.2 %shard_map.169 = (bf16[16,1536]{1,0:T(8,128)(2,1)S(1)}, f32[16,128]{1,0:T(8,128)S(1)}, f32[3,128]{1,0:T(4,128)S(1)}) custom-call(s32[20]{0:T(128)S(1)} %concatenate.6.where_ref, bf16[64,6,128]{2,1,0:T(8,128)(2,1)S(1)} %all_to_all.26.got_ref, bf16[16,1536]{1,0:T(8,128)(2,1)S(1)} %bitcast.23, bf16[16,1536]{1,0:T(8,128)(2,1)S(1)} %bitcast.24, s32[2,16]{1,0:T(2,128)S(1)} %bitcast.25), custom_call_target="tpu_custom_call" | custom-call | tf_op jit(solution)/shard_map/pallas_call | solution.py:373
  78.1 0.6 shard_map.170
  78.7 15.4 %all_to_all.27.fresh_ref = bf16[64,8,128]{2,1,0:T(8,128)(2,1)S(1)} all-to-all(bf16[64,8,128]{2,1,0:T(8,128)(2,1)S(1)} %bitcast.20), channel_id=1, replica_groups=mesh['guide'=2,'y'=8,'z'=8,'batch'=4] {'y','z'}, dimensions={0} | all-to-all | bytes 262144 | tf_op jit(solution)/shard_map/all_to_all | solution.py:27
  94.1 0.1 add_reduce_fusion
  94.3 21.7 %all_to_all.28 = bf16[256,4,128]{2,1,0:T(4,128)(2,1)S(1)} all-to-all(bf16[256,4,128]{2,1,0:T(4,128)(2,1)S(1)} %broadcast_in_dim.5), channel_id=1, replica_groups=mesh['guide'=2,'y'=8,'z'=8,'batch'=4] {'batch','y','z'}, dimensions={0} | all-to-all | bytes 524288 | tf_op jit(solution)/shard_map/all_to_all | solution.py:27
  116.1 0.2 reshape.53
  116.3 0.1 multiply_reduce_fusion
  116.5 0.3 convolution_convert_fusion
  116.8 7.0 %all-gather = bf16[128,256]{1,0:T(8,128)(2,1)S(1)} all-gather(bf16[64,256]{1,0:T(8,128)(2,1)S(1)} %convolution_convert_fusion), channel_id=2, replica_groups=mesh['guide'=2,'y'=8,'z'=8,'batch'=4] {'guide'}, dimensions={0}, use_global_device_ids=true | all-gather | bytes 98304 | tf_op jit(solution)/shard_map/all_gather | solution.py:100
  123.8 0.7 shard_map.171
  (33 shorter events, 0.4 us)
Async XLA Ops:
  0.6 115.8 %copy-start = (bf16[1536,256]{1,0:T(8,128)(2,1)S(1)}, bf16[1536,256]{1,0:T(8,128)(2,1)}, u32[]{:S(2)}) copy-start(bf16[1536,256]{1,0:T(8,128)(2,1)} %param.26) | copy-start | bytes 2359300
  0.7 19.8 %copy-start.7 = (bf16[24,1536]{1,0:T(8,128)(2,1)S(1)}, bf16[24,1536]{1,0:T(8,128)(2,1)}, u32[]{:S(2)}) copy-start(bf16[24,1536]{1,0:T(8,128)(2,1)} %param.20) | copy-start | bytes 221188
  3.3 35.7 %all-to-all-start = ((bf16[64,40,128]{2,1,0:T(8,128)(2,1)}), bf16[64,40,128]{2,1,0:T(8,128)(2,1)S(1)}, u32[]{:S(2)}, u32[]{:S(2)}) async-start(bf16[64,40,128]{2,1,0:T(8,128)(2,1)} %shard_map.166), calls=%async_computation | async-start | bytes 1310720 | tf_op jit(solution)/shard_map/all_to_all | solution.py:27
  21.9 3.5 %copy-start.9 = (f32[8]{0:T(128)S(1)}, f32[8]{0:T(128)}, u32[]{:S(2)}) copy-start(f32[8]{0:T(128)} %param.29) | copy-start | bytes 100
  21.9 3.5 %copy-start.10 = (s32[8]{0:T(128)S(1)}, s32[8]{0:T(128)}, u32[]{:S(2)}) copy-start(s32[8]{0:T(128)} %param.28) | copy-start | bytes 100
  21.9 3.7 %copy-start.11 = (s32[64]{0:T(128)S(1)}, s32[64]{0:T(128)}, u32[]{:S(2)}) copy-start(s32[64]{0:T(128)} %param.27) | copy-start | bytes 772
  22.0 3.9 %copy-start.8 = (s32[1,16]{1,0:T(1,128)S(1)}, s32[1,16]{1,0:T(1,128)}, u32[]{:S(2)}) copy-start(s32[1,16]{1,0:T(1,128)} %param.19) | copy-start | bytes 196
  23.7 53.1 %copy-start.5 = (bf16[1536,16]{0,1:T(8,128)(2,1)S(1)}, bf16[1536,16]{0,1:T(8,128)(2,1)}, u32[]{:S(2)}) copy-start(bf16[1536,16]{0,1:T(8,128)(2,1)} %param.21) | copy-start | bytes 147460
  25.2 51.6 %copy-start.4 = (bf16[1,16,1536]{2,1,0:T(8,128)(2,1)S(1)}, bf16[1,16,1536]{2,1,0:T(8,128)(2,1)}, u32[]{:S(2)}) copy-start(bf16[1,16,1536]{2,1,0:T(8,128)(2,1)} %param.15) | copy-start | bytes 147460
  25.2 51.6 %copy-start.6 = (s32[1,16,2]{1,2,0:T(2,128)S(1)}, s32[1,16,2]{1,2,0:T(2,128)}, u32[]{:S(2)}) copy-start(s32[1,16,2]{1,2,0:T(2,128)} %param.22) | copy-start | bytes 388
  25.2 52.9 %copy-start.1 = (bf16[1536,256]{1,0:T(8,128)(2,1)S(1)}, bf16[1536,256]{1,0:T(8,128)(2,1)}, u32[]{:S(2)}) copy-start(bf16[1536,256]{1,0:T(8,128)(2,1)} %gate_ref.1) | copy-start | bytes 2359300
  25.2 52.8 %copy-start.2 = (bf16[1536,256]{1,0:T(8,128)(2,1)S(1)}, bf16[1536,256]{1,0:T(8,128)(2,1)}, u32[]{:S(2)}) copy-start(bf16[1536,256]{1,0:T(8,128)(2,1)} %up_ref.1) | copy-start | bytes 2359300
  39.0 39.1 %copy-start.3 = (bf16[256,1536]{1,0:T(8,128)(2,1)S(1)}, bf16[256,1536]{1,0:T(8,128)(2,1)}, u32[]{:S(2)}) copy-start(bf16[256,1536]{1,0:T(8,128)(2,1)} %down_ref.1) | copy-start | bytes 2359300

commit v12 on v11

--- a/solution.py
+++ b/solution.py
@@ -250,7 +250,20 @@
 
 
 def first_payload_kernel(
-    block_ref, hidden_hbm, w_hbm, key_hbm, value_hbm, out_ref, hidden_ref, w_ref, key_ref, value_ref, lines, sems
+    block_ref,
+    hidden_hbm,
+    w_hbm,
+    key_hbm,
+    value_hbm,
+    out_hbm,
+    hidden_ref,
+    w_ref,
+    key_ref,
+    value_ref,
+    lines,
+    out_ref,
+    sems,
+    out_sems,
 ):
     copies = [
         pltpu.make_async_copy(source, target, sems.at[n])
@@ -289,6 +302,7 @@
     out_ref[:, 2 * span :, :] = lines[...].astype(BF16)
     copies[2].wait()
     copies[3].wait()
+    writes = []
     low_lane = lax.broadcasted_iota(jnp.int32, (count, span, 128), 2) < 64
     for m in range(width_k // 128):
         keys = key_ref[:, :, 128 * m : 128 * m + 128].astype(F32)
@@ -298,6 +312,11 @@
         for y, pair in ((2 * m, even), (2 * m + 1, odd)):
             for i in range(count // nz):
                 out_ref[nz * y : nz * y + nz, span * i : span * i + span, :] = pair[nz * i : nz * i + nz]
+        piece = pl.ds(2 * nz * m, 2 * nz)
+        writes.append(pltpu.make_async_copy(out_ref.at[piece], out_hbm.at[piece], out_sems.at[m]))
+        writes[-1].start()
+    for write in writes:
+        write.wait()
 
 
 def first_payload(block, hidden, w_qkv, keys, values, blocks):
@@ -306,9 +325,14 @@
         first_payload_kernel,
         out_shape=jax.ShapeDtypeStruct((blocks, 2 * span + 8, 128), BF16),
         in_specs=[SMEM] + [HBM] * 4,
-        out_specs=VMEM,
+        out_specs=HBM,
         scratch_shapes=[pltpu.VMEM(a.shape, a.dtype) for a in (hidden, w_qkv, keys, values)]
-        + [pltpu.VMEM((blocks, 8, 128), F32), pltpu.SemaphoreType.DMA((4,))],
+        + [
+            pltpu.VMEM((blocks, 8, 128), F32),
+            pltpu.VMEM((blocks, 2 * span + 8, 128), BF16),
+            pltpu.SemaphoreType.DMA((4,)),
+            pltpu.SemaphoreType.DMA((keys.shape[2] // 128,)),
+        ],
         compiler_params=pltpu.CompilerParams(vmem_limit_bytes=60 << 20),
     )(block.reshape(1), hidden, w_qkv, keys, values)
 

time: 125 us -> 125 us (level)
  no operation moved by 1% of the time
where the time goes in v12:
time: 125 us; the launch traced here: 124 us
  blocking collectives  79.8 us (64%)
  starting transfers between devices  17.1 us (14%)
  waiting for transfers between devices  13.1 us (10%)
  Pallas kernels  7.27 us (6%)
  local copies, waits for them, and re-layouts  5.45 us (4%)
    all_to_all x4, blocking collectives, exchange(): return lax.all_to_all(value, axes, 0, 0, tiled=True)  72.8 us
    all_to_all x1, starting transfers between devices, exchange(): return lax.all_to_all(value, axes, 0, 0, tiled=True)  17.1 us
    all_to_all x1, waiting for transfers between devices, exchange(): return lax.all_to_all(value, axes, 0, 0, tiled=True)  13.1 us
    all_gather x1, blocking collectives, local(): both = lax.all_gather(stream_logits, 'guide', axis=0, tiled=False)  6.97 us
    pallas_call x1, Pallas kernels, first_payload(): pl.pallas_call(first_payload_kernel, out_shape=jax.ShapeDtypeStruct((bloc...  2.54 us
  transfers between devices with their start and end apart: 1, of which 1 were waited for; matrix products, arithmetic and copies ran while one was open for 4% of the time, Pallas kernels for 0%

profile of v12, /device:TPU:1, one launch (start us, length us, event | category | flops | bytes accessed | tf_op | source)
XLA Modules:
  0.0 124.4 jit_solution(12808403040170890731)
XLA Ops:
  0.7 2.5 %shard_map.166 = bf16[64,40,128]{2,1,0:T(8,128)(2,1)} custom-call(s32[1]{0:T(128)} %bitcast.block_ref, bf16[16,1536]{1,0:T(8,128)(2,1)} %bitcast.22, bf16[24,2560]{1,0:T(8,128)(2,1)} %w_hbm.1, bf16[16,16,512]{2,1,0:T(8,128)(2,1)} %bitcast.27, bf16[16,16,512]{2,1,0:T(8,128)(2,1)} %bitcast.28), custom_call_target="tpu_custom_call" | custom-call | tf_op jit(solution)/shard_map/pallas_call | solution.py:324
  3.2 17.1 %all-to-all-start = ((bf16[64,40,128]{2,1,0:T(8,128)(2,1)}), bf16[64,40,128]{2,1,0:T(8,128)(2,1)S(1)}, u32[]{:S(2)}, u32[]{:S(2)}) async-start(bf16[64,40,128]{2,1,0:T(8,128)(2,1)} %shard_map.166), calls=%async_computation | async-start | bytes 1310720 | tf_op jit(solution)/shard_map/all_to_all | solution.py:27
  20.4 1.4 %reshape.47 = bf16[5,5,4,3,16,8]{5,4,3,2,1,0:T(8,128)(2,1)S(1)} reshape(bf16[25,1536]{1,0:T(8,128)(2,1)S(1)} %pad.9) | data formatting | bytes 153600 | tf_op jit(solution)/shard_map/reshape | solution.py:68
  21.9 1.7 %copy.21 = bf16[4,16,5,5,3,8]{1,0,5,4,3,2:T(4,128)(2,1)} copy(bf16[4,16,5,5,3,8]{5,1,4,0,2,3:T(8,128)(2,1)S(1)} %bitcast.26) | data formatting | bytes 153600 | tf_op jit(solution)/shard_map/transpose | solution.py:68
  23.6 1.5 %reshape.48 = bf16[64,5,120]{0,2,1:T(8,128)(2,1)S(1)} reshape(bf16[4,16,5,5,3,8]{1,0,5,4,3,2:T(4,128)(2,1)} %copy.21) | data formatting | bytes 153600 | tf_op jit(solution)/shard_map/reshape | solution.py:69
  25.2 0.2 copy.22
  25.4 0.2 select_reduce_fusion.1
  25.6 0.1 select_reduce_fusion
  25.8 0.1 concatenate.6.where_ref
  25.8 13.1 %all-to-all-done.got_ref = bf16[64,40,128]{2,1,0:T(8,128)(2,1)S(1)} async-done(((bf16[64,40,128]{2,1,0:T(8,128)(2,1)}), bf16[64,40,128]{2,1,0:T(8,128)(2,1)S(1)}, u32[]{:S(2)}, u32[]{:S(2)}) %all-to-all-start) | async-done | bytes 655392 | tf_op jit(solution)/shard_map/all_to_all | solution.py:27
  39.0 1.3 %shard_map.167 = (bf16[64,8,128]{2,1,0:T(8,128)(2,1)S(1)}, bf16[2,128]{1,0:T(2,128)(2,1)S(1)}) custom-call(s32[20]{0:T(128)S(1)} %concatenate.6.where_ref, bf16[64,40,128]{2,1,0:T(8,128)(2,1)S(1)} %all-to-all-done.got_ref, bf16[64,5,128]{2,1,0:T(8,128)(2,1)S(1)} %pad.10.w_ref), custom_call_target="tpu_custom_call" | custom-call | tf_op jit(solution)/shard_map/pallas_call | solution.py:230
  40.3 20.1 %all_to_all.25.got_ref = bf16[64,8,128]{2,1,0:T(8,128)(2,1)S(1)} all-to-all(bf16[64,8,128]{2,1,0:T(8,128)(2,1)S(1)} %get-tuple-element.15), channel_id=1, replica_groups=mesh['guide'=2,'y'=8,'z'=8,'batch'=4] {'y','z'}, dimensions={0} | all-to-all | bytes 262144 | tf_op jit(solution)/shard_map/all_to_all | solution.py:27
  60.4 0.8 shard_map.168
  61.2 15.5 %all_to_all.26.got_ref = bf16[64,6,128]{2,1,0:T(8,128)(2,1)S(1)} all-to-all(bf16[64,6,128]{2,1,0:T(8,128)(2,1)S(1)} %shard_map.168), channel_id=1, replica_groups=mesh['guide'=2,'y'=8,'z'=8,'batch'=4] {'y','z'}, dimensions={0} | all-to-all | bytes 196608 | tf_op jit(solution)/shard_map/all_to_all | solution.py:27
  76.8 1.2 %shard_map.169 = (bf16[16,1536]{1,0:T(8,128)(2,1)S(1)}, f32[16,128]{1,0:T(8,128)S(1)}, f32[3,128]{1,0:T(4,128)S(1)}) custom-call(s32[20]{0:T(128)S(1)} %concatenate.6.where_ref, bf16[64,6,128]{2,1,0:T(8,128)(2,1)S(1)} %all_to_all.26.got_ref, bf16[16,1536]{1,0:T(8,128)(2,1)S(1)} %bitcast.23, bf16[16,1536]{1,0:T(8,128)(2,1)S(1)} %bitcast.24, s32[2,16]{1,0:T(2,128)S(1)} %bitcast.25), custom_call_target="tpu_custom_call" | custom-call | tf_op jit(solution)/shard_map/pallas_call | solution.py:397
  78.0 0.6 shard_map.170
  78.7 15.4 %all_to_all.27.fresh_ref = bf16[64,8,128]{2,1,0:T(8,128)(2,1)S(1)} all-to-all(bf16[64,8,128]{2,1,0:T(8,128)(2,1)S(1)} %bitcast.20), channel_id=1, replica_groups=mesh['guide'=2,'y'=8,'z'=8,'batch'=4] {'y','z'}, dimensions={0} | all-to-all | bytes 262144 | tf_op jit(solution)/shard_map/all_to_all | solution.py:27
  94.1 0.1 add_reduce_fusion
  94.2 21.7 %all_to_all.28 = bf16[256,4,128]{2,1,0:T(4,128)(2,1)S(1)} all-to-all(bf16[256,4,128]{2,1,0:T(4,128)(2,1)S(1)} %broadcast_in_dim.5), channel_id=1, replica_groups=mesh['guide'=2,'y'=8,'z'=8,'batch'=4] {'batch','y','z'}, dimensions={0} | all-to-all | bytes 524288 | tf_op jit(solution)/shard_map/all_to_all | solution.py:27
  116.0 0.2 reshape.53
  116.3 0.1 multiply_reduce_fusion
  116.4 0.3 convolution_convert_fusion
  116.7 7.0 %all-gather = bf16[128,256]{1,0:T(8,128)(2,1)S(1)} all-gather(bf16[64,256]{1,0:T(8,128)(2,1)S(1)} %convolution_convert_fusion), channel_id=2, replica_groups=mesh['guide'=2,'y'=8,'z'=8,'batch'=4] {'guide'}, dimensions={0}, use_global_device_ids=true | all-gather | bytes 98304 | tf_op jit(solution)/shard_map/all_gather | solution.py:100
  123.7 0.7 shard_map.171
  (33 shorter events, 0.4 us)
Async XLA Ops:
  0.6 115.8 %copy-start = (bf16[1536,256]{1,0:T(8,128)(2,1)S(1)}, bf16[1536,256]{1,0:T(8,128)(2,1)}, u32[]{:S(2)}) copy-start(bf16[1536,256]{1,0:T(8,128)(2,1)} %param.26) | copy-start | bytes 2359300
  0.7 19.7 %copy-start.7 = (bf16[24,1536]{1,0:T(8,128)(2,1)S(1)}, bf16[24,1536]{1,0:T(8,128)(2,1)}, u32[]{:S(2)}) copy-start(bf16[24,1536]{1,0:T(8,128)(2,1)} %param.20) | copy-start | bytes 221188
  3.2 35.7 %all-to-all-start = ((bf16[64,40,128]{2,1,0:T(8,128)(2,1)}), bf16[64,40,128]{2,1,0:T(8,128)(2,1)S(1)}, u32[]{:S(2)}, u32[]{:S(2)}) async-start(bf16[64,40,128]{2,1,0:T(8,128)(2,1)} %shard_map.166), calls=%async_computation | async-start | bytes 1310720 | tf_op jit(solution)/shard_map/all_to_all | solution.py:27
  21.9 3.5 %copy-start.9 = (f32[8]{0:T(128)S(1)}, f32[8]{0:T(128)}, u32[]{:S(2)}) copy-start(f32[8]{0:T(128)} %param.29) | copy-start | bytes 100
  21.9 3.5 %copy-start.10 = (s32[8]{0:T(128)S(1)}, s32[8]{0:T(128)}, u32[]{:S(2)}) copy-start(s32[8]{0:T(128)} %param.28) | copy-start | bytes 100
  21.9 3.7 %copy-start.11 = (s32[64]{0:T(128)S(1)}, s32[64]{0:T(128)}, u32[]{:S(2)}) copy-start(s32[64]{0:T(128)} %param.27) | copy-start | bytes 772
  21.9 3.9 %copy-start.8 = (s32[1,16]{1,0:T(1,128)S(1)}, s32[1,16]{1,0:T(1,128)}, u32[]{:S(2)}) copy-start(s32[1,16]{1,0:T(1,128)} %param.19) | copy-start | bytes 196
  23.6 53.1 %copy-start.5 = (bf16[1536,16]{0,1:T(8,128)(2,1)S(1)}, bf16[1536,16]{0,1:T(8,128)(2,1)}, u32[]{:S(2)}) copy-start(bf16[1536,16]{0,1:T(8,128)(2,1)} %param.21) | copy-start | bytes 147460
  25.1 51.6 %copy-start.4 = (bf16[1,16,1536]{2,1,0:T(8,128)(2,1)S(1)}, bf16[1,16,1536]{2,1,0:T(8,128)(2,1)}, u32[]{:S(2)}) copy-start(bf16[1,16,1536]{2,1,0:T(8,128)(2,1)} %param.15) | copy-start | bytes 147460
  25.1 51.6 %copy-start.6 = (s32[1,16,2]{1,2,0:T(2,128)S(1)}, s32[1,16,2]{1,2,0:T(2,128)}, u32[]{:S(2)}) copy-start(s32[1,16,2]{1,2,0:T(2,128)} %param.22) | copy-start | bytes 388
  25.1 52.9 %copy-start.1 = (bf16[1536,256]{1,0:T(8,128)(2,1)S(1)}, bf16[1536,256]{1,0:T(8,128)(2,1)}, u32[]{:S(2)}) copy-start(bf16[1536,256]{1,0:T(8,128)(2,1)} %gate_ref.1) | copy-start | bytes 2359300
  25.2 52.8 %copy-start.2 = (bf16[1536,256]{1,0:T(8,128)(2,1)S(1)}, bf16[1536,256]{1,0:T(8,128)(2,1)}, u32[]{:S(2)}) copy-start(bf16[1536,256]{1,0:T(8,128)(2,1)} %up_ref.1) | copy-start | bytes 2359300
  38.9 39.1 %copy-start.3 = (bf16[256,1536]{1,0:T(8,128)(2,1)S(1)}, bf16[256,1536]{1,0:T(8,128)(2,1)}, u32[]{:S(2)}) copy-start(bf16[256,1536]{1,0:T(8,128)(2,1)} %down_ref.1) | copy-start | bytes 2359300

commit v13 on v12

--- a/solution.py
+++ b/solution.py
@@ -91,7 +91,6 @@
 
     piece = jnp.sum(got[:, :own_lines].astype(F32) + got[:, own_lines : 2 * own_lines].astype(F32), axis=0)
     piece = (mixed_piece + piece).astype(BF16)
-    piece = jnp.concatenate([piece, jnp.zeros((1, 128), BF16)], axis=0)
     everyone = blocks * lax.axis_size("batch")
     got = exchange(jnp.broadcast_to(piece[None], (everyone,) + piece.shape), ("batch",) + BLK)
     outgoing = lax.optimization_barrier(got[:, :own_lines].astype(F32).reshape(-1, width))

time: 125 us -> 125 us (level)
  no operation moved by 1% of the time
where the time goes in v13:
time: 125 us; the launch traced here: 124 us
  blocking collectives  79.8 us (64%)
  starting transfers between devices  17.1 us (14%)
  waiting for transfers between devices  13.1 us (10%)
  Pallas kernels  7.27 us (6%)
  local copies, waits for them, and re-layouts  5.38 us (4%)
    all_to_all x4, blocking collectives, exchange(): return lax.all_to_all(value, axes, 0, 0, tiled=True)  72.8 us
    all_to_all x1, starting transfers between devices, exchange(): return lax.all_to_all(value, axes, 0, 0, tiled=True)  17.1 us
    all_to_all x1, waiting for transfers between devices, exchange(): return lax.all_to_all(value, axes, 0, 0, tiled=True)  13.1 us
    all_gather x1, blocking collectives, local(): both = lax.all_gather(stream_logits, 'guide', axis=0, tiled=False)  6.97 us
    pallas_call x1, Pallas kernels, first_payload(): pl.pallas_call(first_payload_kernel, out_shape=jax.ShapeDtypeStruct((bloc...  2.54 us
  transfers between devices with their start and end apart: 1, of which 1 were waited for; matrix products, arithmetic and copies ran while one was open for 4% of the time, Pallas kernels for 0%

profile of v13, /device:TPU:1, one launch (start us, length us, event | category | flops | bytes accessed | tf_op | source)
XLA Modules:
  0.0 124.3 jit_solution(15493277044465032079)
XLA Ops:
  0.7 2.5 %shard_map.166 = bf16[64,40,128]{2,1,0:T(8,128)(2,1)} custom-call(s32[1]{0:T(128)} %bitcast.block_ref, bf16[16,1536]{1,0:T(8,128)(2,1)} %bitcast.22, bf16[24,2560]{1,0:T(8,128)(2,1)} %w_hbm.1, bf16[16,16,512]{2,1,0:T(8,128)(2,1)} %bitcast.27, bf16[16,16,512]{2,1,0:T(8,128)(2,1)} %bitcast.28), custom_call_target="tpu_custom_call" | custom-call | tf_op jit(solution)/shard_map/pallas_call | solution.py:323
  3.2 17.1 %all-to-all-start = ((bf16[64,40,128]{2,1,0:T(8,128)(2,1)}), bf16[64,40,128]{2,1,0:T(8,128)(2,1)S(1)}, u32[]{:S(2)}, u32[]{:S(2)}) async-start(bf16[64,40,128]{2,1,0:T(8,128)(2,1)} %shard_map.166), calls=%async_computation | async-start | bytes 1310720 | tf_op jit(solution)/shard_map/all_to_all | solution.py:27
  20.4 1.4 %reshape.47 = bf16[5,5,4,3,16,8]{5,4,3,2,1,0:T(8,128)(2,1)S(1)} reshape(bf16[25,1536]{1,0:T(8,128)(2,1)S(1)} %pad.8) | data formatting | bytes 153600 | tf_op jit(solution)/shard_map/reshape | solution.py:68
  21.9 1.7 %copy.21 = bf16[4,16,5,5,3,8]{1,0,5,4,3,2:T(4,128)(2,1)} copy(bf16[4,16,5,5,3,8]{5,1,4,0,2,3:T(8,128)(2,1)S(1)} %bitcast.26) | data formatting | bytes 153600 | tf_op jit(solution)/shard_map/transpose | solution.py:68
  23.6 1.5 %reshape.48 = bf16[64,5,120]{0,2,1:T(8,128)(2,1)S(1)} reshape(bf16[4,16,5,5,3,8]{1,0,5,4,3,2:T(4,128)(2,1)} %copy.21) | data formatting | bytes 153600 | tf_op jit(solution)/shard_map/reshape | solution.py:69
  25.2 0.2 copy.22
  25.4 0.2 select_reduce_fusion.1
  25.6 0.1 select_reduce_fusion
  25.8 0.1 concatenate.3.where_ref
  25.8 13.1 %all-to-all-done.got_ref = bf16[64,40,128]{2,1,0:T(8,128)(2,1)S(1)} async-done(((bf16[64,40,128]{2,1,0:T(8,128)(2,1)}), bf16[64,40,128]{2,1,0:T(8,128)(2,1)S(1)}, u32[]{:S(2)}, u32[]{:S(2)}) %all-to-all-start) | async-done | bytes 655392 | tf_op jit(solution)/shard_map/all_to_all | solution.py:27
  39.0 1.3 %shard_map.167 = (bf16[64,8,128]{2,1,0:T(8,128)(2,1)S(1)}, bf16[2,128]{1,0:T(2,128)(2,1)S(1)}) custom-call(s32[20]{0:T(128)S(1)} %concatenate.3.where_ref, bf16[64,40,128]{2,1,0:T(8,128)(2,1)S(1)} %all-to-all-done.got_ref, bf16[64,5,128]{2,1,0:T(8,128)(2,1)S(1)} %pad.9.w_ref), custom_call_target="tpu_custom_call" | custom-call | tf_op jit(solution)/shard_map/pallas_call | solution.py:229
  40.3 20.1 %all_to_all.25.got_ref = bf16[64,8,128]{2,1,0:T(8,128)(2,1)S(1)} all-to-all(bf16[64,8,128]{2,1,0:T(8,128)(2,1)S(1)} %get-tuple-element.15), channel_id=1, replica_groups=mesh['guide'=2,'y'=8,'z'=8,'batch'=4] {'y','z'}, dimensions={0} | all-to-all | bytes 262144 | tf_op jit(solution)/shard_map/all_to_all | solution.py:27
  60.4 0.8 shard_map.168
  61.2 15.5 %all_to_all.26.got_ref = bf16[64,6,128]{2,1,0:T(8,128)(2,1)S(1)} all-to-all(bf16[64,6,128]{2,1,0:T(8,128)(2,1)S(1)} %shard_map.168), channel_id=1, replica_groups=mesh['guide'=2,'y'=8,'z'=8,'batch'=4] {'y','z'}, dimensions={0} | all-to-all | bytes 196608 | tf_op jit(solution)/shard_map/all_to_all | solution.py:27
  76.8 1.2 %shard_map.169 = (bf16[16,1536]{1,0:T(8,128)(2,1)S(1)}, f32[16,128]{1,0:T(8,128)S(1)}, f32[3,128]{1,0:T(4,128)S(1)}) custom-call(s32[20]{0:T(128)S(1)} %concatenate.3.where_ref, bf16[64,6,128]{2,1,0:T(8,128)(2,1)S(1)} %all_to_all.26.got_ref, bf16[16,1536]{1,0:T(8,128)(2,1)S(1)} %bitcast.23, bf16[16,1536]{1,0:T(8,128)(2,1)S(1)} %bitcast.24, s32[2,16]{1,0:T(2,128)S(1)} %bitcast.25), custom_call_target="tpu_custom_call" | custom-call | tf_op jit(solution)/shard_map/pallas_call | solution.py:396
  78.0 0.6 shard_map.170
  78.7 15.4 %all_to_all.27.fresh_ref = bf16[64,8,128]{2,1,0:T(8,128)(2,1)S(1)} all-to-all(bf16[64,8,128]{2,1,0:T(8,128)(2,1)S(1)} %bitcast.20), channel_id=1, replica_groups=mesh['guide'=2,'y'=8,'z'=8,'batch'=4] {'y','z'}, dimensions={0} | all-to-all | bytes 262144 | tf_op jit(solution)/shard_map/all_to_all | solution.py:27
  94.1 0.1 add_reduce_fusion
  94.2 21.7 %all_to_all.28 = bf16[256,3,128]{2,1,0:T(4,128)(2,1)S(1)} all-to-all(bf16[256,3,128]{2,1,0:T(4,128)(2,1)S(1)} %broadcast_in_dim.5), channel_id=1, replica_groups=mesh['guide'=2,'y'=8,'z'=8,'batch'=4] {'batch','y','z'}, dimensions={0} | all-to-all | bytes 393216 | tf_op jit(solution)/shard_map/all_to_all | solution.py:27
  116.0 0.2 reshape.53
  116.1 0.1 multiply_reduce_fusion
  116.3 0.3 convolution_convert_fusion
  116.6 7.0 %all-gather = bf16[128,256]{1,0:T(8,128)(2,1)S(1)} all-gather(bf16[64,256]{1,0:T(8,128)(2,1)S(1)} %convolution_convert_fusion), channel_id=2, replica_groups=mesh['guide'=2,'y'=8,'z'=8,'batch'=4] {'guide'}, dimensions={0}, use_global_device_ids=true | all-gather | bytes 98304 | tf_op jit(solution)/shard_map/all_gather | solution.py:99
  123.5 0.7 shard_map.171
  (31 shorter events, 0.4 us)
Async XLA Ops:
  0.6 115.6 %copy-start = (bf16[1536,256]{1,0:T(8,128)(2,1)S(1)}, bf16[1536,256]{1,0:T(8,128)(2,1)}, u32[]{:S(2)}) copy-start(bf16[1536,256]{1,0:T(8,128)(2,1)} %param.26) | copy-start | bytes 2359300
  0.7 19.7 %copy-start.7 = (bf16[24,1536]{1,0:T(8,128)(2,1)S(1)}, bf16[24,1536]{1,0:T(8,128)(2,1)}, u32[]{:S(2)}) copy-start(bf16[24,1536]{1,0:T(8,128)(2,1)} %param.20) | copy-start | bytes 221188
  3.2 35.7 %all-to-all-start = ((bf16[64,40,128]{2,1,0:T(8,128)(2,1)}), bf16[64,40,128]{2,1,0:T(8,128)(2,1)S(1)}, u32[]{:S(2)}, u32[]{:S(2)}) async-start(bf16[64,40,128]{2,1,0:T(8,128)(2,1)} %shard_map.166), calls=%async_computation | async-start | bytes 1310720 | tf_op jit(solution)/shard_map/all_to_all | solution.py:27
  21.9 3.5 %copy-start.9 = (f32[8]{0:T(128)S(1)}, f32[8]{0:T(128)}, u32[]{:S(2)}) copy-start(f32[8]{0:T(128)} %param.29) | copy-start | bytes 100
  21.9 3.5 %copy-start.10 = (s32[8]{0:T(128)S(1)}, s32[8]{0:T(128)}, u32[]{:S(2)}) copy-start(s32[8]{0:T(128)} %param.28) | copy-start | bytes 100
  21.9 3.7 %copy-start.11 = (s32[64]{0:T(128)S(1)}, s32[64]{0:T(128)}, u32[]{:S(2)}) copy-start(s32[64]{0:T(128)} %param.27) | copy-start | bytes 772
  21.9 3.9 %copy-start.8 = (s32[1,16]{1,0:T(1,128)S(1)}, s32[1,16]{1,0:T(1,128)}, u32[]{:S(2)}) copy-start(s32[1,16]{1,0:T(1,128)} %param.19) | copy-start | bytes 196
  23.6 53.1 %copy-start.5 = (bf16[1536,16]{0,1:T(8,128)(2,1)S(1)}, bf16[1536,16]{0,1:T(8,128)(2,1)}, u32[]{:S(2)}) copy-start(bf16[1536,16]{0,1:T(8,128)(2,1)} %param.21) | copy-start | bytes 147460
  25.1 51.6 %copy-start.4 = (bf16[1,16,1536]{2,1,0:T(8,128)(2,1)S(1)}, bf16[1,16,1536]{2,1,0:T(8,128)(2,1)}, u32[]{:S(2)}) copy-start(bf16[1,16,1536]{2,1,0:T(8,128)(2,1)} %param.15) | copy-start | bytes 147460
  25.1 51.6 %copy-start.6 = (s32[1,16,2]{1,2,0:T(2,128)S(1)}, s32[1,16,2]{1,2,0:T(2,128)}, u32[]{:S(2)}) copy-start(s32[1,16,2]{1,2,0:T(2,128)} %param.22) | copy-start | bytes 388
  25.1 52.9 %copy-start.1 = (bf16[1536,256]{1,0:T(8,128)(2,1)S(1)}, bf16[1536,256]{1,0:T(8,128)(2,1)}, u32[]{:S(2)}) copy-start(bf16[1536,256]{1,0:T(8,128)(2,1)} %gate_ref.1) | copy-start | bytes 2359300
  25.2 52.8 %copy-start.2 = (bf16[1536,256]{1,0:T(8,128)(2,1)S(1)}, bf16[1536,256]{1,0:T(8,128)(2,1)}, u32[]{:S(2)}) copy-start(bf16[1536,256]{1,0:T(8,128)(2,1)} %up_ref.1) | copy-start | bytes 2359300
  38.9 39.1 %copy-start.3 = (bf16[256,1536]{1,0:T(8,128)(2,1)S(1)}, bf16[256,1536]{1,0:T(8,128)(2,1)}, u32[]{:S(2)}) copy-start(bf16[256,1536]{1,0:T(8,128)(2,1)} %down_ref.1) | copy-start | bytes 2359300
